TPU v7x, 128 devices: a whole 4x4x4 slice. The times are simulated.
128 devices in a mesh: seq: 32 (over x, z, core), head: 4 (over y).
Axes of the slice: x: 4, y: 4, z: 4, core: 2. Of those that a mesh axis runs over, the one named last changes fastest.
Arguments:
- tokens: bfloat16 [16384, 1024], P('seq'), may hold values from -6 to 6
- segment_ids: int32 [16384], replicated, may hold values from 0 to 4, as said below
- mix_gain: float32 [1024], replicated, may hold values from 0.1 to 1.9
- in_weight: bfloat16 [1024, 3, 1024], P(None, None, 'head'), may hold values from -0.1875 to 0.1875
- conv_weight: bfloat16 [3, 1024], P(None, 'head'), may hold values from -3 to 3
- out_weight: bfloat16 [1024, 1024], P(None, 'head'), may hold values from -0.1875 to 0.1875
- ffn_gain: float32 [1024], replicated, may hold values from 0.1 to 1.9
- gate_weight: bfloat16 [1024, 4608], P(None, 'head'), may hold values from -0.1875 to 0.1875
- up_weight: bfloat16 [1024, 4608], P(None, 'head'), may hold values from -0.1875 to 0.1875
- down_weight: bfloat16 [1024, 4608], P(None, 'head'), may hold values from -0.125 to 0.125
- cotangent: bfloat16 [16384, 1024], P('seq'), may hold values from -6 to 6
Outputs:
- result: bfloat16 [16384, 1024], P('seq')
- grad_tokens: float32 [16384, 1024], P('seq')
- grad_mix_gain: float32 [1024], replicated
- grad_in_weight: float32 [1024, 3, 1024], P('seq', None, 'head')
- grad_conv_weight: float32 [3, 1024], P(None, 'head')
- grad_out_weight: float32 [1024, 1024], P('seq', 'head')
- grad_ffn_gain: float32 [1024], replicated
- grad_gate_weight: float32 [1024, 4608], P('seq', 'head')
- grad_up_weight: float32 [1024, 4608], P('seq', 'head')
- grad_down_weight: float32 [1024, 4608], P('seq', 'head')
Inputs may be any that keep to these rules, and one draw needn't show every extreme that they name: `segment_ids`: ids start at 0, never fall along the tokens and rise by one at each sequence boundary; the tokens of one id form one sequence of at most 4096 tokens.
All inputs are finite; a program needn't handle non-finite values.
Results may differ from a plain program's by a relative error of at most 0.0095.
Values sent between devices are 32-bit elements; how exact they have to be, the bound alone decides.
A program may use at most 128 MiB of HBM per device.

v0:
```python
import jax
import jax.numpy as jnp
from jax import lax
from jax.sharding import PartitionSpec as P

EPS = 1e-05


def from_behind(block, axis, distance):
    devices = range(lax.axis_size(axis))
    route = [(i - distance, i) for i in devices if i - distance in devices]
    return lax.ppermute(block, axis, route)


def copy_for_each(x, axis):
    copies = jnp.broadcast_to(x, (lax.axis_size(axis), *x.shape))
    return lax.all_to_all(copies, axis, split_axis=0, concat_axis=0, tiled=True)


def of_everyone(x, axis):
    return copy_for_each(x, axis).sum(axis=0)


def in_one(arrays, axis):
    ends = [0]
    for a in arrays:
        ends.append(ends[-1] + a.size)
    so_far = of_everyone(jnp.concatenate([a.ravel() for a in arrays]), axis)
    return tuple((so_far[b:e].reshape(a.shape) for a, b, e in zip(arrays, ends, ends[1:])))


def in_one_piece(arrays, axis, dim, along):
    columns = [a.reshape(*a.shape[:along], -1) for a in arrays]
    both = jnp.concatenate(columns, axis=along)
    whole, at, finished = (lax.psum_scatter(both, axis, scatter_dimension=dim, tiled=True), 0, [])
    for a, column in zip(arrays, columns):
        piece = whole[..., at : at + column.shape[along]]
        finished.append(piece.reshape(*piece.shape[:along], *a.shape[along:]))
        at += column.shape[along]
    return tuple(finished)


def rms_scale(values):
    return lax.rsqrt(jnp.mean(values * values, axis=-1, keepdims=True) + EPS)


def norm_back(grad_normed, values, scale, gain):
    weighted = grad_normed * gain
    inner = jnp.mean(weighted * values, axis=-1, keepdims=True)
    grad_values = scale * weighted - values * (scale * scale * scale) * inner
    gain_grad = jnp.sum(grad_normed * values * scale, axis=0)
    return (grad_values, gain_grad)


def right_product(left, right):
    return lax.dot_general(
        left, right, (((1,), (1,)), ((), ())), preferred_element_type=jnp.float32
    )


def token_product(left, right):
    return lax.dot_general(
        left, right, (((0,), (0,)), ((), ())), preferred_element_type=jnp.float32
    )


def on_device(
    tokens,
    segment_ids,
    mix_gain,
    in_weight,
    conv_weight,
    out_weight,
    ffn_gain,
    gate_weight,
    up_weight,
    down_weight,
    cotangent,
):
    tok_rows = tokens.shape[0]
    first_row = lax.axis_index("seq") * tok_rows
    padded_ids = jnp.concatenate(
        [jnp.full((2,), -1, jnp.int32), segment_ids, jnp.full((2,), -2, jnp.int32)]
    )
    id_window = lax.dynamic_slice_in_dim(padded_ids, first_row, tok_rows + 4)
    near_ext = (id_window[2 : tok_rows + 4] == id_window[1 : tok_rows + 3]).astype(jnp.float32)
    far_ext = (id_window[2 : tok_rows + 4] == id_window[0 : tok_rows + 2]).astype(jnp.float32)
    near_own = near_ext[:tok_rows, None]
    far_own = far_ext[:tok_rows, None]
    inputs = tokens.astype(jnp.float32)
    mix_scale = rms_scale(inputs)
    mix_normed = (inputs * mix_scale * mix_gain).astype(jnp.bfloat16)
    projected = jnp.einsum("td,dkc->tkc", mix_normed, in_weight, preferred_element_type=jnp.float32)
    chan_b = projected[:, 0]
    chan_c = projected[:, 1]
    chan_x = projected[:, 2]
    mixed = chan_b * chan_x
    edge_rows = from_behind(mixed[tok_rows - 2 :], "seq", 1)
    extended = jnp.concatenate([edge_rows, mixed])
    kernel = conv_weight.astype(jnp.float32)
    prev_one = extended[1 : tok_rows + 1]
    prev_two = extended[0:tok_rows]
    conv_out = kernel[0] * mixed + kernel[1] * near_own * prev_one + kernel[2] * far_own * prev_two
    gated = (chan_c * conv_out).astype(jnp.bfloat16)
    resid = inputs + lax.psum(right_product(gated, out_weight), "head")
    ffn_scale = rms_scale(resid)
    ffn_normed = (resid * ffn_scale * ffn_gain).astype(jnp.bfloat16)
    gate = jnp.dot(ffn_normed, gate_weight, preferred_element_type=jnp.float32)
    upper = jnp.dot(ffn_normed, up_weight, preferred_element_type=jnp.float32)
    sigma = jax.nn.sigmoid(gate)
    act = (gate * sigma * upper).astype(jnp.bfloat16)
    result = (resid + lax.psum(right_product(act, down_weight), "head")).astype(jnp.bfloat16)
    d_act = jnp.dot(cotangent, down_weight, preferred_element_type=jnp.float32)
    d_gate = (d_act * upper * sigma * (1.0 + gate * (1.0 - sigma))).astype(jnp.bfloat16)
    d_up = (d_act * gate * sigma).astype(jnp.bfloat16)
    grad_down = token_product(cotangent, act)
    grad_gate = token_product(ffn_normed, d_gate)
    grad_up = token_product(ffn_normed, d_up)
    d_normed = lax.psum(right_product(d_gate, gate_weight) + right_product(d_up, up_weight), "head")
    d_hidden, grad_ffn_gain = norm_back(d_normed, resid, ffn_scale, ffn_gain)
    d_resid = d_hidden + cotangent.astype(jnp.float32)
    d_resid_low = d_resid.astype(jnp.bfloat16)
    d_gated = jnp.dot(d_resid_low, out_weight, preferred_element_type=jnp.float32)
    grad_out = token_product(d_resid_low, gated)
    d_chan_c = d_gated * conv_out
    d_conv = d_gated * chan_c
    tail_rows = from_behind(d_conv[:2], "seq", -1)
    later = jnp.concatenate([d_conv, tail_rows])
    d_mixed = (
        kernel[0] * d_conv
        + kernel[1] * near_ext[1 : tok_rows + 1, None] * later[1 : tok_rows + 1]
        + kernel[2] * far_ext[2 : tok_rows + 2, None] * later[2 : tok_rows + 2]
    )
    grad_conv = jnp.stack(
        [
            jnp.sum(d_conv * mixed, axis=0),
            jnp.sum(d_conv * near_own * prev_one, axis=0),
            jnp.sum(d_conv * far_own * prev_two, axis=0),
        ]
    )
    d_projected = jnp.stack([d_mixed * chan_x, d_chan_c, d_mixed * chan_b], axis=1).astype(
        jnp.bfloat16
    )
    grad_in = jnp.einsum("td,tkc->dkc", mix_normed, d_projected, preferred_element_type=jnp.float32)
    d_mix_normed = lax.psum(
        jnp.einsum("tkc,dkc->td", d_projected, in_weight, preferred_element_type=jnp.float32),
        "head",
    )
    d_inputs, grad_mix_gain = norm_back(d_mix_normed, inputs, mix_scale, mix_gain)
    grad_tokens = d_resid + d_inputs
    conv_total, gain_totals = in_one((grad_conv, jnp.stack([grad_mix_gain, grad_ffn_gain])), "seq")
    in_share, out_share, gate_share, up_share, down_share = in_one_piece(
        (grad_in, grad_out, grad_gate, grad_up, grad_down), "seq", 0, 1
    )
    return (
        result,
        grad_tokens,
        gain_totals[0],
        in_share,
        conv_total,
        out_share,
        gain_totals[1],
        gate_share,
        up_share,
        down_share,
    )


def solution(mesh):
    placed = (
        P("seq", None),
        P(),
        P(),
        P(None, None, "head"),
        P(None, "head"),
        P(None, "head"),
        P(),
        P(None, "head"),
        P(None, "head"),
        P(None, "head"),
        P("seq", None),
    )
    return jax.shard_map(
        on_device,
        mesh=mesh,
        in_specs=placed,
        out_specs=(
            P("seq", None),
            P("seq", None),
            P(),
            P("seq", None, "head"),
            P(None, "head"),
            P("seq", "head"),
            P(),
            P("seq", "head"),
            P("seq", "head"),
            P("seq", "head"),
        ),
        check_vma=False,
    )
```

profile of v0, /device:TPU:0, one launch (start us, length us, event | category | flops | bytes accessed | tf_op | source)
XLA Modules:
  0.0 405.6 jit_solution(4112243098430087586)
XLA Ops:
  8.9 2.8 fusion.12
  15.2 2.2 multiply_convert_fusion.7
  18.1 2.9 fusion.39
  21.1 64.1 %all-reduce.5.cloned.1.call-done = f32[512,1024]{1,0:T(8,128)} async-done(((f32[512,1024]{1,0:T(8,128)}), f32[512,1024]{1,0:T(8,128)}) %all-reduce.5.cloned.1.call-update) | async-done | bytes 2097168 | tf_op jit(solution)/shard_map/psum | solution.py:105
  85.1 1.9 multiply_reduce_fusion.2
  87.4 2.1 copy-done.32
  93.1 3.3 multiply_convert_fusion
  98.0 2.9 convolution_add_fusion
  101.0 58.6 %all-reduce.7.cloned.1.call-done = f32[512,1024]{1,0:T(8,128)} async-done(((f32[512,1024]{1,0:T(8,128)}), f32[512,1024]{1,0:T(8,128)}) %all-reduce.7.cloned.1.call-update) | async-done | bytes 2097168 | tf_op jit(solution)/shard_map/psum | solution.py:119
  159.6 2.9 multiply_reduce_fusion
  169.2 2.9 fusion.42
  173.5 2.4 convolution_bitcast_fusion
  176.9 2.7 fusion.10
  179.6 3.6 copy.39
  183.2 4.3 %constant_dynamic-update-slice_fusion = f32[1024,4480]{1,0:T(8,128)} fusion(f32[1024,768]{1,0:T(8,128)} %copy.39), kind=kLoop, calls=%fused_computation.68 | loop fusion | bytes 6291456
  189.4 4.0 convolution_dynamic-update-slice_fusion.1
  193.5 3.8 convolution_dynamic-update-slice_fusion
  197.3 3.9 bitcast_dynamic-update-slice_fusion
  201.2 68.6 %all-reduce.9.cloned.1.call-done = (f32[512,1024]{1,0:T(8,128)}, f32[512,1024]{1,0:T(8,128)}) async-done(((f32[512,1024]{1,0:T(8,128)}, f32[512,1024]{1,0:T(8,128)}), (f32[512,1024]{1,0:T(8,128)}, f32[512,1024]{1,0:T(8,128)})) %all-reduce.9.cloned.1.call-update) | async-done | bytes 4194320 | tf_op jit(solution)/shard_map/psum | solution.py:112
  269.8 2.3 fusion.8
  273.1 7.3 %all-to-all-start = ((f32[32,1,2816]{2,1,0:T(1,128)}), f32[32,1,2816]{2,1,0:T(1,128)}, u32[]{:S(2)}, u32[]{:S(2)}) async-start(f32[32,1,2816]{2,1,0:T(1,128)} %broadcast_in_dim.2), calls=%async_computation | async-start | bytes 720896 | tf_op jit(solution)/shard_map/all_to_all | solution.py:17
  280.5 3.6 fusion.5
  285.4 4.7 %all-to-all-done = f32[32,1,2816]{2,1,0:T(1,128)} async-done(((f32[32,1,2816]{2,1,0:T(1,128)}), f32[32,1,2816]{2,1,0:T(1,128)}, u32[]{:S(2)}, u32[]{:S(2)}) %all-to-all-start) | async-done | bytes 360480 | tf_op jit(solution)/shard_map/all_to_all | solution.py:17
  292.6 101.8 %reduce-scatter.2.cloned.1.call-done = f32[32,4480]{1,0:T(8,128)} async-done(((f32[1024,4480]{1,0:T(8,128)}), f32[32,4480]{1,0:T(8,128)}) %reduce-scatter.2.cloned.1.call-update) | async-done | bytes 573456 | tf_op jit(solution)/shard_map/reduce_scatter | solution.py:35
  (125 shorter events, 31.7 us)
Async XLA Ops:
  7.2 85.9 %copy-start = (bf16[1024,1152]{1,0:T(8,128)(2,1)S(1)}, bf16[1024,1152]{1,0:T(8,128)(2,1)}, u32[]{:S(2)}) copy-start(bf16[1024,1152]{1,0:T(8,128)(2,1)} %param.20) | copy-start | bytes 7077892
  7.2 78.0 %all-reduce.5.cloned.1.call-start = ((), (), s32[]{:S(2)}) async-start(), calls=%async_computation.2 | async-start | bytes 4194304 | tf_op jit(solution)/shard_map/psum | solution.py:105
  8.9 5.5 %copy-start.28 = (s32[16384]{0:T(1024)S(1)}, s32[16384]{0:T(1024)}, u32[]{:S(2)}) copy-start(s32[16384]{0:T(1024)} %param.12) | copy-start | bytes 196612
  8.9 5.8 %copy-start.31 = (bf16[3,256]{1,0:T(4,128)(2,1)S(1)}, bf16[3,256]{1,0:T(4,128)(2,1)}, u32[]{:S(2)}) copy-start(bf16[3,256]{1,0:T(4,128)(2,1)} %param.15) | copy-start | bytes 4612
  13.0 4.3 %copy-start.13 = (f32[512,256]{1,0:T(8,128)}, f32[512,256]{1,0:T(8,128)S(1)}, u32[]{:S(2)}) copy-start(f32[512,256]{1,0:T(8,128)S(1)} %fusion.24) | copy-start | bytes 1572868
  13.1 2.1 collective-permute-start
  18.1 67.1 %copy-start.7 = (bf16[512,1024]{1,0:T(8,128)(2,1)S(1)}, bf16[512,1024]{1,0:T(8,128)(2,1)}, u32[]{:S(2)}) copy-start(bf16[512,1024]{1,0:T(8,128)(2,1)} %param.11) | copy-start | bytes 3145732
  21.0 66.1 %copy-start.29 = (f32[1024]{0:T(1024)S(1)}, f32[1024]{0:T(1024)}, u32[]{:S(2)}) copy-start(f32[1024]{0:T(1024)} %param.17) | copy-start | bytes 12292
  21.0 138.5 %all-reduce.7.cloned.1.call-start = ((), (), s32[]{:S(2)}) async-start(), calls=%async_computation.3 | async-start | bytes 4194304 | tf_op jit(solution)/shard_map/psum | solution.py:119
  87.1 4.0 copy-start.2
  100.9 168.9 %all-reduce.9.cloned.1.call-start = ((), (), s32[]{:S(2)}) async-start(), calls=%async_computation.5 | async-start | bytes 8388608 | tf_op jit(solution)/shard_map/psum | solution.py:112
  165.4 3.8 copy-start.35
  167.7 4.8 %copy-start.26 = (bf16[512,1,256]{2,0,1:T(8,128)(2,1)}, bf16[512,1,256]{2,0,1:T(8,128)(2,1)S(1)}, u32[]{:S(2)}) copy-start(bf16[512,1,256]{2,0,1:T(8,128)(2,1)S(1)} %get-tuple-element.72) | copy-start | bytes 786436
  167.7 4.4 %collective-permute-start.1 = (f32[2,256]{1,0:T(2,128)S(1)}, f32[2,256]{1,0:T(2,128)S(1)}, u32[]{:S(2)}, u32[]{:S(2)}) collective-permute-start(f32[2,256]{1,0:T(2,128)S(1)} %slice.137), channel_id=1, source_target_pairs={{4,0},{8,4},{12,8},{16,12},{20,16},{24,20},{28,24},{32,28},{36,32}... | collective-permute-start | bytes 6152 | tf_op jit(solution)/shard_map/ppermute | solution.py:12
  176.0 218.4 %reduce-scatter.2.cloned.1.call-start = ((), (), s32[]{:S(2)}) async-start(), calls=%async_computation.4 | async-start | bytes 18923520 | tf_op jit(solution)/shard_map/reduce_scatter | solution.py:35
  183.2 4.3 %copy-start.6 = (f32[512,1024]{1,0:T(8,128)S(1)}, f32[512,1024]{1,0:T(8,128)}, u32[]{:S(2)}) copy-start(f32[512,1024]{1,0:T(8,128)} %copy-done.5) | copy-start | bytes 6291460
  183.2 4.3 %copy-start.16 = (bf16[512,256]{1,0:T(8,128)(2,1)S(1)}, bf16[512,256]{1,0:T(8,128)(2,1)}, u32[]{:S(2)}) copy-start(bf16[512,256]{1,0:T(8,128)(2,1)} %copy-done.15) | copy-start | bytes 786436
  189.4 4.0 copy-start.21
  193.5 3.8 copy-start.25
  193.5 3.8 copy-start.36
  273.1 17.0 %all-to-all-start = ((f32[32,1,2816]{2,1,0:T(1,128)}), f32[32,1,2816]{2,1,0:T(1,128)}, u32[]{:S(2)}, u32[]{:S(2)}) async-start(f32[32,1,2816]{2,1,0:T(1,128)} %broadcast_in_dim.2), calls=%async_computation | async-start | bytes 720896 | tf_op jit(solution)/shard_map/all_to_all | solution.py:17
  280.5 3.6 copy-start.4
  280.5 3.6 copy-start.17
  284.1 115.0 %copy-start.1 = (bf16[1024,1152]{1,0:T(8,128)(2,1)S(1)}, bf16[1024,1152]{1,0:T(8,128)(2,1)}, u32[]{:S(2)}) copy-start(bf16[1024,1152]{1,0:T(8,128)(2,1)} %param.20) | copy-start | bytes 7077892
  (20 other events, 37.4 us)
Sparse Core Ops, SparseCore 0:
  21.1 63.9 all-reduce.4
  101.0 58.4 all-reduce.6
  176.1 93.6 all-reduce.8
  274.2 120.0 reduce-scatter.1
where the time goes:
time: 406 us
  waiting for transfers between devices  298 us (73%)
  matrix products  38.2 us (9%)
  local copies, waits for them, and re-layouts  24.5 us (6%)
  other arithmetic  20.2 us (5%)
  between operations  14.2 us (3%)
  starting transfers between devices  10.3 us (3%)
    reduce_scatter x1, waiting for transfers between devices, in_one_piece(): lax.psum_scatter(both, axis, scatter_dimension=dim, tiled=True)  102 us
    psum x1, waiting for transfers between devices, on_device(): lax.psum(right_product(act, down_weight), 'head')  68.6 us
    psum x1, waiting for transfers between devices, on_device(): resid = inputs + lax.psum(right_product(gated, out_weight), 'head')  64.1 us
    psum x1, waiting for transfers between devices, on_device(): lax.psum(right_product(d_gate, gate_weight) + right_product(d_up, up_weig...  58.6 us
    unnamed x76, local copies, waits for them, and re-layouts  13.7 us
    dot_general x4, matrix products, token_product(): lax.dot_general(left, right, (((0,), (0,)), ((), ())), preferred_element_...  13.2 us
    dot_general x4, matrix products, right_product(): lax.dot_general(left, right, (((1,), (1,)), ((), ())), preferred_element_...  10.2 us
  transfers between devices with their start and end apart: 7, of which 6 were waited for; matrix products, arithmetic and copies ran while one was open for 9% of the time, Pallas kernels for 0%

commit v1 on v0

v1 whole, which is shorter than its diff:
```python
import jax
import jax.numpy as jnp
from jax import lax
from jax.experimental import pallas as pl
from jax.experimental.pallas import tpu as pltpu
from jax.sharding import PartitionSpec as P

EPS = 1e-05
MESH = pl.DeviceIdType.MESH
HEADS = 4


def norm_back_rows(grad_normed, values, gain, extra):
    scale = lax.rsqrt(jnp.mean(values * values, axis=-1, keepdims=True) + EPS)
    weighted = grad_normed * gain
    inner = jnp.mean(weighted * values, axis=-1, keepdims=True)
    return extra + (scale * weighted - values * (scale * scale * scale) * inner)


def ring_kernel(kinds, *refs):
    jobs = len(kinds)
    at = 0
    ins = []
    for kind in kinds:
        n = 4 if kind == "norm" else 2
        ins.append(refs[at : at + n])
        at += n
    outs = refs[at : at + jobs]
    at += jobs
    scratch = [refs[at + 4 * j : at + 4 * j + 4] for j in range(jobs)]
    s_sem, r_sem = refs[at + 4 * jobs : at + 4 * jobs + 2]
    T = outs[0].shape[0]
    C = T // HEADS
    H = C // 2

    me = lax.axis_index("head")
    R = lax.rem(me + 1, HEADS)
    L = lax.rem(me + HEADS - 1, HEADS)
    O = lax.rem(me + 2, HEADS)
    barrier = pltpu.get_barrier_semaphore()
    for other in (R, L):
        pl.semaphore_signal(barrier, inc=1, device_id={"head": other}, device_id_type=MESH)
    pl.semaphore_wait(barrier, 2)

    def rows(k, half):
        return pl.ds(pl.multiple_of(k * C + half * H, H), H)

    def send(src, dst, job, i, dev):
        copy = pltpu.make_async_remote_copy(
            src_ref=src,
            dst_ref=dst,
            send_sem=s_sem.at[job, i],
            recv_sem=r_sem.at[job, i],
            device_id={"head": dev},
            device_id_type=MESH,
        )
        copy.start()
        return copy

    def finish(job, half, total):
        kind = kinds[job]
        mine = pl.ds(half * H, H)
        if kind == "norm":
            _, values, gain, extra = ins[job]
            total = norm_back_rows(
                total, values[mine, :].astype(jnp.float32), gain[...], extra[mine, :].astype(jnp.float32)
            )
        else:
            total = total + ins[job][1][mine, :].astype(jnp.float32)
        outs[job][rows(me, half), :] = total

    every = []
    live = []
    for j in range(jobs):
        p = ins[j][0]
        t1, t2, fl, fr = scratch[j]
        a0 = send(p.at[rows(O, 0)], t1.at[0], j, 0, R)
        a1 = send(p.at[rows(O, 1)], t2.at[0], j, 1, L)
        a2 = send(p.at[rows(R, 1)], fl.at[1], j, 2, R)
        a3 = send(p.at[rows(L, 0)], fr.at[0], j, 3, L)
        live.append((a0, a1, a2, a3))
        every += [a0, a1, a2, a3]
    second = []
    for j in range(jobs):
        p = ins[j][0]
        t1, t2, fl, fr = scratch[j]
        a0, a1, a2, a3 = live[j]
        a0.wait_recv()
        t1[1] = p[rows(R, 0), :] + t1[0]
        a4 = send(t1.at[1], fl.at[0], j, 4, R)
        a1.wait_recv()
        t2[1] = p[rows(L, 1), :] + t2[0]
        a5 = send(t2.at[1], fr.at[1], j, 5, L)
        second.append((a2, a3, a4, a5))
        every += [a4, a5]
    shares = []
    for j in range(jobs):
        p, o = ins[j][0], outs[j]
        t1, t2, fl, fr = scratch[j]
        a2, a3, a4, a5 = second[j]
        a3.wait_recv()
        a4.wait_recv()
        finish(j, 0, p[rows(me, 0), :] + fl[0] + fr[0])
        b0 = send(o.at[rows(me, 0)], o.at[rows(me, 0)], j, 6, R)
        c0 = send(o.at[rows(me, 0)], o.at[rows(me, 0)], j, 8, L)
        a2.wait_recv()
        a5.wait_recv()
        finish(j, 1, p[rows(me, 1), :] + fl[1] + fr[1])
        b1 = send(o.at[rows(me, 1)], o.at[rows(me, 1)], j, 7, R)
        c1 = send(o.at[rows(me, 1)], o.at[rows(me, 1)], j, 9, L)
        shares.append((b0, b1, c0, c1))
        every += [b0, b1, c0, c1]
    last = []
    for j in range(jobs):
        o = outs[j]
        b0, b1, c0, c1 = shares[j]
        b0.wait_recv()
        d0 = send(o.at[rows(L, 0)], o.at[rows(L, 0)], j, 10, R)
        c1.wait_recv()
        d1 = send(o.at[rows(R, 1)], o.at[rows(R, 1)], j, 11, L)
        last += [b1, c0, d0, d1]
        every += [d0, d1]
    for copy in last:
        copy.wait_recv()
    for copy in every:
        copy.wait_send()


def ring(jobs, cid):
    kinds = tuple(job[0] for job in jobs)
    arrays = [a for job in jobs for a in job[1:]]
    T, D = jobs[0][1].shape
    H = T // HEADS // 2
    n = len(jobs)
    outs = pl.pallas_call(
        lambda *refs: ring_kernel(kinds, *refs),
        out_shape=tuple(jax.ShapeDtypeStruct((T, D), jnp.float32) for _ in jobs),
        in_specs=[pl.BlockSpec(memory_space=pltpu.VMEM)] * len(arrays),
        out_specs=tuple(pl.BlockSpec(memory_space=pltpu.VMEM) for _ in jobs),
        scratch_shapes=[pltpu.VMEM((2, H, D), jnp.float32)] * (4 * n)
        + [pltpu.SemaphoreType.DMA((n, 12))] * 2,
        compiler_params=pltpu.CompilerParams(
            collective_id=cid, has_side_effects=True, vmem_limit_bytes=32 << 20
        ),
        cost_estimate=pl.CostEstimate(flops=1, bytes_accessed=1, transcendentals=0),
        name=f"ring{cid}",
    )(*arrays)
    return outs


def from_behind(block, axis, distance):
    devices = range(lax.axis_size(axis))
    route = [(i - distance, i) for i in devices if i - distance in devices]
    return lax.ppermute(block, axis, route)


def rms_scale(values):
    return lax.rsqrt(jnp.mean(values * values, axis=-1, keepdims=True) + EPS)


def right_product(left, right):
    return lax.dot_general(
        left, right, (((1,), (1,)), ((), ())), preferred_element_type=jnp.float32
    )


def token_product(left, right):
    return lax.dot_general(
        left, right, (((0,), (0,)), ((), ())), preferred_element_type=jnp.float32
    )


def shared(grad):
    return lax.psum_scatter(grad, "seq", scatter_dimension=0, tiled=True)


def on_device(
    tokens,
    segment_ids,
    mix_gain,
    in_weight,
    conv_weight,
    out_weight,
    ffn_gain,
    gate_weight,
    up_weight,
    down_weight,
    cotangent,
):
    tok_rows = tokens.shape[0]
    own = tok_rows // HEADS
    own_at = lax.axis_index("head") * own

    def own_rows(x):
        return lax.dynamic_slice_in_dim(x, own_at, own, 0)

    first_row = lax.axis_index("seq") * tok_rows
    padded_ids = jnp.concatenate(
        [jnp.full((2,), -1, jnp.int32), segment_ids, jnp.full((2,), -2, jnp.int32)]
    )
    id_window = lax.dynamic_slice_in_dim(padded_ids, first_row, tok_rows + 4)
    near_ext = (id_window[2 : tok_rows + 4] == id_window[1 : tok_rows + 3]).astype(jnp.float32)
    far_ext = (id_window[2 : tok_rows + 4] == id_window[0 : tok_rows + 2]).astype(jnp.float32)
    near_own = near_ext[:tok_rows, None]
    far_own = far_ext[:tok_rows, None]
    inputs = tokens.astype(jnp.float32)
    mix_scale = rms_scale(inputs)
    mix_normed = (inputs * mix_scale * mix_gain).astype(jnp.bfloat16)
    projected = jnp.einsum("td,dkc->tkc", mix_normed, in_weight, preferred_element_type=jnp.float32)
    chan_b = projected[:, 0]
    chan_c = projected[:, 1]
    chan_x = projected[:, 2]
    mixed = chan_b * chan_x
    edge_rows = from_behind(mixed[tok_rows - 2 :], "seq", 1)
    extended = jnp.concatenate([edge_rows, mixed])
    kernel = conv_weight.astype(jnp.float32)
    prev_one = extended[1 : tok_rows + 1]
    prev_two = extended[0:tok_rows]
    conv_out = kernel[0] * mixed + kernel[1] * near_own * prev_one + kernel[2] * far_own * prev_two
    gated = (chan_c * conv_out).astype(jnp.bfloat16)
    (resid,) = ring([("add", right_product(gated, out_weight), own_rows(tokens))], 1)
    ffn_scale = rms_scale(resid)
    ffn_normed = (resid * ffn_scale * ffn_gain).astype(jnp.bfloat16)
    gate = jnp.dot(ffn_normed, gate_weight, preferred_element_type=jnp.float32)
    upper = jnp.dot(ffn_normed, up_weight, preferred_element_type=jnp.float32)
    sigma = jax.nn.sigmoid(gate)
    act = (gate * sigma * upper).astype(jnp.bfloat16)
    d_act = jnp.dot(cotangent, down_weight, preferred_element_type=jnp.float32)
    d_gate = (d_act * upper * sigma * (1.0 + gate * (1.0 - sigma))).astype(jnp.bfloat16)
    d_up = (d_act * gate * sigma).astype(jnp.bfloat16)
    grad_down = token_product(cotangent, act)
    grad_gate = token_product(ffn_normed, d_gate)
    grad_up = token_product(ffn_normed, d_up)
    down_share, gate_share, up_share = shared(grad_down), shared(grad_gate), shared(grad_up)
    d_normed_part = right_product(d_gate, gate_weight) + right_product(d_up, up_weight)
    grad_ffn_gain = jnp.sum(d_normed_part * resid * ffn_scale, axis=0)
    d_normed_part, _, _, _ = lax.optimization_barrier((d_normed_part, grad_down, grad_gate, grad_up))
    (d_resid,) = ring(
        [("norm", d_normed_part, own_rows(resid), ffn_gain[None], own_rows(cotangent))], 2
    )
    d_resid_low = d_resid.astype(jnp.bfloat16)
    d_gated = jnp.dot(d_resid_low, out_weight, preferred_element_type=jnp.float32)
    grad_out = token_product(d_resid_low, gated)
    d_chan_c = d_gated * conv_out
    d_conv = d_gated * chan_c
    tail_rows = from_behind(d_conv[:2], "seq", -1)
    later = jnp.concatenate([d_conv, tail_rows])
    next_one = later[1 : tok_rows + 1]
    next_two = later[2 : tok_rows + 2]
    near_next = near_ext[1 : tok_rows + 1, None]
    far_next = far_ext[2 : tok_rows + 2, None]
    d_mixed = kernel[0] * d_conv + kernel[1] * near_next * next_one + kernel[2] * far_next * next_two
    grad_conv = jnp.stack(
        [
            jnp.sum(d_conv * mixed, axis=0),
            jnp.sum(d_conv * near_own * prev_one, axis=0),
            jnp.sum(d_conv * far_own * prev_two, axis=0),
        ]
    )
    d_projected = jnp.stack([d_mixed * chan_x, d_chan_c, d_mixed * chan_b], axis=1).astype(
        jnp.bfloat16
    )
    grad_in = jnp.einsum("td,tkc->dkc", mix_normed, d_projected, preferred_element_type=jnp.float32)
    in_share = shared(grad_in)
    out_share = shared(grad_out)
    d_mix_part = jnp.einsum(
        "tkc,dkc->td", d_projected, in_weight, preferred_element_type=jnp.float32
    )
    grad_mix_gain = jnp.sum(d_mix_part * inputs * mix_scale, axis=0)
    gain_totals = lax.psum(jnp.stack([grad_mix_gain, grad_ffn_gain]), ("seq", "head"))
    conv_total = lax.psum(grad_conv, "seq")
    result_part = right_product(act, down_weight)
    d_mix_part, result_part, _, _ = lax.optimization_barrier((d_mix_part, result_part, grad_in, grad_out))
    grad_tokens, result = ring(
        [
            ("norm", d_mix_part, own_rows(tokens), mix_gain[None], own_rows(d_resid)),
            ("add", result_part, own_rows(resid)),
        ],
        3,
    )
    return (
        result.astype(jnp.bfloat16),
        grad_tokens,
        gain_totals[0],
        in_share,
        conv_total,
        out_share,
        gain_totals[1],
        gate_share,
        up_share,
        down_share,
    )


def solution(mesh):
    placed = (
        P("seq", None),
        P(),
        P(),
        P(None, None, "head"),
        P(None, "head"),
        P(None, "head"),
        P(),
        P(None, "head"),
        P(None, "head"),
        P(None, "head"),
        P("seq", None),
    )
    return jax.shard_map(
        on_device,
        mesh=mesh,
        in_specs=placed,
        out_specs=(
            P("seq", None),
            P("seq", None),
            P(),
            P("seq", None, "head"),
            P(None, "head"),
            P("seq", "head"),
            P(),
            P("seq", "head"),
            P("seq", "head"),
            P("seq", "head"),
        ),
        check_vma=False,
    )
```

time: 406 us -> 572 us (1.41)
  Pallas kernels: 0 us -> 152 us
  blocking collectives: 0 us -> 128 us
  waiting for transfers between devices: 298 us -> 205 us
  other arithmetic: 20.2 us -> 7.38 us
  starting transfers between devices: 10.3 us -> 2.91 us
    psum x3 -> x0, waiting for transfers between devices: 191 us -> none  [the longest x1 68.6 us: on_device(): lax.psum(right_product(act, down_weight), 'head')]
    pallas_call x0 -> x3, Pallas kernels: none -> 152 us  [ring(): pl.pallas_call(lambda *refs: ring_kernel(kinds, *refs), out_shape=tuple((...]
    psum x0 -> x2, blocking collectives: none -> 128 us  [the longest x1 65.7 us: on_device(): conv_total = lax.psum(grad_conv, 'seq')]
    unnamed x4 -> x6, waiting for transfers between devices: 0.07 us -> 88.4 us
    reduce_scatter x1 -> x4, waiting for transfers between devices: 102 us -> 115 us  [shared(): return lax.psum_scatter(grad, 'seq', scatter_dimension=0, tiled=True)]
    all_to_all x1 -> x0, starting transfers between devices: 7.34 us -> none  [copy_for_each(): return lax.all_to_all(copies, axis, split_axis=0, concat_axis=0, tiled=True)]
    reduce_sum x3 -> x0, other arithmetic: 6.47 us -> none  [the longest x2 5.25 us: norm_back(): gain_grad = jnp.sum(grad_normed * values * scale, axis=0)]
    unnamed x76 -> x56, local copies, waits for them, and re-layouts: 13.7 us -> 15.2 us
  transfers between devices with their start and end apart: 7 -> 7, of which waited for: 6 -> 4; matrix products, arithmetic and copies ran while one was open for 9% -> 4% of each run, Pallas kernels for 0% -> 12%
where the time goes in v1:
time: 572 us
  waiting for transfers between devices  205 us (36%)
  Pallas kernels  152 us (27%)
  blocking collectives  128 us (22%)
  matrix products  43.1 us (8%)
  local copies, waits for them, and re-layouts  19.2 us (3%)
  between operations  14.3 us (2%)
  other arithmetic  7.38 us (1%)
    pallas_call x3, Pallas kernels, ring(): pl.pallas_call(lambda *refs: ring_kernel(kinds, *refs), out_shape=tuple((...  152 us
    reduce_scatter x4, waiting for transfers between devices, shared(): return lax.psum_scatter(grad, 'seq', scatter_dimension=0, tiled=True)  115 us
    unnamed x6, waiting for transfers between devices  88.4 us
    psum x1, blocking collectives, on_device(): conv_total = lax.psum(grad_conv, 'seq')  65.7 us
    psum x1, blocking collectives, on_device(): lax.psum(jnp.stack([grad_mix_gain, grad_ffn_gain]), ('seq', 'head'))  62.5 us
    unnamed x56, local copies, waits for them, and re-layouts  15.2 us
    dot_general x4, matrix products, token_product(): lax.dot_general(left, right, (((0,), (0,)), ((), ())), preferred_element_...  14.1 us
  transfers between devices with their start and end apart: 7, of which 4 were waited for; matrix products, arithmetic and copies ran while one was open for 4% of the time, Pallas kernels for 12%

profile of v1, /device:TPU:0, one launch (start us, length us, event | category | flops | bytes accessed | tf_op | source)
XLA Modules:
  0.0 571.7 jit_solution(1958574625102718326)
XLA Ops:
  7.2 1.7 fusion
  8.9 2.8 fusion.8
  14.7 3.5 fusion.35
  19.3 2.1 multiply_convert_fusion.7
  23.0 42.5 %ring1.1 = f32[512,1024]{1,0:T(8,128)S(1)} custom-call(f32[512,1024]{1,0:T(8,128)S(1)} %fusion.36.refs_0_, bf16[128,1024]{1,0:T(8,128)(2,1)S(1)} %constant_dynamic-slice_fusion.3.refs_1_), custom_call_target="tpu_custom_call" | custom-call | flops 1 | bytes 1 | tf_op jit(solution)/shard_map/ring1/pallas_call | solution.py:135
  69.6 3.7 multiply_convert_fusion
  73.2 2.9 fusion.38
  76.1 3.7 fusion.39
  79.8 5.3 fusion.40
  85.1 4.3 multiply_reduce_fusion
  89.5 3.6 convolution_bitcast_fusion
  93.1 39.5 %ring2.1 = f32[512,1024]{1,0:T(8,128)S(1)} custom-call(f32[512,1024]{1,0:T(8,128)S(1)} %get-tuple-element.15.refs_0_, f32[128,1024]{1,0:T(8,128)S(1)} %constant_dynamic-slice_fusion.2.refs_1_.refs_5_, f32[1,1024]{1,0:T(1,128)S(1)} %bitcast.75, bf16[128,1024]{1,0:T(8,128)(2,1)S(1)} %constant_dynamic-slice_fusion.1.refs_3_), custom_call_target="tpu_custom_call" | custom-call | flops 1 | bytes 1 | tf_op jit(solution)/shard_map/ring2/pallas_call | solution.py:135
  135.5 2.2 fusion.18
  140.6 1.8 collective-permute-done.1
  143.4 2.8 fusion.6
  147.6 6.1 %copy.27 = f32[1024,1152]{1,0:T(8,128)} copy(f32[1024,1152]{0,1:T(8,128)} %convolution_bitcast_fusion) | data formatting | bytes 9437184
  153.8 65.7 %psum.15 = f32[3,256]{1,0:T(4,128)} all-reduce(f32[3,256]{1,0:T(4,128)S(1)} %pad_maximum_fusion.6), channel_id=1, replica_groups=mesh['seq'=32,'head'=4] {'seq'}, use_global_device_ids=true, to_apply=%region_9.0 | all-reduce | flops 768 | bytes 6144 | tf_op jit(solution)/shard_map/psum | solution.py:271
  220.6 3.7 fusion.41.refs_4_
  225.5 69.8 %ring3.1 = (f32[512,1024]{1,0:T(8,128)S(1)}, f32[512,1024]{1,0:T(8,128)S(1)}) custom-call(f32[512,1024]{1,0:T(8,128)S(1)} %get-tuple-element.16.refs_0_, bf16[128,1024]{1,0:T(8,128)(2,1)S(1)} %constant_dynamic-slice_fusion.3.refs_1_, f32[1,1024]{1,0:T(1,128)S(1)} %bitcast.76, f32[128,1024]{1,0:T(8,128)S(1)} %constant_dynamic-slice_fusion.refs_3_, ...), custom_call_target="tpu_custom_call" | custom-call | flops 1 | bytes 1 | tf_op jit(solution)/shard_map/ring3/pallas_call | solution.py:135
  297.0 62.5 %psum.14 = f32[2,1024]{1,0:T(2,128)S(1)} all-reduce(f32[2,1024]{1,0:T(2,128)S(1)} %pad_maximum_fusion.5), channel_id=1, replica_groups=mesh['seq'=32,'head'=4] {'seq','head'}, use_global_device_ids=true, to_apply=%region_4.0 | all-reduce | flops 2048 | bytes 16384 | tf_op jit(solution)/shard_map/psum | solution.py:270
  360.1 27.0 %reduce-scatter.14.cloned.1.call-done = f32[32,1152]{1,0:T(8,128)} async-done(((f32[1024,1152]{1,0:T(8,128)}), f32[32,1152]{1,0:T(8,128)}) %reduce-scatter.14.cloned.1.call-update) | async-done | bytes 147472 | tf_op jit(solution)/shard_map/reduce_scatter | solution.py:174
  387.1 87.6 %reduce-scatter.12.cloned.1.call-done = f32[32,1152]{1,0:T(8,128)} async-done(((f32[1024,1152]{1,0:T(8,128)}), f32[32,1152]{1,0:T(8,128)}) %reduce-scatter.12.cloned.1.call-update) | async-done | bytes 147472 | tf_op jit(solution)/shard_map/reduce_scatter | solution.py:174
  474.7 87.1 %reduce-scatter.16.cloned.1.call-done = f32[32,1152]{1,0:T(8,128)} async-done(((f32[1024,1152]{1,0:T(8,128)}), f32[32,1152]{1,0:T(8,128)}) %reduce-scatter.16.cloned.1.call-update) | async-done | bytes 147472
  561.8 3.3 copy.30
  (98 shorter events, 22.1 us)
Async XLA Ops:
  7.2 62.4 %copy-start = (bf16[1024,1152]{1,0:T(8,128)(2,1)S(1)}, bf16[1024,1152]{1,0:T(8,128)(2,1)}, u32[]{:S(2)}) copy-start(bf16[1024,1152]{1,0:T(8,128)(2,1)} %param.19) | copy-start | bytes 7077892
  7.2 352.9 %reduce-scatter.10.cloned.1.call-start = ((), (), s32[]{:S(2)}) async-start(), calls=%async_computation.6 | async-start | bytes 1081344 | tf_op jit(solution)/shard_map/reduce_scatter | solution.py:174
  8.9 5.4 copy-start.24
  8.9 5.4 copy-start.23
  13.0 6.3 %copy-start.10 = (f32[512,256]{1,0:T(8,128)}, f32[512,256]{1,0:T(8,128)S(1)}, u32[]{:S(2)}) copy-start(f32[512,256]{1,0:T(8,128)S(1)} %fusion.21) | copy-start | bytes 1572868
  13.0 6.3 %collective-permute-start = (f32[2,256]{1,0:T(2,128)S(1)}, f32[2,256]{1,0:T(2,128)S(1)}, u32[]{:S(2)}, u32[]{:S(2)}) collective-permute-start(f32[2,256]{1,0:T(2,128)S(1)} %slice.93), channel_id=1, source_target_pairs={{0,4},{4,8},{8,12},{12,16},{16,20},{20,24},{24,28},{28,32},{32,36}... | collective-permute-start | bytes 6152 | tf_op jit(solution)/shard_map/ppermute | solution.py:154
  18.2 3.2 copy-start.14
  68.0 8.1 %copy-start.7 = (bf16[512,1024]{1,0:T(8,128)(2,1)}, bf16[512,1024]{1,0:T(8,128)(2,1)S(1)}, u32[]{:S(2)}) copy-start(bf16[512,1024]{1,0:T(8,128)(2,1)S(1)} %multiply_convert_fusion.3) | copy-start | bytes 3145732
  85.1 4.3 copy-start.17
  85.1 4.3 copy-start.18
  93.1 40.8 %copy-start.13 = (bf16[512,256]{1,0:T(8,128)(2,1)S(1)}, bf16[512,256]{1,0:T(8,128)(2,1)}, u32[]{:S(2)}) copy-start(bf16[512,256]{1,0:T(8,128)(2,1)} %copy-done.12) | copy-start | bytes 786436
  135.4 224.7 %reduce-scatter.8.cloned.1.call-start = ((), (), s32[]{:S(2)}) async-start(), calls=%async_computation.5 | async-start | bytes 3244032 | tf_op jit(solution)/shard_map/reduce_scatter | solution.py:174
  139.1 3.6 copy-start.21
  139.1 4.3 copy-start.6
  139.1 4.3 copy-start.15
  139.2 3.2 collective-permute-start.1
  146.3 240.8 %reduce-scatter.14.cloned.1.call-start = ((), (), s32[]{:S(2)}) async-start(), calls=%async_computation.8 | async-start | bytes 4866048 | tf_op jit(solution)/shard_map/reduce_scatter | solution.py:174
  147.0 327.7 %reduce-scatter.12.cloned.1.call-start = ((), (), s32[]{:S(2)}) async-start(), calls=%async_computation.7 | async-start | bytes 4866048 | tf_op jit(solution)/shard_map/reduce_scatter | solution.py:174
  147.6 414.2 %reduce-scatter.16.cloned.1.call-start = ((), (), s32[]{:S(2)}) async-start(), calls=%async_computation.9 | async-start | bytes 4866048
  220.6 3.8 copy-start.16
  220.6 3.8 copy-start.20
  220.6 3.8 copy-start.22
  220.6 3.8 copy-start.26
  561.8 3.3 copy-start.1
  (10 other events, 14.5 us)
Sparse Core Ops, SparseCore 0:
  135.5 79.2 reduce-scatter.9
  219.5 79.6 reduce-scatter.7
  303.5 83.5 reduce-scatter.13
  391.7 82.9 reduce-scatter.11
  478.8 82.9 reduce-scatter.15

commit v2 on v1

--- a/solution.py
+++ b/solution.py
@@ -148,6 +148,356 @@
     return outs
 
 
+def end_kernel(*refs):
+    (dm, toks, gain, d_res, rp, res, g_gate, g_up, g_down, g_in, g_out, small) = refs[:12]
+    (o_tok, o_res, o_gate, o_up, o_down, o_in, o_out, o_small) = refs[12:20]
+    (yt, yf, S, RC, tA, tB, fA, fB, t2A, t2B, f2A, f2B, sm, sr) = refs[20:34]
+    (ys, yr, cs, cr, lc, as_, ar, bs, br, ss, sr_sem) = refs[34:]
+    T, D = o_tok.shape
+    C = T // HEADS
+    H = C // 2
+    WA, WB = tA.shape[-1], tB.shape[-1]
+    seq = lax.axis_index("seq")
+    me = lax.axis_index("head")
+    core = lax.rem(seq, 2)
+    z = lax.rem(lax.div(seq, 2), 4)
+    x = lax.div(seq, 8)
+
+    def ahead(k, n):
+        return lax.rem(k + n, 4)
+
+    def at_x(n):
+        return {"seq": (ahead(x, n) * 4 + z) * 2 + core, "head": me}
+
+    def at_z(n):
+        return {"seq": (x * 4 + ahead(z, n)) * 2 + core, "head": me}
+
+    def at_y(n):
+        return {"seq": seq, "head": ahead(me, n)}
+
+    twin = {"seq": (x * 4 + z) * 2 + (1 - core), "head": me}
+
+    barrier = pltpu.get_barrier_semaphore()
+    for n in (1, 2, 3):
+        for axis in (at_x, at_z, at_y):
+            pl.semaphore_signal(barrier, inc=1, device_id=axis(n), device_id_type=MESH)
+    pl.semaphore_signal(barrier, inc=1, device_id=twin, device_id_type=MESH)
+    pl.semaphore_wait(barrier, 10)
+
+    every = []
+
+    def send(src, dst, s_sem, r_sem, dev):
+        copy = pltpu.make_async_remote_copy(
+            src_ref=src, dst_ref=dst, send_sem=s_sem, recv_sem=r_sem, device_id=dev, device_id_type=MESH
+        )
+        copy.start()
+        every.append(copy)
+        return copy
+
+    def add_up(dst, *srcs):
+        n, r = dst.shape[:2]
+        q = r // 8
+
+        def body(i, carry):
+            b, at = lax.div(i, q), pl.ds(pl.multiple_of(lax.rem(i, q) * 8, 8), 8)
+            total = dst[b, at, :]
+            for src in srcs:
+                total = total + src[b, at, :]
+            dst[b, at, :] = total
+            return carry
+
+        lax.fori_loop(0, n * q, body, 0)
+
+    steps = []
+
+    def when(time):
+        def add(fn):
+            steps.append((time, len(steps), fn))
+            return fn
+
+        return add
+
+    def y_job(j, p, o, finish, times):
+        t1, t2, fl, fr = (yt.at[j, 0], yt.at[j, 1], yf.at[j, 0], yf.at[j, 1])
+        R, L, O = ahead(me, 1), ahead(me, 3), ahead(me, 2)
+        c = {}
+
+        def rows(k, half):
+            return pl.ds(pl.multiple_of(k * C + half * H, H), H)
+
+        def go(name, src, dst, i, n):
+            c[name] = send(src, dst, ys.at[j, i], yr.at[j, i], at_y(n))
+
+        @when(times[0])
+        def _():
+            go("a0", p.at[rows(O, 0)], t1.at[0], 0, 1)
+            go("a1", p.at[rows(O, 1)], t2.at[0], 1, 3)
+            go("a2", p.at[rows(R, 1)], fl.at[1], 2, 1)
+            go("a3", p.at[rows(L, 0)], fr.at[0], 3, 3)
+
+        @when(times[1])
+        def _():
+            c["a0"].wait_recv()
+            t1[1] = p[rows(R, 0), :] + t1[0]
+            go("a4", t1.at[1], fl.at[0], 4, 1)
+            c["a1"].wait_recv()
+            t2[1] = p[rows(L, 1), :] + t2[0]
+            go("a5", t2.at[1], fr.at[1], 5, 3)
+
+        @when(times[2])
+        def _():
+            c["a3"].wait_recv()
+            c["a4"].wait_recv()
+            o[rows(me, 0), :] = finish(0, p[rows(me, 0), :] + fl[0] + fr[0])
+            go("b0", o.at[rows(me, 0)], o.at[rows(me, 0)], 6, 1)
+            go("c0", o.at[rows(me, 0)], o.at[rows(me, 0)], 8, 3)
+            c["a2"].wait_recv()
+            c["a5"].wait_recv()
+            o[rows(me, 1), :] = finish(1, p[rows(me, 1), :] + fl[1] + fr[1])
+            go("c1", o.at[rows(me, 1)], o.at[rows(me, 1)], 9, 3)
+            go("b1", o.at[rows(me, 1)], o.at[rows(me, 1)], 7, 1)
+
+        @when(times[3])
+        def _():
+            c["b0"].wait_recv()
+            go("d0", o.at[rows(L, 0)], o.at[rows(L, 0)], 10, 1)
+            c["c1"].wait_recv()
+            go("d1", o.at[rows(R, 1)], o.at[rows(R, 1)], 11, 3)
+
+        @when(900)
+        def _():
+            for name in ("b1", "c0", "d0", "d1"):
+                c[name].wait_recv()
+
+    def finish_tokens(half, total):
+        mine = pl.ds(half * H, H)
+        return norm_back_rows(total, toks[mine, :].astype(jnp.float32), gain[...], d_res[mine, :])
+
+    def finish_result(half, total):
+        return total + res[pl.ds(half * H, H), :]
+
+    y_job(0, dm, o_tok, finish_tokens, (0, 9, 20, 35))
+    y_job(1, rp, o_res, finish_result, (0, 14, 27, 45))
+
+    A = [(g_gate, 0, WA // 2), (g_up, WA // 2, WA // 2)]
+    B = [(g_down, 0, 1152)] + [(g_in.at[k], 1152 + 256 * k, 256) for k in range(3)] + [(g_out, 1920, 256)]
+    pairs = {}
+
+    def cut(ref, which, k):
+        return ref.at[k] if which == "A" else ref.at[:, k]
+
+    def offer(which, turn, k, base):
+        pieces, offset = (A, 0) if which == "A" else (B, WA)
+        got = []
+        for i, (g, at, w) in enumerate(pieces):
+            n = base + i
+            cols = pl.ds(offset + at, w)
+            src = cut(g, which, k)
+            mine = pltpu.make_async_copy(src.at[:, core], cut(S, which, k).at[:, :, cols], lc.at[n])
+            mine.start()
+            other = send(src.at[:, 1 - core], cut(RC, which, k).at[:, :, cols], cs.at[n], cr.at[n], twin)
+            got.append((mine, other))
+        pairs[which, turn] = got
+        return base + len(pieces)
+
+    pos = {"A": x, "B": z}
+    turns = [("A", 2), ("B", 2), ("A", 1), ("B", 1), ("A", 3), ("B", 3), ("A", 0), ("B", 0)]
+
+    @when(0)
+    def _():
+        base = 0
+        for which, turn in turns:
+            base = offer(which, turn, ahead(pos[which], turn), base)
+
+    def half_cols(which):
+        return pl.ds(0, WA) if which == "A" else pl.ds(WA, WB)
+
+    def settle(which, turn):
+        for mine, other in pairs[which, turn]:
+            mine.wait()
+            other.wait_recv()
+        k = ahead(pos[which], turn)
+        cols = half_cols(which)
+        add_up(cut(S, which, k).at[:, :, cols], cut(RC, which, k).at[:, :, cols])
+
+    def ring_of(chunk, t, f, s_sem, r_sem, base, to, tag, times, settle_at, done):
+        c = {}
+
+        def go(name, src, dst, i, n):
+            c[name] = send(src, dst, s_sem.at[base + i], r_sem.at[base + i], to(n))
+
+        @when(times[0])
+        def _():
+            settle_at(2)
+            go("a0", chunk(2, 0), t.at[0], 0, 1)
+            go("a1", chunk(2, 1), t.at[1], 1, 3)
+
+        @when(times[1])
+        def _():
+            settle_at(1)
+            go("a2", chunk(1, 1), f.at[0, 1], 2, 1)
+            settle_at(3)
+            go("a3", chunk(3, 0), f.at[1, 0], 3, 3)
+
+        @when(times[2])
+        def _():
+            c["a0"].wait_recv()
+            add_up(t.at[0], chunk(1, 0))
+            go("a4", t.at[0], f.at[0, 0], 4, 1)
+            c["a1"].wait_recv()
+            add_up(t.at[1], chunk(3, 1))
+            go("a5", t.at[1], f.at[1, 1], 5, 3)
+
+        @when(times[3])
+        def _():
+            settle_at(0)
+
+        @when(times[4])
+        def _():
+            c["a3"].wait_recv()
+            c["a4"].wait_recv()
+            add_up(chunk(0, 0), f.at[0, 0], f.at[1, 0])
+            c["a2"].wait_recv()
+            c["a5"].wait_recv()
+            add_up(chunk(0, 1), f.at[0, 1], f.at[1, 1])
+            done()
+
+    def chunk1(which):
+        def chunk(turn, half):
+            k = ahead(pos[which], turn)
+            return cut(S, which, k).at[pl.ds(half * 2, 2), :, half_cols(which)]
+
+        return chunk
+
+    def chunk2(which):
+        def chunk(turn, half):
+            k = ahead(z if which == "A" else x, turn)
+            mine = cut(S, which, pos[which])
+            return mine.at[pl.ds(k, 1), pl.ds(half * 16, 16), half_cols(which)]
+
+        return chunk
+
+    nothing = lambda *a: None
+    ring_of(chunk1("A"), tA, fA, as_, ar, 0, at_x, "A", (1, 5, 15, 12, 33), lambda n: settle("A", n), nothing)
+    ring_of(chunk1("B"), tB, fB, bs, br, 0, at_z, "B", (2, 6, 16, 13, 34), lambda n: settle("B", n), nothing)
+
+    def out_A():
+        rows = S[x, z, :, pl.ds(0, WA)]
+        o_gate[...] = rows[:, : WA // 2]
+        o_up[...] = rows[:, WA // 2 :]
+
+    def out_B():
+        rows = S[x, z, :, pl.ds(WA, WB)]
+        o_down[...] = rows[:, :1152]
+        for k in range(3):
+            o_in[k] = rows[:, 1152 + 256 * k : 1408 + 256 * k]
+        o_out[...] = rows[:, 1920:]
+
+    ring_of(chunk2("A"), t2A, f2A, as_, ar, 6, at_z, "A2", (36, 37, 41, 42, 48), nothing, out_A)
+    ring_of(chunk2("B"), t2B, f2B, bs, br, 6, at_x, "B2", (38, 39, 43, 44, 49), nothing, out_B)
+
+    axes = [(at_z, z, 5), (at_x, x, 10), (at_y, me, 16)]
+    first = {}
+
+    @when(0.5)
+    def _():
+        first["c"] = send(small, sr.at[3, 0], ss.at[9], sr_sem.at[9], twin)
+
+    @when(4.5)
+    def _():
+        first["c"].wait_recv()
+        sm[0] = small[...] + sr[3, 0]
+
+    for a, (to, here, time) in enumerate(axes):
+        copies = []
+
+        def begin(a=a, to=to, here=here, copies=copies):
+            sr[a, here] = sm[a]
+            for n in (1, 2, 3):
+                copies.append(send(sm.at[a], sr.at[a, here], ss.at[a * 3 + n - 1], sr_sem.at[a * 3 + n - 1], to(n)))
+
+        def end(a=a, copies=copies):
+            for copy in copies:
+                copy.wait_recv()
+            total = (sr[a, 0] + sr[a, 1]) + (sr[a, 2] + sr[a, 3])
+            if a < 2:
+                sm[a + 1] = total
+            else:
+                o_small[0:8] = total[0:8]
+                o_small[8:16] = sm[2][8:16]
+
+        when(time)(begin)
+        when(time + 4)(end)
+
+    for _, _, fn in sorted(steps, key=lambda s: s[:2]):
+        fn()
+    for copy in every:
+        copy.wait_send()
+
+
+def finish_all(dm, toks, gain, d_res, rp, res, gate, up, down, inw, outw, small):
+    T, D = dm.shape
+    H = T // HEADS // 2
+    wa = gate.shape[1] + up.shape[1]
+    wb = down.shape[1] + inw.shape[0] * inw.shape[2] + outw.shape[1]
+    f32 = jnp.float32
+
+    def blocks(g):
+        return g.reshape(*g.shape[:-2], 4, 4, 2, 32, g.shape[-1])
+
+    vmem = pl.BlockSpec(memory_space=pltpu.VMEM)
+    anywhere = pl.BlockSpec(memory_space=pl.ANY)
+    shape = jax.ShapeDtypeStruct
+    dma = pltpu.SemaphoreType.DMA
+    return pl.pallas_call(
+        end_kernel,
+        out_shape=(
+            shape((T, D), f32),
+            shape((T, D), f32),
+            shape((32, gate.shape[1]), f32),
+            shape((32, up.shape[1]), f32),
+            shape((32, down.shape[1]), f32),
+            shape((3, 32, inw.shape[2]), f32),
+            shape((32, outw.shape[1]), f32),
+            shape((16, 256), f32),
+        ),
+        in_specs=[vmem] * 6 + [anywhere] * 5 + [vmem],
+        out_specs=(vmem,) * 8,
+        scratch_shapes=[
+            pltpu.VMEM((2, 2, 2, H, D), f32),
+            pltpu.VMEM((2, 2, 2, H, D), f32),
+            pltpu.VMEM((4, 4, 32, wa + wb), f32),
+            pltpu.VMEM((4, 4, 32, wa + wb), f32),
+            pltpu.VMEM((2, 2, 32, wa), f32),
+            pltpu.VMEM((2, 2, 32, wb), f32),
+            pltpu.VMEM((2, 2, 2, 32, wa), f32),
+            pltpu.VMEM((2, 2, 2, 32, wb), f32),
+            pltpu.VMEM((2, 1, 16, wa), f32),
+            pltpu.VMEM((2, 1, 16, wb), f32),
+            pltpu.VMEM((2, 2, 1, 16, wa), f32),
+            pltpu.VMEM((2, 2, 1, 16, wb), f32),
+            pltpu.VMEM((3, 16, 256), f32),
+            pltpu.VMEM((4, 4, 16, 256), f32),
+            dma((2, 12)),
+            dma((2, 12)),
+            dma((28,)),
+            dma((28,)),
+            dma((28,)),
+            dma((12,)),
+            dma((12,)),
+            dma((12,)),
+            dma((12,)),
+            dma((10,)),
+            dma((10,)),
+        ],
+        compiler_params=pltpu.CompilerParams(
+            collective_id=7, has_side_effects=True, vmem_limit_bytes=50 << 20
+        ),
+        cost_estimate=pl.CostEstimate(flops=1, bytes_accessed=1, transcendentals=0),
+        name="end",
+    )(dm, toks, gain, d_res, rp, res, *map(blocks, (gate, up, down, inw, outw)), small)
+
+
 def from_behind(block, axis, distance):
     devices = range(lax.axis_size(axis))
     route = [(i - distance, i) for i in devices if i - distance in devices]
@@ -168,10 +518,6 @@
     return lax.dot_general(
         left, right, (((0,), (0,)), ((), ())), preferred_element_type=jnp.float32
     )
-
-
-def shared(grad):
-    return lax.psum_scatter(grad, "seq", scatter_dimension=0, tiled=True)
 
 
 def on_device(
@@ -231,7 +577,6 @@
     grad_down = token_product(cotangent, act)
     grad_gate = token_product(ffn_normed, d_gate)
     grad_up = token_product(ffn_normed, d_up)
-    down_share, gate_share, up_share = shared(grad_down), shared(grad_gate), shared(grad_up)
     d_normed_part = right_product(d_gate, gate_weight) + right_product(d_up, up_weight)
     grad_ffn_gain = jnp.sum(d_normed_part * resid * ffn_scale, axis=0)
     d_normed_part, _, _, _ = lax.optimization_barrier((d_normed_part, grad_down, grad_gate, grad_up))
@@ -260,32 +605,42 @@
     d_projected = jnp.stack([d_mixed * chan_x, d_chan_c, d_mixed * chan_b], axis=1).astype(
         jnp.bfloat16
     )
-    grad_in = jnp.einsum("td,tkc->dkc", mix_normed, d_projected, preferred_element_type=jnp.float32)
-    in_share = shared(grad_in)
-    out_share = shared(grad_out)
+    grad_in = jnp.einsum("td,tkc->kdc", mix_normed, d_projected, preferred_element_type=jnp.float32)
     d_mix_part = jnp.einsum(
         "tkc,dkc->td", d_projected, in_weight, preferred_element_type=jnp.float32
     )
     grad_mix_gain = jnp.sum(d_mix_part * inputs * mix_scale, axis=0)
-    gain_totals = lax.psum(jnp.stack([grad_mix_gain, grad_ffn_gain]), ("seq", "head"))
-    conv_total = lax.psum(grad_conv, "seq")
+    small = jnp.concatenate(
+        [
+            grad_mix_gain.reshape(4, 256),
+            grad_ffn_gain.reshape(4, 256),
+            grad_conv,
+            jnp.zeros((5, 256), jnp.float32),
+        ]
+    )
     result_part = right_product(act, down_weight)
-    d_mix_part, result_part, _, _ = lax.optimization_barrier((d_mix_part, result_part, grad_in, grad_out))
-    grad_tokens, result = ring(
-        [
-            ("norm", d_mix_part, own_rows(tokens), mix_gain[None], own_rows(d_resid)),
-            ("add", result_part, own_rows(resid)),
-        ],
-        3,
+    grad_tokens, result, gate_share, up_share, down_share, in_share, out_share, totals = finish_all(
+        d_mix_part,
+        own_rows(tokens),
+        mix_gain[None],
+        own_rows(d_resid),
+        result_part,
+        own_rows(resid),
+        grad_gate,
+        grad_up,
+        grad_down,
+        grad_in,
+        grad_out,
+        small,
     )
     return (
         result.astype(jnp.bfloat16),
         grad_tokens,
-        gain_totals[0],
-        in_share,
-        conv_total,
+        totals[0:4].reshape(1024),
+        in_share.transpose(1, 0, 2),
+        totals[8:11],
         out_share,
-        gain_totals[1],
+        totals[4:8].reshape(1024),
         gate_share,
         up_share,
         down_share,

time: 572 us -> 229 us (0.40)
  waiting for transfers between devices: 205 us -> 1.66 us
  blocking collectives: 128 us -> 0 us
  between operations: 14.3 us -> 1.04 us
  Pallas kernels: 152 us -> 165 us
  matrix products: 43.1 us -> 34.4 us
    psum x2 -> x0, blocking collectives: 128 us -> none  [the longest x1 65.7 us: on_device(): conv_total = lax.psum(grad_conv, 'seq')]
    reduce_scatter x4 -> x0, waiting for transfers between devices: 115 us -> none  [shared(): return lax.psum_scatter(grad, 'seq', scatter_dimension=0, tiled=True)]
    unnamed x6 -> x0, waiting for transfers between devices: 88.4 us -> none
    pallas_call x0 -> x1, Pallas kernels: none -> 82.8 us  [finish_all(): pl.pallas_call(end_kernel, out_shape=(shape((T, D), f32), shape((T, D), f...]
    pallas_call x3 -> x2, Pallas kernels: 152 us -> 82.1 us  [ring(): pl.pallas_call(lambda *refs: ring_kernel(kinds, *refs), out_shape=tuple((...]
    unnamed x56 -> x43, local copies, waits for them, and re-layouts: 15.2 us -> 9.32 us
  transfers between devices with their start and end apart: 7 -> 2, of which waited for: 4 -> 1; matrix products, arithmetic and copies ran while one was open for 4% -> 2% of each run, Pallas kernels for 12% -> 0%
where the time goes in v2:
time: 229 us; the launch traced here: 228 us
  Pallas kernels  165 us (72%)
  matrix products  34.4 us (15%)
  local copies, waits for them, and re-layouts  14.9 us (7%)
  other arithmetic  7.99 us (3%)
  starting transfers between devices  2.58 us (1%)
    pallas_call x1, Pallas kernels, finish_all(): pl.pallas_call(end_kernel, out_shape=(shape((T, D), f32), shape((T, D), f...  82.8 us
    pallas_call x2, Pallas kernels, ring(): pl.pallas_call(lambda *refs: ring_kernel(kinds, *refs), out_shape=tuple((...  82.1 us
    dot_general x4, matrix products, token_product(): lax.dot_general(left, right, (((0,), (0,)), ((), ())), preferred_element_...  11.9 us
    unnamed x43, local copies, waits for them, and re-layouts  9.32 us
    dot_general x4, matrix products, right_product(): lax.dot_general(left, right, (((1,), (1,)), ((), ())), preferred_element_...  6.5 us
  transfers between devices with their start and end apart: 2, of which 1 were waited for; matrix products, arithmetic and copies ran while one was open for 2% of the time, Pallas kernels for 0%

profile of v2, /device:TPU:0, one launch (start us, length us, event | category | flops | bytes accessed | tf_op | source)
XLA Modules:
  0.0 227.6 jit_solution(9232511296810710079)
XLA Ops:
  0.7 1.7 fusion
  2.3 2.8 %fusion.7 = f32[512,3,256]{2,0,1:T(8,128)S(1)} fusion(bf16[1024,3,256]{2,0,1:T(8,128)(2,1)} %param.14, bf16[512,1024]{1,0:T(8,128)(2,1)} %param.11, f32[1024]{0:T(1024)} %param.13, f32[512]{0:T(512)S(1)} %add_rsqrt_fusion.1), kind=kOutput, calls=%fused_computation.20 | convolution fusion | flops 807403520 | bytes 4200448 | tf_op jit(solution)/shard_map/td,dkc->tkc/dot_general | solution.py:555
  5.2 1.1 copy-done.4
  6.4 1.3 collective-permute-start
  8.1 3.6 %fusion.33 = f32[512,1152]{1,0:T(8,128)S(1)} fusion(bf16[512,1024]{1,0:T(8,128)(2,1)} %param.21, bf16[1024,1152]{1,0:T(8,128)(2,1)} %param.20), kind=kOutput, calls=%fused_computation.70 | convolution fusion | flops 1207959552 | bytes 5767168 | tf_op jit(solution)/shard_map/dot_general | solution.py:574
  13.6 42.5 %ring1.1 = f32[512,1024]{1,0:T(8,128)S(1)} custom-call(f32[512,1024]{1,0:T(8,128)S(1)} %fusion.34.refs_0_, bf16[128,1024]{1,0:T(8,128)(2,1)S(1)} %get-tuple-element.58.refs_1_), custom_call_target="tpu_custom_call" | custom-call | flops 1 | bytes 1 | tf_op jit(solution)/shard_map/ring1/pallas_call | solution.py:135
  58.1 1.5 fusion.35
  59.6 2.3 %multiply_convert_fusion = (bf16[512,1152]{1,0:T(8,128)(2,1)S(1)}, bf16[512,1152]{1,0:T(8,128)(2,1)S(1)}, bf16[512,1152]{1,0:T(8,128)(2,1)S(1)}) fusion(f32[512,1152]{1,0:T(8,128)S(1)} %fusion.35, f32[512,1152]{1,0:T(8,128)S(1)} %fusion.33, bf16[512,1024]{1,0:T(8,128)(2,1)S(1)} %multiply_convert_fusion.3, bf16[1024,1152]{1,0:T(8,128)(2,1)S(1)} %copy-done), kind=kOutput, calls=%fused_computation.3 | convolution fusion | flops 1217396736 | bytes 11665408 | tf_op jit(solution)/shard_map/dot_general | solution.py:571
  61.9 1.5 fusion.36
  63.5 3.7 %fusion.38 = f32[1024,1152]{1,0:T(8,128)} fusion(bf16[512,1024]{1,0:T(8,128)(2,1)S(1)} %multiply_convert_fusion.3, bf16[512,1152]{1,0:T(8,128)(2,1)S(1)} %get-tuple-element.37), kind=kOutput, calls=%fused_computation.75 | convolution fusion | flops 1207959552 | bytes 6946816 | tf_op jit(solution)/shard_map/dot_general | solution.py:518
  67.2 3.8 %fusion.39 = f32[1024,1152]{1,0:T(8,128)} fusion(bf16[512,1024]{1,0:T(8,128)(2,1)S(1)} %multiply_convert_fusion.3, bf16[512,1152]{1,0:T(8,128)(2,1)S(1)} %get-tuple-element.38), kind=kOutput, calls=%fused_computation.76 | convolution fusion | flops 1207959552 | bytes 6946816 | tf_op jit(solution)/shard_map/dot_general | solution.py:518
  70.9 1.6 multiply_reduce_fusion
  72.6 39.6 %ring2.1 = f32[512,1024]{1,0:T(8,128)S(1)} custom-call(f32[512,1024]{1,0:T(8,128)S(1)} %get-tuple-element.19.refs_0_, f32[128,1024]{1,0:T(8,128)S(1)} %constant_dynamic-slice_fusion.2.refs_1_.refs_5_, f32[1,1024]{1,0:T(1,128)S(1)} %bitcast.85, bf16[128,1024]{1,0:T(8,128)(2,1)S(1)} %get-tuple-element.57.refs_3_), custom_call_target="tpu_custom_call" | custom-call | flops 1 | bytes 1 | tf_op jit(solution)/shard_map/ring2/pallas_call | solution.py:135
  114.3 2.9 %fusion.40.refs_4_ = f32[512,1024]{1,0:T(8,128)} fusion(bf16[512,1152]{1,0:T(8,128)(2,1)S(1)} %get-tuple-element.36, bf16[1024,1152]{1,0:T(8,128)(2,1)S(1)} %copy-done.15), kind=kOutput, calls=%fused_computation.77 | convolution fusion | flops 1207959552 | bytes 5636096 | tf_op jit(solution)/shard_map/dot_general | solution.py:512
  117.1 3.8 %fusion.37 = f32[1152,1024]{0,1:T(8,128)} fusion(bf16[512,1152]{1,0:T(8,128)(2,1)S(1)} %get-tuple-element.36, bf16[512,1024]{1,0:T(8,128)(2,1)S(1)} %copy-done.11), kind=kOutput, calls=%fused_computation.74 | convolution fusion | flops 1207959552 | bytes 6946816 | tf_op jit(solution)/shard_map/dot_general | solution.py:518
  121.3 1.3 collective-permute-start.1
  122.7 1.7 collective-permute-done.1
  124.3 1.3 fusion.21
  126.8 2.4 %fusion.4 = (f32[1024]{0:T(1024)S(1)}, f32[512,1024]{1,0:T(8,128)}) fusion(bf16[512,1024]{1,0:T(8,128)(2,1)S(1)} %copy-done.10, f32[512]{0:T(512)S(1)} %add_rsqrt_fusion.1, bf16[1024,3,256]{2,0,1:T(8,128)(2,1)S(1)} %copy-done.16, bf16[512,1,256]{2,0,1:T(8,128)(2,1)S(1)} %fusion.23, bf16[512,1,256]{2,0,1:T(8,128)(2,1)S(1)} %get-tuple-element.39, ...), kind=kOutput, calls=%fused_computation.11 | convolution fusion | flops 808188928 | bytes 5511168 | tf_op jit(solution)/shard_map/tkc,dkc->td/dot_general | solution.py:609
  129.1 2.9 %convolution_bitcast_fusion = f32[3,1024,256]{1,2,0:T(8,128)} fusion(bf16[512,1024]{1,0:T(8,128)(2,1)S(1)} %copy-done.10, f32[1024]{0:T(1024)S(1)} %copy-done.3, f32[512]{0:T(512)S(1)} %add_rsqrt_fusion.1, bf16[512,1,256]{2,0,1:T(8,128)(2,1)S(1)} %fusion.23, bf16[512,1,256]{2,0,1:T(8,128)(2,1)S(1)} %get-tuple-element.39, ...), kind=kOutput, calls=%fused_computation.15 | convolution fusion | flops 808189952 | bytes 4986880 | tf_op jit(solution)/shard_map/td,tkc->kdc/dot_general | solution.py:608
  132.0 3.6 %copy.22 = f32[3,1024,256]{2,1,0:T(8,128)} copy(f32[3,1024,256]{1,2,0:T(8,128)} %convolution_bitcast_fusion) | data formatting | bytes 6291456 | tf_op jit(solution)/shard_map/td,tkc->kdc/transpose | solution.py:608
  135.6 82.8 %end.1 = (f32[512,1024]{1,0:T(8,128)}, f32[512,1024]{1,0:T(8,128)}, f32[32,1152]{1,0:T(8,128)S(1)}, f32[32,1152]{1,0:T(8,128)S(1)}, f32[32,1152]{1,0:T(8,128)S(1...) custom-call(f32[512,1024]{1,0:T(8,128)} %get-tuple-element.52.refs_0_, ...), custom_call_target="tpu_custom_call" | custom-call | flops 1 | bytes 1 | tf_op jit(solution)/shard_map/end/pallas_call | solution.py:452
  219.1 2.8 %convert_element_type.48 = bf16[512,1024]{1,0:T(8,128)(2,1)} convert(f32[512,1024]{1,0:T(8,128)} %get-tuple-element.20) | non-fusion elementwise | flops 524288 | bytes 3145728 | tf_op jit(solution)/shard_map/convert_element_type | solution.py:637
  223.0 1.3 copy.32
  (70 shorter events, 12.8 us)
Async XLA Ops:
  0.6 59.0 %copy-start = (bf16[1024,1152]{1,0:T(8,128)(2,1)S(1)}, bf16[1024,1152]{1,0:T(8,128)(2,1)}, u32[]{:S(2)}) copy-start(bf16[1024,1152]{1,0:T(8,128)(2,1)} %param.19) | copy-start | bytes 7077892
  2.3 5.4 %copy-start.13 = (bf16[3,256]{1,0:T(4,128)(2,1)S(1)}, bf16[3,256]{1,0:T(4,128)(2,1)}, u32[]{:S(2)}) copy-start(bf16[3,256]{1,0:T(4,128)(2,1)} %param.15) | copy-start | bytes 4612
  2.3 5.4 %copy-start.12 = (s32[16384]{0:T(1024)S(1)}, s32[16384]{0:T(1024)}, u32[]{:S(2)}) copy-start(s32[16384]{0:T(1024)} %param.12) | copy-start | bytes 196612
  5.2 1.1 copy-start.4
  6.4 6.5 %copy-start.6 = (f32[512,256]{1,0:T(8,128)}, f32[512,256]{1,0:T(8,128)S(1)}, u32[]{:S(2)}) copy-start(f32[512,256]{1,0:T(8,128)S(1)} %fusion.20) | copy-start | bytes 1572868
  6.4 6.4 %collective-permute-start = (f32[2,256]{1,0:T(2,128)S(1)}, f32[2,256]{1,0:T(2,128)S(1)}, u32[]{:S(2)}, u32[]{:S(2)}) collective-permute-start(f32[2,256]{1,0:T(2,128)S(1)} %slice.97), channel_id=1, source_target_pairs={{0,4},{4,8},{8,12},{12,16},{16,20},{20,24},{24,28},{28,32},{32,36}... | collective-permute-start | bytes 6152 | tf_op jit(solution)/shard_map/ppermute | solution.py:504
  8.1 3.7 %copy-start.11 = (bf16[512,1024]{1,0:T(8,128)(2,1)S(1)}, bf16[512,1024]{1,0:T(8,128)(2,1)}, u32[]{:S(2)}) copy-start(bf16[512,1024]{1,0:T(8,128)(2,1)} %param.21) | copy-start | bytes 3145732
  8.1 4.8 %copy-start.5 = (f32[512,3,256]{2,0,1:T(8,128)S(1)}, f32[512,3,256]{2,0,1:T(8,128)}, u32[]{:S(2)}) copy-start(f32[512,3,256]{2,0,1:T(8,128)} %copy-done.4) | copy-start | bytes 4718596
  11.8 1.4 copy-start.9
  56.2 0.7 copy-start.2
  56.4 1.7 copy-start.14
  112.6 1.7 copy-start.15
  117.1 3.8 %copy-start.7 = (f32[512,256]{1,0:T(8,128)S(1)}, f32[512,256]{1,0:T(8,128)}, u32[]{:S(2)}) copy-start(f32[512,256]{1,0:T(8,128)} %copy-done.6) | copy-start | bytes 1572868
  121.3 3.1 %collective-permute-start.1 = (f32[2,256]{1,0:T(2,128)S(1)}, f32[2,256]{1,0:T(2,128)S(1)}, u32[]{:S(2)}, u32[]{:S(2)}) collective-permute-start(f32[2,256]{1,0:T(2,128)S(1)} %slice.101), channel_id=1, source_target_pairs={{4,0},{8,4},{12,8},{16,12},{20,16},{24,20},{28,24},{32,28},{36,32}... | collective-permute-start | bytes 6152 | tf_op jit(solution)/shard_map/ppermute | solution.py:504
  122.6 4.1 %copy-start.10 = (bf16[512,1024]{1,0:T(8,128)(2,1)S(1)}, bf16[512,1024]{1,0:T(8,128)(2,1)}, u32[]{:S(2)}) copy-start(bf16[512,1024]{1,0:T(8,128)(2,1)} %param.11) | copy-start | bytes 3145732
  122.7 4.1 %copy-start.16 = (bf16[1024,3,256]{2,0,1:T(8,128)(2,1)S(1)}, bf16[1024,3,256]{2,0,1:T(8,128)(2,1)}, u32[]{:S(2)}) copy-start(bf16[1024,3,256]{2,0,1:T(8,128)(2,1)} %param.14) | copy-start | bytes 4718596
  126.8 2.4 %copy-start.3 = (f32[1024]{0:T(1024)S(1)}, f32[1024]{0:T(1024)}, u32[]{:S(2)}) copy-start(f32[1024]{0:T(1024)} %param.13) | copy-start | bytes 12292
  218.4 4.6 %copy-start.8 = (f32[512,1024]{1,0:T(8,128)S(1)}, f32[512,1024]{1,0:T(8,128)}, u32[]{:S(2)}) copy-start(f32[512,1024]{1,0:T(8,128)} %get-tuple-element.70) | copy-start | bytes 6291460
  223.0 4.6 %copy-start.1 = (bf16[1024,1152]{1,0:T(8,128)(2,1)S(1)}, bf16[1024,1152]{1,0:T(8,128)(2,1)}, u32[]{:S(2)}) copy-start(bf16[1024,1152]{1,0:T(8,128)(2,1)} %param.19) | copy-start | bytes 7077892

commit v3 on v1

--- a/solution.py
+++ b/solution.py
@@ -148,6 +148,483 @@
     return outs
 
 
+class Comm:
+    def __init__(self):
+        seq = lax.axis_index("seq")
+        self.me = lax.axis_index("head")
+        self.core = lax.rem(seq, 2)
+        self.z = lax.rem(lax.div(seq, 2), 4)
+        self.x = lax.div(seq, 8)
+        self.every = []
+        self.steps = []
+
+    def at_x(self, n):
+        return {"seq": (ahead(self.x, n) * 4 + self.z) * 2 + self.core, "head": self.me}
+
+    def at_z(self, n):
+        return {"seq": (self.x * 4 + ahead(self.z, n)) * 2 + self.core, "head": self.me}
+
+    def at_y(self, n):
+        return {"seq": (self.x * 4 + self.z) * 2 + self.core, "head": ahead(self.me, n)}
+
+    def twin(self, n=1):
+        return {"seq": (self.x * 4 + self.z) * 2 + (1 - self.core), "head": self.me}
+
+    def greet(self, devices):
+        barrier = pltpu.get_barrier_semaphore()
+        for device in devices:
+            pl.semaphore_signal(barrier, inc=1, device_id=device, device_id_type=MESH)
+        pl.semaphore_wait(barrier, len(devices))
+
+    def send(self, src, dst, s_sem, r_sem, dev):
+        copy = pltpu.make_async_remote_copy(
+            src_ref=src, dst_ref=dst, send_sem=s_sem, recv_sem=r_sem, device_id=dev, device_id_type=MESH
+        )
+        copy.start()
+        self.every.append(copy)
+        return copy
+
+    def when(self, time):
+        def add(fn):
+            self.steps.append((time, len(self.steps), fn))
+            return fn
+
+        return add
+
+    def run(self):
+        for _, _, fn in sorted(self.steps, key=lambda s: s[:2]):
+            fn()
+        for copy in self.every:
+            copy.wait_send()
+
+
+def ahead(k, n):
+    return lax.rem(k + n, 4)
+
+
+def add_up(dst, *srcs):
+    n, r = dst.shape[:2]
+    q = r // 8
+
+    def body(i, carry):
+        b, at = lax.div(i, q), pl.ds(pl.multiple_of(lax.rem(i, q) * 8, 8), 8)
+        total = dst[b, at, :]
+        for src in srcs:
+            total = total + src[b, at, :]
+        dst[b, at, :] = total
+        return carry
+
+    lax.fori_loop(0, n * q, body, 0)
+
+
+def head_sum(cm, p, o, t, f, s_sem, r_sem, finish, times, closing):
+    T = o.shape[0]
+    C = T // 4
+    H = C // 2
+    R, L, O = ahead(cm.me, 1), ahead(cm.me, 3), ahead(cm.me, 2)
+    me = cm.me
+    c = {}
+
+    def rows(k, half):
+        return pl.ds(pl.multiple_of(k * C + half * H, H), H)
+
+    def go(name, src, dst, i, n):
+        c[name] = cm.send(src, dst, s_sem.at[i], r_sem.at[i], cm.at_y(n))
+
+    @cm.when(times[0])
+    def _():
+        go("a0", p.at[rows(O, 0)], t.at[0], 0, 1)
+        go("a1", p.at[rows(O, 1)], t.at[1], 1, 3)
+        go("a2", p.at[rows(R, 1)], f.at[0, 1], 2, 1)
+        go("a3", p.at[rows(L, 0)], f.at[1, 0], 3, 3)
+
+    @cm.when(times[1])
+    def _():
+        c["a0"].wait_recv()
+        t[0] = p[rows(R, 0), :] + t[0]
+        go("a4", t.at[0], f.at[0, 0], 4, 1)
+        c["a1"].wait_recv()
+        t[1] = p[rows(L, 1), :] + t[1]
+        go("a5", t.at[1], f.at[1, 1], 5, 3)
+
+    @cm.when(times[2])
+    def _():
+        c["a3"].wait_recv()
+        c["a4"].wait_recv()
+        o[rows(me, 0), :] = finish(0, p[rows(me, 0), :] + f[0, 0] + f[1, 0])
+        go("b0", o.at[rows(me, 0)], o.at[rows(me, 0)], 6, 1)
+        go("c0", o.at[rows(me, 0)], o.at[rows(me, 0)], 8, 3)
+        c["a2"].wait_recv()
+        c["a5"].wait_recv()
+        o[rows(me, 1), :] = finish(1, p[rows(me, 1), :] + f[0, 1] + f[1, 1])
+        go("c1", o.at[rows(me, 1)], o.at[rows(me, 1)], 9, 3)
+        go("b1", o.at[rows(me, 1)], o.at[rows(me, 1)], 7, 1)
+
+    @cm.when(times[3])
+    def _():
+        c["b0"].wait_recv()
+        go("d0", o.at[rows(L, 0)], o.at[rows(L, 0)], 10, 1)
+        c["c1"].wait_recv()
+        go("d1", o.at[rows(R, 1)], o.at[rows(R, 1)], 11, 3)
+
+    @cm.when(900)
+    def _():
+        for name in ("b1", "c0", "d0", "d1"):
+            c[name].wait_recv()
+        closing()
+
+
+def scatter_ring(cm, chunk, t, f, s_sem, r_sem, base, to, times, done):
+    c = {}
+
+    def go(name, src, dst, i, n):
+        c[name] = cm.send(src, dst, s_sem.at[base + i], r_sem.at[base + i], to(n))
+
+    @cm.when(times[0])
+    def _():
+        go("a0", chunk(2, 0), t.at[0], 0, 1)
+        go("a1", chunk(2, 1), t.at[1], 1, 3)
+
+    @cm.when(times[1])
+    def _():
+        go("a2", chunk(1, 1), f.at[0, 1], 2, 1)
+
+    @cm.when(times[2])
+    def _():
+        go("a3", chunk(3, 0), f.at[1, 0], 3, 3)
+
+    @cm.when(times[3])
+    def _():
+        c["a0"].wait_recv()
+        add_up(t.at[0], chunk(1, 0))
+        go("a4", t.at[0], f.at[0, 0], 4, 1)
+        c["a1"].wait_recv()
+        add_up(t.at[1], chunk(3, 1))
+        go("a5", t.at[1], f.at[1, 1], 5, 3)
+
+    @cm.when(times[4])
+    def _():
+        c["a3"].wait_recv()
+        c["a4"].wait_recv()
+        add_up(chunk(0, 0), f.at[0, 0], f.at[1, 0])
+        c["a2"].wait_recv()
+        c["a5"].wait_recv()
+        add_up(chunk(0, 1), f.at[0, 1], f.at[1, 1])
+        done()
+
+
+def grad_scatter(cm, products, G, RC, wa, bufs, sems, times, done_a, done_b):
+    tA, tB, fA, fB, t2A, t2B, f2A, f2B = bufs
+    cs, cr, as_, ar, bs, br = sems
+    W = G.shape[-1]
+    quarter = products[0][0].shape[1] // 4
+    got = {}
+
+    def block(turn):
+        k = ahead(cm.x, turn)
+        for left, rights, at in products:
+            right = jnp.concatenate([r[...] for r in rights], axis=1)
+            w = right.shape[1]
+            lhs = left[:, pl.ds(pl.multiple_of(k * quarter, quarter), quarter)]
+            value = lax.dot_general(
+                lhs, right, (((0,), (0,)), ((), ())), preferred_element_type=jnp.float32
+            )
+            G[k, :, :, :, pl.ds(at, w)] = value.reshape(4, 2, 32, w)
+        got[turn] = cm.send(G.at[k, :, 1 - cm.core], RC.at[k], cs.at[turn], cr.at[turn], cm.twin())
+
+    def settle(turn):
+        k = ahead(cm.x, turn)
+        got[turn].wait_recv()
+        add_up(G.at[k, :, cm.core], RC.at[k])
+
+    for i, turn in enumerate((2, 1, 3, 0)):
+        cm.when(times["block"][i])(lambda turn=turn: block(turn))
+        cm.when(times["settle"][i])(lambda turn=turn: settle(turn))
+
+    cols_a, cols_b = pl.ds(0, wa), pl.ds(wa, W - wa)
+    core = cm.core
+
+    def a1(turn, half):
+        return G.at[ahead(cm.x, turn), pl.ds(half * 2, 2), core, :, cols_a]
+
+    def b1(turn, half):
+        return G.at[pl.ds(half * 2, 2), ahead(cm.z, turn), core, :, cols_b]
+
+    def a2(turn, half):
+        return G.at[cm.x, pl.ds(ahead(cm.z, turn), 1), core, pl.ds(half * 16, 16), cols_a]
+
+    def b2(turn, half):
+        return G.at[pl.ds(ahead(cm.x, turn), 1), cm.z, core, pl.ds(half * 16, 16), cols_b]
+
+    nothing = lambda: None
+    scatter_ring(cm, a1, tA, fA, as_, ar, 0, cm.at_x, times["A"], nothing)
+    scatter_ring(cm, b1, tB, fB, bs, br, 0, cm.at_z, times["B"], nothing)
+    scatter_ring(cm, a2, t2A, f2A, as_, ar, 6, cm.at_z, times["A2"], done_a)
+    scatter_ring(cm, b2, t2B, f2B, bs, br, 6, cm.at_x, times["B2"], done_b)
+
+
+def small_sums(cm, small, sm, sr, s_sem, r_sem, times, done):
+    axes = [(cm.at_z, cm.z), (cm.at_x, cm.x), (cm.at_y, cm.me)]
+    first = {}
+
+    @cm.when(times[0])
+    def _():
+        first["c"] = cm.send(small, sr.at[3, 0], s_sem.at[9], r_sem.at[9], cm.twin())
+
+    @cm.when(times[1])
+    def _():
+        first["c"].wait_recv()
+        sm[0] = small[...] + sr[3, 0]
+
+    for a, (to, here) in enumerate(axes):
+        copies = []
+
+        def begin(a=a, to=to, here=here, copies=copies):
+            sr[a, here] = sm[a]
+            for n in (1, 2, 3):
+                i = a * 3 + n - 1
+                copies.append(cm.send(sm.at[a], sr.at[a, here], s_sem.at[i], r_sem.at[i], to(n)))
+
+        def end(a=a, copies=copies):
+            for copy in copies:
+                copy.wait_recv()
+            total = (sr[a, 0] + sr[a, 1]) + (sr[a, 2] + sr[a, 3])
+            if a < 2:
+                sm[a + 1] = total
+            else:
+                done(total[0:16], sm[2][16:24])
+
+        cm.when(times[1] + 0.01)(begin) if a == 0 else cm.when(times[1 + a] + 0.01)(begin)
+        cm.when(times[2 + a])(end)
+
+
+def greet_all(cm):
+    cm.greet([axis(n) for n in (1, 2, 3) for axis in (cm.at_x, cm.at_z, cm.at_y)] + [cm.twin()])
+
+
+def middle_kernel(*refs):
+    (dn, own_resid, gain, own_cot, normed, d_gate, d_up, act, cot, down) = refs[:10]
+    (o_dres, o_res, o_gate, o_up, o_down) = refs[10:15]
+    (rp, full, yt, yf, G, RC) = refs[15:21]
+    bufs, (ys, yr), sems = refs[21:29], refs[29:31], refs[31:]
+    H = own_resid.shape[0] // 2
+    cm = Comm()
+    greet_all(cm)
+
+    def finish_dres(half, total):
+        mine = pl.ds(half * H, H)
+        return norm_back_rows(total, own_resid[mine, :], gain[...], own_cot[mine, :].astype(jnp.float32))
+
+    def finish_result(half, total):
+        return total + own_resid[pl.ds(half * H, H), :]
+
+    def rounded():
+        o_res[...] = full[...].astype(jnp.bfloat16)
+
+    @cm.when(13)
+    def _():
+        n = act.shape[0] // 4
+
+        def body(i, carry):
+            rows = pl.ds(pl.multiple_of(i * n, n), n)
+            rp[rows, :] = lax.dot_general(
+                act[rows, :], down[...], (((1,), (1,)), ((), ())), preferred_element_type=jnp.float32
+            )
+            return carry
+
+        lax.fori_loop(0, 4, body, 0)
+
+    head_sum(cm, dn, o_dres, yt.at[0], yf.at[0], ys.at[0], yr.at[0], finish_dres, (0, 6.5, 17, 30), lambda: None)
+    head_sum(cm, rp, full, yt.at[1], yf.at[1], ys.at[1], yr.at[1], finish_result, (16, 25, 35, 49), rounded)
+
+    w = act.shape[1]
+    wa = 1792
+
+    def done_a():
+        rows = G[cm.x, cm.z, cm.core, :, pl.ds(0, wa)]
+        o_gate[...] = rows[:, :w]
+        o_up[:, pl.ds(0, wa - w)] = rows[:, w:]
+
+    def done_b():
+        rows = G[cm.x, cm.z, cm.core, :, pl.ds(wa, 3 * w - wa)]
+        o_up[:, pl.ds(wa - w, 2 * w - wa)] = rows[:, : 2 * w - wa]
+        o_down[...] = rows[:, 2 * w - wa :]
+
+    times = {
+        "block": (0.1, 3, 6, 9),
+        "settle": (3.3, 6.3, 9.3, 12),
+        "A": (3.4, 6.4, 9.4, 14.5, 33),
+        "B": (12.1, 12.2, 12.3, 22, 40),
+        "A2": (33.1, 33.2, 33.3, 37, 42.5),
+        "B2": (40.1, 40.2, 40.3, 44, 50),
+    }
+    products = [(normed, [d_gate], 0), (normed, [d_up], w), (cot, [act], 2 * w)]
+    grad_scatter(cm, products, G, RC, wa, bufs, sems, times, done_a, done_b)
+    cm.run()
+
+
+def end_kernel(*refs):
+    (dm, toks, gain, d_res, normed) = refs[:5]
+    d_proj = refs[5:8]
+    (d_low, gated, small) = refs[8:11]
+    (o_tok, o_in, o_out, o_mix, o_ffn, o_conv) = refs[11:17]
+    (yt, yf, G, RC) = refs[17:21]
+    bufs = refs[21:29]
+    sm, sr = refs[29:31]
+    ys, yr = refs[31:33]
+    sems = refs[33:39]
+    ss, sr_sem = refs[39:]
+    H = toks.shape[0] // 2
+    cm = Comm()
+    greet_all(cm)
+
+    def finish_tokens(half, total):
+        mine = pl.ds(half * H, H)
+        return norm_back_rows(total, toks[mine, :].astype(jnp.float32), gain[...], d_res[mine, :])
+
+    head_sum(cm, dm, o_tok, yt, yf, ys, yr, finish_tokens, (0, 6.5, 17, 26), lambda: None)
+
+    wa = 512
+
+    def done_a():
+        rows = G[cm.x, cm.z, cm.core, :, pl.ds(0, wa)]
+        o_in[0] = rows[:, :256]
+        o_in[1] = rows[:, 256:]
+
+    def done_b():
+        rows = G[cm.x, cm.z, cm.core, :, pl.ds(wa, 512)]
+        o_in[2] = rows[:, :256]
+        o_out[...] = rows[:, 256:]
+
+    times = {
+        "block": (0.1, 1, 2, 3),
+        "settle": (1.5, 2.5, 3.5, 4.5),
+        "A": (1.6, 2.6, 3.6, 6, 14),
+        "B": (4.6, 4.7, 4.8, 8.5, 16),
+        "A2": (14.1, 14.2, 14.3, 17.2, 20),
+        "B2": (16.1, 16.2, 16.3, 18.5, 21),
+    }
+    products = [(normed, d_proj, 0), (d_low, [gated], 768)]
+    grad_scatter(cm, products, G, RC, wa, bufs, sems, times, done_a, done_b)
+
+    def small_done(gains, rest):
+        o_mix[...] = gains[0:8]
+        o_ffn[...] = gains[8:16]
+        for k in range(3):
+            for h in range(2):
+                o_conv[k : k + 1, pl.ds(128 * h, 128)] = rest[2 * k + h : 2 * k + h + 1]
+
+    small_sums(cm, small, sm, sr, ss, sr_sem, (0.05, 5, 9, 15, 22), small_done)
+    cm.run()
+
+
+VMEM_SPEC = pl.BlockSpec(memory_space=pltpu.VMEM)
+
+
+def call(kernel, name, cid, args, outs, scratch, limit):
+    return pl.pallas_call(
+        kernel,
+        out_shape=outs,
+        in_specs=[VMEM_SPEC] * len(args),
+        out_specs=(VMEM_SPEC,) * len(outs),
+        scratch_shapes=scratch,
+        compiler_params=pltpu.CompilerParams(
+            collective_id=cid, has_side_effects=True, vmem_limit_bytes=limit << 20
+        ),
+        cost_estimate=pl.CostEstimate(flops=1, bytes_accessed=1, transcendentals=0),
+        name=name,
+    )(*args)
+
+
+def scatter_scratch(W, wa):
+    f32 = jnp.float32
+    wb = W - wa
+    return [
+        pltpu.VMEM((4, 4, 2, 32, W), f32),
+        pltpu.VMEM((4, 4, 32, W), f32),
+        pltpu.VMEM((2, 2, 32, wa), f32),
+        pltpu.VMEM((2, 2, 32, wb), f32),
+        pltpu.VMEM((2, 2, 2, 32, wa), f32),
+        pltpu.VMEM((2, 2, 2, 32, wb), f32),
+        pltpu.VMEM((2, 1, 16, wa), f32),
+        pltpu.VMEM((2, 1, 16, wb), f32),
+        pltpu.VMEM((2, 2, 1, 16, wa), f32),
+        pltpu.VMEM((2, 2, 1, 16, wb), f32),
+    ]
+
+
+SCATTER_SEMS = [pltpu.SemaphoreType.DMA((n,)) for n in (4, 4, 12, 12, 12, 12)]
+
+
+def middle(dn, own_resid, gain, own_cot, normed, d_gate, d_up, act, cot, down):
+    T, D = dn.shape
+    H = T // 8
+    f32, shape, dma = jnp.float32, jax.ShapeDtypeStruct, pltpu.SemaphoreType.DMA
+    w = act.shape[1]
+    outs = (shape((T, D), f32), shape((T, D), jnp.bfloat16)) + (shape((32, w), f32),) * 3
+    scratch = [
+        pltpu.VMEM((T, D), f32),
+        pltpu.VMEM((T, D), f32),
+        pltpu.VMEM((2, 2, H, D), f32),
+        pltpu.VMEM((2, 2, 2, H, D), f32),
+        *scatter_scratch(3 * w, 1792),
+        dma((2, 12)),
+        dma((2, 12)),
+        *SCATTER_SEMS,
+    ]
+    args = (dn, own_resid, gain, own_cot, normed, d_gate, d_up, act, cot, down)
+    return call(middle_kernel, "middle", 5, args, outs, scratch, 56)
+
+
+def end(dm, toks, gain, d_res, normed, d_proj, d_low, gated, small):
+    T, D = dm.shape
+    H = T // 8
+    f32, shape, dma = jnp.float32, jax.ShapeDtypeStruct, pltpu.SemaphoreType.DMA
+    outs = (
+        shape((T, D), f32),
+        shape((3, 32, 256), f32),
+        shape((32, 256), f32),
+        shape((8, 128), f32),
+        shape((8, 128), f32),
+        shape((3, 256), f32),
+    )
+    scratch = [
+        pltpu.VMEM((2, H, D), f32),
+        pltpu.VMEM((2, 2, H, D), f32),
+        *scatter_scratch(1024, 512),
+        pltpu.VMEM((3, 24, 128), f32),
+        pltpu.VMEM((4, 4, 24, 128), f32),
+        dma((12,)),
+        dma((12,)),
+        *SCATTER_SEMS,
+        dma((10,)),
+        dma((10,)),
+    ]
+    args = (dm, toks, gain, d_res, normed, *d_proj, d_low, gated, small)
+    return call(end_kernel, "end", 7, args, outs, scratch, 40)
+
+
+def place(*arrays):
+    n = len(arrays)
+
+    def kernel(*refs):
+        copies = [pltpu.make_async_copy(refs[i], refs[n + i], refs[2 * n].at[i]) for i in range(n)]
+        for copy in copies:
+            copy.start()
+        for copy in copies:
+            copy.wait()
+
+    anywhere = pl.BlockSpec(memory_space=pl.ANY)
+    return pl.pallas_call(
+        kernel,
+        out_shape=tuple(jax.ShapeDtypeStruct(a.shape, a.dtype) for a in arrays),
+        in_specs=[anywhere] * n,
+        out_specs=(anywhere,) * n,
+        scratch_shapes=[pltpu.SemaphoreType.DMA((n,))],
+        name="place",
+    )(*arrays)
+
+
 def from_behind(block, axis, distance):
     devices = range(lax.axis_size(axis))
     route = [(i - distance, i) for i in devices if i - distance in devices]
@@ -162,16 +639,6 @@
     return lax.dot_general(
         left, right, (((1,), (1,)), ((), ())), preferred_element_type=jnp.float32
     )
-
-
-def token_product(left, right):
-    return lax.dot_general(
-        left, right, (((0,), (0,)), ((), ())), preferred_element_type=jnp.float32
-    )
-
-
-def shared(grad):
-    return lax.psum_scatter(grad, "seq", scatter_dimension=0, tiled=True)
 
 
 def on_device(
@@ -228,19 +695,22 @@
     d_act = jnp.dot(cotangent, down_weight, preferred_element_type=jnp.float32)
     d_gate = (d_act * upper * sigma * (1.0 + gate * (1.0 - sigma))).astype(jnp.bfloat16)
     d_up = (d_act * gate * sigma).astype(jnp.bfloat16)
-    grad_down = token_product(cotangent, act)
-    grad_gate = token_product(ffn_normed, d_gate)
-    grad_up = token_product(ffn_normed, d_up)
-    down_share, gate_share, up_share = shared(grad_down), shared(grad_gate), shared(grad_up)
     d_normed_part = right_product(d_gate, gate_weight) + right_product(d_up, up_weight)
     grad_ffn_gain = jnp.sum(d_normed_part * resid * ffn_scale, axis=0)
-    d_normed_part, _, _, _ = lax.optimization_barrier((d_normed_part, grad_down, grad_gate, grad_up))
-    (d_resid,) = ring(
-        [("norm", d_normed_part, own_rows(resid), ffn_gain[None], own_rows(cotangent))], 2
+    d_resid, result, gate_share, up_share, down_share = middle(
+        d_normed_part,
+        own_rows(resid),
+        ffn_gain[None],
+        own_rows(cotangent),
+        ffn_normed,
+        d_gate,
+        d_up,
+        act,
+        cotangent,
+        down_weight,
     )
     d_resid_low = d_resid.astype(jnp.bfloat16)
     d_gated = jnp.dot(d_resid_low, out_weight, preferred_element_type=jnp.float32)
-    grad_out = token_product(d_resid_low, gated)
     d_chan_c = d_gated * conv_out
     d_conv = d_gated * chan_c
     tail_rows = from_behind(d_conv[:2], "seq", -1)
@@ -257,35 +727,64 @@
             jnp.sum(d_conv * far_own * prev_two, axis=0),
         ]
     )
-    d_projected = jnp.stack([d_mixed * chan_x, d_chan_c, d_mixed * chan_b], axis=1).astype(
-        jnp.bfloat16
-    )
-    grad_in = jnp.einsum("td,tkc->dkc", mix_normed, d_projected, preferred_element_type=jnp.float32)
-    in_share = shared(grad_in)
-    out_share = shared(grad_out)
+    d_projected = [p.astype(jnp.bfloat16) for p in (d_mixed * chan_x, d_chan_c, d_mixed * chan_b)]
     d_mix_part = jnp.einsum(
-        "tkc,dkc->td", d_projected, in_weight, preferred_element_type=jnp.float32
+        "tkc,dkc->td",
+        jnp.stack(d_projected, axis=1),
+        in_weight,
+        preferred_element_type=jnp.float32,
     )
     grad_mix_gain = jnp.sum(d_mix_part * inputs * mix_scale, axis=0)
-    gain_totals = lax.psum(jnp.stack([grad_mix_gain, grad_ffn_gain]), ("seq", "head"))
-    conv_total = lax.psum(grad_conv, "seq")
-    result_part = right_product(act, down_weight)
-    d_mix_part, result_part, _, _ = lax.optimization_barrier((d_mix_part, result_part, grad_in, grad_out))
-    grad_tokens, result = ring(
+    small = jnp.concatenate(
         [
-            ("norm", d_mix_part, own_rows(tokens), mix_gain[None], own_rows(d_resid)),
-            ("add", result_part, own_rows(resid)),
-        ],
-        3,
-    )
-    return (
-        result.astype(jnp.bfloat16),
+            grad_mix_gain.reshape(8, 128),
+            grad_ffn_gain.reshape(8, 128),
+            grad_conv.reshape(6, 128),
+            jnp.zeros((2, 128), jnp.float32),
+        ]
+    )
+    grad_tokens, in_share, out_share, mix_total, ffn_total, conv_total = end(
+        d_mix_part,
+        own_rows(tokens),
+        mix_gain[None],
+        own_rows(d_resid),
+        mix_normed,
+        d_projected,
+        d_resid_low,
+        gated,
+        small,
+    )
+    (
+        result,
         grad_tokens,
-        gain_totals[0],
+        mix_total,
         in_share,
         conv_total,
         out_share,
-        gain_totals[1],
+        ffn_total,
+        gate_share,
+        up_share,
+        down_share,
+    ) = place(
+        result,
+        grad_tokens,
+        mix_total,
+        in_share,
+        conv_total,
+        out_share,
+        ffn_total,
+        gate_share,
+        up_share,
+        down_share,
+    )
+    return (
+        result,
+        grad_tokens,
+        mix_total.reshape(-1),
+        in_share.transpose(1, 0, 2),
+        conv_total,
+        out_share,
+        ffn_total.reshape(-1),
         gate_share,
         up_share,
         down_share,

time: 572 us -> 332 us (0.58)
  waiting for transfers between devices: 205 us -> 1.69 us
  Pallas kernels: 152 us -> 286 us
  blocking collectives: 128 us -> 0 us
  matrix products: 43.1 us -> 15.8 us
  between operations: 14.3 us -> 1.25 us
    pallas_call x0 -> x3, Pallas kernels: none -> 244 us  [the longest x2 130 us: call(): pl.pallas_call(kernel, out_shape=outs, in_specs=[VMEM_SPEC] * len(args),...]
    psum x2 -> x0, blocking collectives: 128 us -> none  [the longest x1 65.7 us: on_device(): conv_total = lax.psum(grad_conv, 'seq')]
    reduce_scatter x4 -> x0, waiting for transfers between devices: 115 us -> none  [shared(): return lax.psum_scatter(grad, 'seq', scatter_dimension=0, tiled=True)]
    pallas_call x3 -> x1, Pallas kernels: 152 us -> 42.5 us  [ring(): pl.pallas_call(lambda *refs: ring_kernel(kinds, *refs), out_shape=tuple((...]
    unnamed x6 -> x0, waiting for transfers between devices: 88.4 us -> none
    dot_general x6 -> x1, matrix products: 18 us -> 1.04 us  [on_device(): jnp.einsum('tkc,dkc->td', jnp.stack(d_projected, axis=1), in_weight, pref...]
    unnamed x56 -> x64, local copies, waits for them, and re-layouts: 15.2 us -> 7.59 us
    dot_general x4 -> x3, matrix products: 11.4 us -> 4.98 us  [right_product(): lax.dot_general(left, right, (((1,), (1,)), ((), ())), preferred_element_...]
  transfers between devices with their start and end apart: 7 -> 2, of which waited for: 4 -> 1; matrix products, arithmetic and copies ran while one was open for 4% -> 2% of each run, Pallas kernels for 12% -> 0%
where the time goes in v3:
time: 332 us; the launch traced here: 331 us
  Pallas kernels  286 us (86%)
  matrix products  15.8 us (5%)
  local copies, waits for them, and re-layouts  13.5 us (4%)
  other arithmetic  10.1 us (3%)
    pallas_call x2, Pallas kernels, call(): pl.pallas_call(kernel, out_shape=outs, in_specs=[VMEM_SPEC] * len(args),...  130 us
    pallas_call x1, Pallas kernels, place(): pl.pallas_call(kernel, out_shape=tuple((jax.ShapeDtypeStruct(a.shape, a.d...  114 us
    pallas_call x1, Pallas kernels, ring(): pl.pallas_call(lambda *refs: ring_kernel(kinds, *refs), out_shape=tuple((...  42.5 us
    unnamed x64, local copies, waits for them, and re-layouts  7.59 us
  transfers between devices with their start and end apart: 2, of which 1 were waited for; matrix products, arithmetic and copies ran while one was open for 2% of the time, Pallas kernels for 0%

profile of v3, /device:TPU:0, one launch (start us, length us, event | category | flops | bytes accessed | tf_op | source)
XLA Modules:
  0.0 331.1 jit_solution(10434863351582877117)
XLA Ops:
  0.7 1.7 fusion
  2.3 1.5 fusion.2.refs_4_
  3.9 1.0 fusion.5
  5.0 1.1 copy-done.16
  6.1 1.3 collective-permute-start
  8.7 3.6 %fusion.28 = f32[512,1152]{1,0:T(8,128)S(1)} fusion(bf16[512,1024]{1,0:T(8,128)(2,1)} %refs_8_.1, bf16[1024,1152]{1,0:T(8,128)(2,1)} %refs_9_.1), kind=kOutput, calls=%fused_computation.65 | convolution fusion | flops 1207959552 | bytes 5767168 | tf_op jit(solution)/shard_map/dot_general | solution.py:695
  12.4 1.7 constant_dynamic-slice_fusion.1.refs_3_
  15.2 42.5 %ring1.1 = f32[512,1024]{1,0:T(8,128)S(1)} custom-call(f32[512,1024]{1,0:T(8,128)S(1)} %fusion.29.refs_0_, bf16[128,1024]{1,0:T(8,128)(2,1)S(1)} %constant_dynamic-slice_fusion.3.refs_1_), custom_call_target="tpu_custom_call" | custom-call | flops 1 | bytes 1 | tf_op jit(solution)/shard_map/ring1/pallas_call | solution.py:135
  59.8 1.5 fusion.30
  61.3 3.2 multiply_convert_fusion
  64.6 1.5 fusion.31
  66.1 3.0 multiply_reduce_fusion
  69.1 85.3 %middle.1 = (f32[512,1024]{1,0:T(8,128)}, bf16[512,1024]{1,0:T(8,128)(2,1)}, f32[32,1152]{1,0:T(8,128)}, f32[32,1152]{1,0:T(8,128)}, f32[32,1152]{1,0:T(8,128)}) custom-call(f32[512,1024]{1,0:T(8,128)} %get-tuple-element.74.refs_0_, f32[128,1024]{1,0:T(8,128)} %constant_dynamic-slice_fusion.2.refs_1_, f32[1,1024]{1,0:T(1,128)} %bitcast.60, ...), custom_call_target="tpu_custom_call" | custom-call | flops 1 | bytes 1 | tf_op jit(solution)/shard_map/middle/pallas_call | solution.py:525
  154.4 1.7 convert_element_type.52.refs_8_
  156.1 1.9 constant_dynamic-slice_fusion.refs_3_
  158.5 1.0 multiply_reduce_fusion.3
  160.3 1.3 collective-permute-start.1
  161.7 1.7 collective-permute-done.1
  163.4 2.1 multiply_convert_fusion.6
  165.5 1.1 multiply_convert_fusion.4.refs_7_
  166.6 1.0 fusion.4
  168.1 44.3 %end.1 = (f32[512,1024]{1,0:T(8,128)S(1)}, f32[3,32,256]{2,1,0:T(8,128)S(1)}, f32[32,256]{1,0:T(8,128)S(1)}, f32[8,128]{1,0:T(8,128)S(1)}, f32[8,128]{1,0:T(8,128)S(1)}, /*index=5*/f32[3,256]{1,0:T(4,128)S(1)}) custom-call(f32[512,1024]{1,0:T(8,128)S(1)} %get-tuple-element.76.refs_0_, bf16[128,1024]{1,0:T(8,128)(2,1)S(1)} %copy-done.4, ...), custom_call_target="tpu_custom_call" | custom-call | flops 1 | bytes 1 | tf_op jit(solution)/shard_map/end/pallas_call | solution.py:525
  212.4 1.3 copy-done.8
  216.7 114.2 %place.1 = (bf16[512,1024]{1,0:T(8,128)(2,1)}, f32[512,1024]{1,0:T(8,128)}, f32[8,128]{1,0:T(8,128)}, f32[3,32,256]{2,1,0:T(8,128)}, f32[3,256]{1,0:T(4,128)}, /...) custom-call(bf16[512,1024]{1,0:T(8,128)(2,1)} %get-tuple-element.31.re, ...), custom_call_target="tpu_custom_call" | custom-call | tf_op jit(solution)/shard_map/place/pallas_call | solution.py:618
  (87 shorter events, 9.3 us)
Async XLA Ops:
  0.6 60.7 %copy-start = (bf16[1024,1152]{1,0:T(8,128)(2,1)S(1)}, bf16[1024,1152]{1,0:T(8,128)(2,1)}, u32[]{:S(2)}) copy-start(bf16[1024,1152]{1,0:T(8,128)(2,1)} %param.19) | copy-start | bytes 7077892
  0.7 3.2 copy-start.30
  3.9 3.5 %copy-start.26 = (s32[16384]{0:T(1024)S(1)}, s32[16384]{0:T(1024)}, u32[]{:S(2)}) copy-start(s32[16384]{0:T(1024)} %param.12) | copy-start | bytes 196612
  3.9 3.8 %copy-start.28 = (bf16[3,256]{1,0:T(4,128)(2,1)S(1)}, bf16[3,256]{1,0:T(4,128)(2,1)}, u32[]{:S(2)}) copy-start(bf16[3,256]{1,0:T(4,128)(2,1)} %param.15) | copy-start | bytes 4612
  6.1 8.0 %copy-start.19 = (f32[512,256]{1,0:T(8,128)}, f32[512,256]{1,0:T(8,128)S(1)}, u32[]{:S(2)}) copy-start(f32[512,256]{1,0:T(8,128)S(1)} %fusion.19) | copy-start | bytes 1572868
  6.1 8.0 %collective-permute-start = (f32[2,256]{1,0:T(2,128)S(1)}, f32[2,256]{1,0:T(2,128)S(1)}, u32[]{:S(2)}, u32[]{:S(2)}) collective-permute-start(f32[2,256]{1,0:T(2,128)S(1)} %slice.85), channel_id=1, source_target_pairs={{0,4},{4,8},{8,12},{12,16},{16,20},{20,24},{24,28},{28,32},{32,36}... | collective-permute-start | bytes 6152 | tf_op jit(solution)/shard_map/ppermute | solution.py:631
  8.7 6.5 %copy-start.3 = (bf16[128,1024]{1,0:T(8,128)(2,1)}, bf16[128,1024]{1,0:T(8,128)(2,1)S(1)}, u32[]{:S(2)}) copy-start(bf16[128,1024]{1,0:T(8,128)(2,1)S(1)} %constant_dynamic-slice_fusion.3.refs_1_) | copy-start | bytes 786436
  8.7 5.4 %copy-start.17 = (f32[512,3,256]{2,0,1:T(8,128)S(1)}, f32[512,3,256]{2,0,1:T(8,128)}, u32[]{:S(2)}) copy-start(f32[512,3,256]{2,0,1:T(8,128)} %copy-done.16) | copy-start | bytes 4718596
  12.4 2.0 copy-start.24
  57.9 1.9 copy-start.29
  59.8 1.5 copy-start.22
  64.6 1.6 copy-start.25
  64.6 1.6 copy-start.21
  156.1 2.4 copy-start.20
  160.3 3.0 collective-permute-start.1
  161.7 4.9 %copy-start.9 = (bf16[512,256]{1,0:T(8,128)(2,1)S(1)}, bf16[512,256]{1,0:T(8,128)(2,1)}, u32[]{:S(2)}) copy-start(bf16[512,256]{1,0:T(8,128)(2,1)} %get-tuple-element.63.refs_6_) | copy-start | bytes 786436
  161.7 4.9 %copy-start.18 = (bf16[512,1024]{1,0:T(8,128)(2,1)S(1)}, bf16[512,1024]{1,0:T(8,128)(2,1)}, u32[]{:S(2)}) copy-start(bf16[512,1024]{1,0:T(8,128)(2,1)} %param.11) | copy-start | bytes 3145732
  161.7 4.9 %copy-start.31 = (bf16[1024,3,256]{2,0,1:T(8,128)(2,1)S(1)}, bf16[1024,3,256]{2,0,1:T(8,128)(2,1)}, u32[]{:S(2)}) copy-start(bf16[1024,3,256]{2,0,1:T(8,128)(2,1)} %param.14) | copy-start | bytes 4718596
  166.6 1.2 copy-start.2
  166.6 1.3 copy-start.4
  166.6 1.3 copy-start.6
  166.6 1.5 copy-start.7
  166.6 1.5 copy-start.12
  212.4 1.3 copy-start.8
  (10 other events, 7.8 us)

commit v4 on v3

--- a/solution.py
+++ b/solution.py
@@ -421,21 +421,14 @@
     def rounded():
         o_res[...] = full[...].astype(jnp.bfloat16)
 
-    @cm.when(13)
-    def _():
-        n = act.shape[0] // 4
-
-        def body(i, carry):
-            rows = pl.ds(pl.multiple_of(i * n, n), n)
-            rp[rows, :] = lax.dot_general(
-                act[rows, :], down[...], (((1,), (1,)), ((), ())), preferred_element_type=jnp.float32
-            )
-            return carry
-
-        lax.fori_loop(0, 4, body, 0)
-
-    head_sum(cm, dn, o_dres, yt.at[0], yf.at[0], ys.at[0], yr.at[0], finish_dres, (0, 6.5, 17, 30), lambda: None)
-    head_sum(cm, rp, full, yt.at[1], yf.at[1], ys.at[1], yr.at[1], finish_result, (16, 25, 35, 49), rounded)
+    @cm.when(0.02)
+    def _():
+        rp[...] = lax.dot_general(
+            act[...], down[...], (((1,), (1,)), ((), ())), preferred_element_type=jnp.float32
+        )
+
+    head_sum(cm, dn, o_dres, yt.at[0], yf.at[0], ys.at[0], yr.at[0], finish_dres, (0, 7, 28, 43), lambda: None)
+    head_sum(cm, rp, full, yt.at[1], yf.at[1], ys.at[1], yr.at[1], finish_result, (0.03, 18, 36, 56), rounded)
 
     w = act.shape[1]
     wa = 1792
@@ -451,12 +444,12 @@
         o_down[...] = rows[:, 2 * w - wa :]
 
     times = {
-        "block": (0.1, 3, 6, 9),
-        "settle": (3.3, 6.3, 9.3, 12),
-        "A": (3.4, 6.4, 9.4, 14.5, 33),
-        "B": (12.1, 12.2, 12.3, 22, 40),
-        "A2": (33.1, 33.2, 33.3, 37, 42.5),
-        "B2": (40.1, 40.2, 40.3, 44, 50),
+        "block": (4, 5.5, 7.5, 9),
+        "settle": (7.1, 8.5, 10, 12),
+        "A": (7.2, 8.6, 10.1, 18.5, 42),
+        "B": (12.1, 12.2, 12.3, 24, 45),
+        "A2": (42.1, 42.2, 42.3, 46, 52),
+        "B2": (45.1, 45.2, 45.3, 49, 55),
     }
     products = [(normed, [d_gate], 0), (normed, [d_up], w), (cot, [act], 2 * w)]
     grad_scatter(cm, products, G, RC, wa, bufs, sems, times, done_a, done_b)
@@ -618,7 +611,7 @@
     return pl.pallas_call(
         kernel,
         out_shape=tuple(jax.ShapeDtypeStruct(a.shape, a.dtype) for a in arrays),
-        in_specs=[anywhere] * n,
+        in_specs=[VMEM_SPEC] * n,
         out_specs=(anywhere,) * n,
         scratch_shapes=[pltpu.SemaphoreType.DMA((n,))],
         name="place",

time: 332 us -> 218 us (0.66)
  Pallas kernels: 286 us -> 173 us
    pallas_call x1, Pallas kernels: 114 us -> 3.94 us  [place(): pl.pallas_call(kernel, out_shape=tuple((jax.ShapeDtypeStruct(a.shape, a.d...]
    pallas_call x2, Pallas kernels: 130 us -> 126 us  [call(): pl.pallas_call(kernel, out_shape=outs, in_specs=[VMEM_SPEC] * len(args),...]
  transfers between devices with their start and end apart: 2 -> 2, of which waited for: 1 -> 1; matrix products, arithmetic and copies ran while one was open for 2% -> 3% of each run, Pallas kernels for 0% -> 0%
where the time goes in v4:
time: 218 us
  Pallas kernels  173 us (79%)
  matrix products  15.8 us (7%)
  local copies, waits for them, and re-layouts  13.5 us (6%)
  other arithmetic  10.1 us (5%)
  starting transfers between devices  2.56 us (1%)
    pallas_call x2, Pallas kernels, call(): pl.pallas_call(kernel, out_shape=outs, in_specs=[VMEM_SPEC] * len(args),...  126 us
    pallas_call x1, Pallas kernels, ring(): pl.pallas_call(lambda *refs: ring_kernel(kinds, *refs), out_shape=tuple((...  42.5 us
    unnamed x64, local copies, waits for them, and re-layouts  7.59 us
    dynamic_slice x4, local copies, waits for them, and re-layouts, own_rows(): return lax.dynamic_slice_in_dim(x, own_at, own, 0)  5.51 us
    dot_general x3, matrix products, right_product(): lax.dot_general(left, right, (((1,), (1,)), ((), ())), preferred_element_...  4.98 us
  transfers between devices with their start and end apart: 2, of which 1 were waited for; matrix products, arithmetic and copies ran while one was open for 3% of the time, Pallas kernels for 0%

profile of v4, /device:TPU:0, one launch (start us, length us, event | category | flops | bytes accessed | tf_op | source)
XLA Modules:
  0.0 217.5 jit_solution(6709198536184517995)
XLA Ops:
  0.7 1.7 fusion
  2.3 1.5 fusion.2.refs_4_
  3.9 1.0 fusion.5
  5.0 1.1 copy-done.16
  6.1 1.3 collective-permute-start
  8.7 3.6 %fusion.28 = f32[512,1152]{1,0:T(8,128)S(1)} fusion(bf16[512,1024]{1,0:T(8,128)(2,1)} %refs_8_.1, bf16[1024,1152]{1,0:T(8,128)(2,1)} %refs_9_.1), kind=kOutput, calls=%fused_computation.65 | convolution fusion | flops 1207959552 | bytes 5767168 | tf_op jit(solution)/shard_map/dot_general | solution.py:688
  12.4 1.7 constant_dynamic-slice_fusion.1.refs_3_
  15.2 42.5 %ring1.1 = f32[512,1024]{1,0:T(8,128)S(1)} custom-call(f32[512,1024]{1,0:T(8,128)S(1)} %fusion.29.refs_0_, bf16[128,1024]{1,0:T(8,128)(2,1)S(1)} %constant_dynamic-slice_fusion.3.refs_1_), custom_call_target="tpu_custom_call" | custom-call | flops 1 | bytes 1 | tf_op jit(solution)/shard_map/ring1/pallas_call | solution.py:135
  59.8 1.5 fusion.30
  61.3 3.2 %multiply_convert_fusion = (bf16[512,1152]{1,0:T(8,128)(2,1)}, bf16[512,1152]{1,0:T(8,128)(2,1)S(1)}, bf16[512,1152]{1,0:T(8,128)(2,1)S(1)}) fusion(f32[512,1152]{1,0:T(8,128)S(1)} %fusion.30, f32[512,1152]{1,0:T(8,128)S(1)} %fusion.28, bf16[512,1024]{1,0:T(8,128)(2,1)S(1)} %multiply_convert_fusion.3.refs_4_, bf16[1024,1152]{1,0:T(8,128)(2,1)S(1)} %copy-done), kind=kOutput, calls=%fused_computation.3 | convolution fusion | flops 1217396736 | bytes 11665408 | tf_op jit(solution)/shard_map/dot_general | solution.py:685
  64.6 1.5 fusion.31
  66.1 3.0 %multiply_reduce_fusion = (f32[1024]{0:T(1024)S(1)}, f32[512,1024]{1,0:T(8,128)}) fusion(f32[512,1024]{1,0:T(8,128)S(1)} %ring1.1, f32[512]{0:T(512)S(1)} %add_rsqrt_fusion, f32[512,1024]{1,0:T(8,128)S(1)} %fusion.31, bf16[512,1152]{1,0:T(8,128)(2,1)S(1)} %get-tuple-element.62.refs_6_, bf16[1024,1152]{1,0:T(8,128)(2,1)S(1)} %copy-done), kind=kOutput, calls=%fused_computation.12 | convolution fusion | flops 1210055680 | bytes 9836544 | tf_op jit(solution)/shard_map/dot_general | solution.py:632
  69.1 81.9 %middle.1 = (f32[512,1024]{1,0:T(8,128)}, bf16[512,1024]{1,0:T(8,128)(2,1)}, f32[32,1152]{1,0:T(8,128)}, f32[32,1152]{1,0:T(8,128)}, f32[32,1152]{1,0:T(8,128)}) custom-call(f32[512,1024]{1,0:T(8,128)} %get-tuple-element.74.refs_0_, f32[128,1024]{1,0:T(8,128)} %constant_dynamic-slice_fusion.2.refs_1_, f32[1,1024]{1,0:T(1,128)} %bitcast.60, ...), custom_call_target="tpu_custom_call" | custom-call | flops 1 | bytes 1 | tf_op jit(solution)/shard_map/middle/pallas_call | solution.py:518
  151.1 1.7 convert_element_type.52.refs_8_
  152.8 1.9 constant_dynamic-slice_fusion.refs_3_
  155.2 1.0 multiply_reduce_fusion.3
  157.0 1.3 collective-permute-start.1
  158.4 1.7 collective-permute-done.1
  160.1 2.1 multiply_convert_fusion.6
  162.1 1.1 multiply_convert_fusion.4.refs_7_
  163.3 1.0 fusion.4
  164.8 44.3 %end.1 = (f32[512,1024]{1,0:T(8,128)S(1)}, f32[3,32,256]{2,1,0:T(8,128)S(1)}, f32[32,256]{1,0:T(8,128)S(1)}, f32[8,128]{1,0:T(8,128)S(1)}, f32[8,128]{1,0:T(8,128)S(1)}, /*index=5*/f32[3,256]{1,0:T(4,128)S(1)}) custom-call(f32[512,1024]{1,0:T(8,128)S(1)} %get-tuple-element.76.refs_0_, bf16[128,1024]{1,0:T(8,128)(2,1)S(1)} %copy-done.4, ...), custom_call_target="tpu_custom_call" | custom-call | flops 1 | bytes 1 | tf_op jit(solution)/shard_map/end/pallas_call | solution.py:518
  209.1 1.3 copy-done.8
  213.4 3.9 %place.1 = (bf16[512,1024]{1,0:T(8,128)(2,1)}, f32[512,1024]{1,0:T(8,128)}, f32[8,128]{1,0:T(8,128)}, f32[3,32,256]{2,1,0:T(8,128)}, f32[3,256]{1,0:T(4,128)}, /...) custom-call(bf16[512,1024]{1,0:T(8,128)(2,1)} %get-tuple-element.31.re, ...), custom_call_target="tpu_custom_call" | custom-call | tf_op jit(solution)/shard_map/place/pallas_call | solution.py:611
  (87 shorter events, 9.3 us)
Async XLA Ops:
  0.6 60.7 %copy-start = (bf16[1024,1152]{1,0:T(8,128)(2,1)S(1)}, bf16[1024,1152]{1,0:T(8,128)(2,1)}, u32[]{:S(2)}) copy-start(bf16[1024,1152]{1,0:T(8,128)(2,1)} %param.19) | copy-start | bytes 7077892
  0.7 3.2 %copy-start.30 = (bf16[1024,3,256]{2,0,1:T(8,128)(2,1)S(1)}, bf16[1024,3,256]{2,0,1:T(8,128)(2,1)}, u32[]{:S(2)}) copy-start(bf16[1024,3,256]{2,0,1:T(8,128)(2,1)} %param.14) | copy-start | bytes 4718596
  3.9 3.5 %copy-start.26 = (s32[16384]{0:T(1024)S(1)}, s32[16384]{0:T(1024)}, u32[]{:S(2)}) copy-start(s32[16384]{0:T(1024)} %param.12) | copy-start | bytes 196612
  3.9 3.8 %copy-start.28 = (bf16[3,256]{1,0:T(4,128)(2,1)S(1)}, bf16[3,256]{1,0:T(4,128)(2,1)}, u32[]{:S(2)}) copy-start(bf16[3,256]{1,0:T(4,128)(2,1)} %param.15) | copy-start | bytes 4612
  6.1 8.0 %copy-start.19 = (f32[512,256]{1,0:T(8,128)}, f32[512,256]{1,0:T(8,128)S(1)}, u32[]{:S(2)}) copy-start(f32[512,256]{1,0:T(8,128)S(1)} %fusion.19) | copy-start | bytes 1572868
  6.1 8.0 %collective-permute-start = (f32[2,256]{1,0:T(2,128)S(1)}, f32[2,256]{1,0:T(2,128)S(1)}, u32[]{:S(2)}, u32[]{:S(2)}) collective-permute-start(f32[2,256]{1,0:T(2,128)S(1)} %slice.85), channel_id=1, source_target_pairs={{0,4},{4,8},{8,12},{12,16},{16,20},{20,24},{24,28},{28,32},{32,36}... | collective-permute-start | bytes 6152 | tf_op jit(solution)/shard_map/ppermute | solution.py:624
  8.7 6.5 %copy-start.3 = (bf16[128,1024]{1,0:T(8,128)(2,1)}, bf16[128,1024]{1,0:T(8,128)(2,1)S(1)}, u32[]{:S(2)}) copy-start(bf16[128,1024]{1,0:T(8,128)(2,1)S(1)} %constant_dynamic-slice_fusion.3.refs_1_) | copy-start | bytes 786436
  8.7 5.4 %copy-start.17 = (f32[512,3,256]{2,0,1:T(8,128)S(1)}, f32[512,3,256]{2,0,1:T(8,128)}, u32[]{:S(2)}) copy-start(f32[512,3,256]{2,0,1:T(8,128)} %copy-done.16) | copy-start | bytes 4718596
  12.4 2.0 copy-start.24
  57.9 1.9 copy-start.29
  59.8 1.5 copy-start.22
  64.6 1.6 copy-start.25
  64.6 1.6 copy-start.21
  152.8 2.4 %copy-start.20 = (f32[512,256]{1,0:T(8,128)S(1)}, f32[512,256]{1,0:T(8,128)}, u32[]{:S(2)}) copy-start(f32[512,256]{1,0:T(8,128)} %copy-done.19) | copy-start | bytes 1572868
  157.0 3.0 %collective-permute-start.1 = (f32[2,256]{1,0:T(2,128)S(1)}, f32[2,256]{1,0:T(2,128)S(1)}, u32[]{:S(2)}, u32[]{:S(2)}) collective-permute-start(f32[2,256]{1,0:T(2,128)S(1)} %slice.89), channel_id=1, source_target_pairs={{4,0},{8,4},{12,8},{16,12},{20,16},{24,20},{28,24},{32,28},{36,32}... | collective-permute-start | bytes 6152 | tf_op jit(solution)/shard_map/ppermute | solution.py:624
  158.3 4.9 %copy-start.9 = (bf16[512,256]{1,0:T(8,128)(2,1)S(1)}, bf16[512,256]{1,0:T(8,128)(2,1)}, u32[]{:S(2)}) copy-start(bf16[512,256]{1,0:T(8,128)(2,1)} %get-tuple-element.63.refs_6_) | copy-start | bytes 786436
  158.4 4.9 %copy-start.18 = (bf16[512,1024]{1,0:T(8,128)(2,1)S(1)}, bf16[512,1024]{1,0:T(8,128)(2,1)}, u32[]{:S(2)}) copy-start(bf16[512,1024]{1,0:T(8,128)(2,1)} %param.11) | copy-start | bytes 3145732
  158.4 4.9 %copy-start.31 = (bf16[1024,3,256]{2,0,1:T(8,128)(2,1)S(1)}, bf16[1024,3,256]{2,0,1:T(8,128)(2,1)}, u32[]{:S(2)}) copy-start(bf16[1024,3,256]{2,0,1:T(8,128)(2,1)} %param.14) | copy-start | bytes 4718596
  163.3 1.2 copy-start.2
  163.3 1.3 copy-start.4
  163.3 1.3 copy-start.6
  163.3 1.5 copy-start.7
  163.3 1.5 copy-start.12
  209.1 1.3 copy-start.8
  (10 other events, 7.8 us)

commit v5 on v4

--- a/solution.py
+++ b/solution.py
@@ -15,137 +15,6 @@
     weighted = grad_normed * gain
     inner = jnp.mean(weighted * values, axis=-1, keepdims=True)
     return extra + (scale * weighted - values * (scale * scale * scale) * inner)
-
-
-def ring_kernel(kinds, *refs):
-    jobs = len(kinds)
-    at = 0
-    ins = []
-    for kind in kinds:
-        n = 4 if kind == "norm" else 2
-        ins.append(refs[at : at + n])
-        at += n
-    outs = refs[at : at + jobs]
-    at += jobs
-    scratch = [refs[at + 4 * j : at + 4 * j + 4] for j in range(jobs)]
-    s_sem, r_sem = refs[at + 4 * jobs : at + 4 * jobs + 2]
-    T = outs[0].shape[0]
-    C = T // HEADS
-    H = C // 2
-
-    me = lax.axis_index("head")
-    R = lax.rem(me + 1, HEADS)
-    L = lax.rem(me + HEADS - 1, HEADS)
-    O = lax.rem(me + 2, HEADS)
-    barrier = pltpu.get_barrier_semaphore()
-    for other in (R, L):
-        pl.semaphore_signal(barrier, inc=1, device_id={"head": other}, device_id_type=MESH)
-    pl.semaphore_wait(barrier, 2)
-
-    def rows(k, half):
-        return pl.ds(pl.multiple_of(k * C + half * H, H), H)
-
-    def send(src, dst, job, i, dev):
-        copy = pltpu.make_async_remote_copy(
-            src_ref=src,
-            dst_ref=dst,
-            send_sem=s_sem.at[job, i],
-            recv_sem=r_sem.at[job, i],
-            device_id={"head": dev},
-            device_id_type=MESH,
-        )
-        copy.start()
-        return copy
-
-    def finish(job, half, total):
-        kind = kinds[job]
-        mine = pl.ds(half * H, H)
-        if kind == "norm":
-            _, values, gain, extra = ins[job]
-            total = norm_back_rows(
-                total, values[mine, :].astype(jnp.float32), gain[...], extra[mine, :].astype(jnp.float32)
-            )
-        else:
-            total = total + ins[job][1][mine, :].astype(jnp.float32)
-        outs[job][rows(me, half), :] = total
-
-    every = []
-    live = []
-    for j in range(jobs):
-        p = ins[j][0]
-        t1, t2, fl, fr = scratch[j]
-        a0 = send(p.at[rows(O, 0)], t1.at[0], j, 0, R)
-        a1 = send(p.at[rows(O, 1)], t2.at[0], j, 1, L)
-        a2 = send(p.at[rows(R, 1)], fl.at[1], j, 2, R)
-        a3 = send(p.at[rows(L, 0)], fr.at[0], j, 3, L)
-        live.append((a0, a1, a2, a3))
-        every += [a0, a1, a2, a3]
-    second = []
-    for j in range(jobs):
-        p = ins[j][0]
-        t1, t2, fl, fr = scratch[j]
-        a0, a1, a2, a3 = live[j]
-        a0.wait_recv()
-        t1[1] = p[rows(R, 0), :] + t1[0]
-        a4 = send(t1.at[1], fl.at[0], j, 4, R)
-        a1.wait_recv()
-        t2[1] = p[rows(L, 1), :] + t2[0]
-        a5 = send(t2.at[1], fr.at[1], j, 5, L)
-        second.append((a2, a3, a4, a5))
-        every += [a4, a5]
-    shares = []
-    for j in range(jobs):
-        p, o = ins[j][0], outs[j]
-        t1, t2, fl, fr = scratch[j]
-        a2, a3, a4, a5 = second[j]
-        a3.wait_recv()
-        a4.wait_recv()
-        finish(j, 0, p[rows(me, 0), :] + fl[0] + fr[0])
-        b0 = send(o.at[rows(me, 0)], o.at[rows(me, 0)], j, 6, R)
-        c0 = send(o.at[rows(me, 0)], o.at[rows(me, 0)], j, 8, L)
-        a2.wait_recv()
-        a5.wait_recv()
-        finish(j, 1, p[rows(me, 1), :] + fl[1] + fr[1])
-        b1 = send(o.at[rows(me, 1)], o.at[rows(me, 1)], j, 7, R)
-        c1 = send(o.at[rows(me, 1)], o.at[rows(me, 1)], j, 9, L)
-        shares.append((b0, b1, c0, c1))
-        every += [b0, b1, c0, c1]
-    last = []
-    for j in range(jobs):
-        o = outs[j]
-        b0, b1, c0, c1 = shares[j]
-        b0.wait_recv()
-        d0 = send(o.at[rows(L, 0)], o.at[rows(L, 0)], j, 10, R)
-        c1.wait_recv()
-        d1 = send(o.at[rows(R, 1)], o.at[rows(R, 1)], j, 11, L)
-        last += [b1, c0, d0, d1]
-        every += [d0, d1]
-    for copy in last:
-        copy.wait_recv()
-    for copy in every:
-        copy.wait_send()
-
-
-def ring(jobs, cid):
-    kinds = tuple(job[0] for job in jobs)
-    arrays = [a for job in jobs for a in job[1:]]
-    T, D = jobs[0][1].shape
-    H = T // HEADS // 2
-    n = len(jobs)
-    outs = pl.pallas_call(
-        lambda *refs: ring_kernel(kinds, *refs),
-        out_shape=tuple(jax.ShapeDtypeStruct((T, D), jnp.float32) for _ in jobs),
-        in_specs=[pl.BlockSpec(memory_space=pltpu.VMEM)] * len(arrays),
-        out_specs=tuple(pl.BlockSpec(memory_space=pltpu.VMEM) for _ in jobs),
-        scratch_shapes=[pltpu.VMEM((2, H, D), jnp.float32)] * (4 * n)
-        + [pltpu.SemaphoreType.DMA((n, 12))] * 2,
-        compiler_params=pltpu.CompilerParams(
-            collective_id=cid, has_side_effects=True, vmem_limit_bytes=32 << 20
-        ),
-        cost_estimate=pl.CostEstimate(flops=1, bytes_accessed=1, transcendentals=0),
-        name=f"ring{cid}",
-    )(*arrays)
-    return outs
 
 
 class Comm:
@@ -217,8 +86,8 @@
     lax.fori_loop(0, n * q, body, 0)
 
 
-def head_sum(cm, p, o, t, f, s_sem, r_sem, finish, times, closing):
-    T = o.shape[0]
+def head_sum(cm, p, o, t, f, s_sem, r_sem, finish, times, closing, share=True):
+    T = p.shape[0]
     C = T // 4
     H = C // 2
     R, L, O = ahead(cm.me, 1), ahead(cm.me, 3), ahead(cm.me, 2)
@@ -251,7 +120,14 @@
     def _():
         c["a3"].wait_recv()
         c["a4"].wait_recv()
-        o[rows(me, 0), :] = finish(0, p[rows(me, 0), :] + f[0, 0] + f[1, 0])
+        first = finish(0, p[rows(me, 0), :] + f[0, 0] + f[1, 0])
+        if not share:
+            c["a2"].wait_recv()
+            c["a5"].wait_recv()
+            o[0:H, :] = first
+            o[H:C, :] = finish(1, p[rows(me, 1), :] + f[0, 1] + f[1, 1])
+            return
+        o[rows(me, 0), :] = first
         go("b0", o.at[rows(me, 0)], o.at[rows(me, 0)], 6, 1)
         go("c0", o.at[rows(me, 0)], o.at[rows(me, 0)], 8, 3)
         c["a2"].wait_recv()
@@ -259,6 +135,9 @@
         o[rows(me, 1), :] = finish(1, p[rows(me, 1), :] + f[0, 1] + f[1, 1])
         go("c1", o.at[rows(me, 1)], o.at[rows(me, 1)], 9, 3)
         go("b1", o.at[rows(me, 1)], o.at[rows(me, 1)], 7, 1)
+
+    if not share:
+        return
 
     @cm.when(times[3])
     def _():
@@ -402,11 +281,101 @@
     cm.greet([axis(n) for n in (1, 2, 3) for axis in (cm.at_x, cm.at_z, cm.at_y)] + [cm.twin()])
 
 
+def front_kernel(gated, ow, tokens, o_resid, o_full, o_own, GF, WF, ys, yr, ws, wr):
+    cm = Comm()
+    x, z, c, me = cm.x, cm.z, cm.core, cm.me
+    R, L, O = ahead(me, 1), ahead(me, 3), ahead(me, 2)
+    cm.greet([cm.at_x(1), cm.at_x(3), cm.at_z(1), cm.at_z(3), cm.at_y(1), cm.at_y(2), cm.at_y(3), cm.twin()])
+    T = gated.shape[0]
+    N = T // 2
+    piece = ((x * 4 + z) * 2 + c) * 32
+    h = {}
+
+    def weight(name, ref, i, dev):
+        h[name] = cm.send(ref, ref, ws.at[i], wr.at[i], dev)
+
+    def gate(name, ref, i, n):
+        h[name] = cm.send(ref, ref, ys.at[i], yr.at[i], cm.at_y(n))
+
+    low, high = pl.ds(0, 2), pl.ds(2, 2)
+    WF[x, z, c, me] = ow[pl.ds(pl.multiple_of(piece, 32), 32), :].astype(jnp.float32)
+    for n in (1, 2, 3):
+        weight(("y", n), WF.at[x, z, c, me], n - 1, cm.at_y(n))
+    GF[me] = gated[...].astype(jnp.float32)
+    first, second = pl.ds(0, N), pl.ds(N, N)
+    gate("r0", GF.at[me, first], 0, 1)
+    gate("l1", GF.at[me, second], 1, 3)
+    gate("r1", GF.at[me, second], 2, 1)
+    gate("l0", GF.at[me, first], 3, 3)
+    for n in (1, 2, 3):
+        h["y", n].wait_recv()
+    weight("ax1", WF.at[x, z, c, low], 3, cm.at_x(1))
+    weight("ax3", WF.at[x, z, c, low], 4, cm.at_x(3))
+    weight("bz1", WF.at[x, z, c, high], 5, cm.at_z(1))
+    weight("bz3", WF.at[x, z, c, high], 6, cm.at_z(3))
+    o_resid[...] = tokens[...].astype(jnp.float32) + lax.dot_general(
+        gated[...], ow[...], (((1,), (1,)), ((), ())), preferred_element_type=jnp.float32
+    )
+    xl, xr, zl, zr = ahead(x, 3), ahead(x, 1), ahead(z, 3), ahead(z, 1)
+    h["ax1"].wait_recv()
+    weight("ax1f", WF.at[xl, z, c, 0], 7, cm.at_x(1))
+    h["ax3"].wait_recv()
+    weight("ax3f", WF.at[xr, z, c, 1], 8, cm.at_x(3))
+    h["bz1"].wait_recv()
+    weight("bz1f", WF.at[x, zl, c, 2], 9, cm.at_z(1))
+    h["bz3"].wait_recv()
+    weight("bz3f", WF.at[x, zr, c, 3], 10, cm.at_z(3))
+    h["ax1f"].wait_recv()
+    h["ax3f"].wait_recv()
+    weight("az1", WF.at[:, z, c, low], 11, cm.at_z(1))
+    weight("az3", WF.at[:, z, c, low], 12, cm.at_z(3))
+    h["bz1f"].wait_recv()
+    h["bz3f"].wait_recv()
+    weight("bx1", WF.at[x, :, c, high], 13, cm.at_x(1))
+    weight("bx3", WF.at[x, :, c, high], 14, cm.at_x(3))
+    h["r0"].wait_recv()
+    gate("r0f", GF.at[L, first], 4, 1)
+    h["l1"].wait_recv()
+    gate("l1f", GF.at[R, second], 5, 3)
+    h["az1"].wait_recv()
+    weight("az1f", WF.at[:, zl, c, 0], 15, cm.at_z(1))
+    h["az3"].wait_recv()
+    weight("az3f", WF.at[:, zr, c, 1], 16, cm.at_z(3))
+    h["bx1"].wait_recv()
+    weight("bx1f", WF.at[xl, :, c, 2], 17, cm.at_x(1))
+    h["bx3"].wait_recv()
+    weight("bx3f", WF.at[xr, :, c, 3], 18, cm.at_x(3))
+    for name in ("az1f", "az3f", "bx1f", "bx3f"):
+        h[name].wait_recv()
+    weight("twin", WF.at[:, :, c], 19, cm.twin())
+    h["r1"].wait_recv()
+    h["l0"].wait_recv()
+    h["twin"].wait_recv()
+    for k in range(4):
+        o_full[k] = WF[:, :, :, k].reshape(1024, 256).astype(jnp.bfloat16)
+    mine = pl.ds(pl.multiple_of(me * (T // 4), T // 4), T // 4)
+
+    def add(k):
+        low_gated = GF[k].astype(jnp.bfloat16)
+        o_resid[...] += lax.dot_general(
+            low_gated, o_full[k], (((1,), (1,)), ((), ())), preferred_element_type=jnp.float32
+        )
+
+    add(L)
+    add(R)
+    h["r0f"].wait_recv()
+    h["l1f"].wait_recv()
+    add(O)
+    for k in range(4):
+        o_own[:, 256 * k : 256 * (k + 1)] = GF[k, mine, :].astype(jnp.bfloat16)
+    cm.run()
+
+
 def middle_kernel(*refs):
-    (dn, own_resid, gain, own_cot, normed, d_gate, d_up, act, cot, down) = refs[:10]
-    (o_dres, o_res, o_gate, o_up, o_down) = refs[10:15]
-    (rp, full, yt, yf, G, RC) = refs[15:21]
-    bufs, (ys, yr), sems = refs[21:29], refs[29:31], refs[31:]
+    (dn, own_resid, gain, own_cot, normed, d_gate, d_up, act, cot, down, ow) = refs[:11]
+    (o_dres, o_dgated, o_res, o_gate, o_up, o_down) = refs[11:17]
+    (rp, full, turned, relay, yt, yf, G, RC) = refs[17:25]
+    bufs, (ys, yr), sems, (xs, xr) = refs[25:33], refs[33:35], refs[35:41], refs[41:]
     H = own_resid.shape[0] // 2
     cm = Comm()
     greet_all(cm)
@@ -427,8 +396,44 @@
             act[...], down[...], (((1,), (1,)), ((), ())), preferred_element_type=jnp.float32
         )
 
-    head_sum(cm, dn, o_dres, yt.at[0], yf.at[0], ys.at[0], yr.at[0], finish_dres, (0, 7, 28, 43), lambda: None)
-    head_sum(cm, rp, full, yt.at[1], yf.at[1], ys.at[1], yr.at[1], finish_result, (0.03, 18, 36, 56), rounded)
+    head_sum(cm, dn, o_dres, yt.at[0], yf.at[0], ys.at[0], yr.at[0], finish_dres, (0, 7, 20, 0), lambda: None, False)
+    head_sum(cm, rp, full, yt.at[1], yf.at[1], ys.at[1], yr.at[1], finish_result, (7.05, 19, 33, 44), rounded)
+
+    C = 2 * H
+    R, L = ahead(cm.me, 1), ahead(cm.me, 3)
+    c = {}
+
+    def rows(k, half=None):
+        if half is None:
+            return pl.ds(pl.multiple_of(k * C, C), C)
+        return pl.ds(pl.multiple_of(k * C + half * H, H), H)
+
+    def go(name, src, dst, i, n):
+        c[name] = cm.send(src, dst, xs.at[i], xr.at[i], cm.at_y(n))
+
+    @cm.when(20.1)
+    def _():
+        low = o_dres[...].astype(jnp.bfloat16)
+        for turn in (2, 1, 3):
+            turned[turn - 1] = jnp.dot(low, ow[ahead(cm.me, turn)], preferred_element_type=jnp.float32)
+            if turn == 2:
+                go("e0", turned.at[1, pl.ds(0, H)], relay.at[0], 0, 1)
+                go("e1", turned.at[1, pl.ds(H, H)], relay.at[1], 1, 3)
+            else:
+                go(("d", turn), turned.at[turn - 1], o_dgated.at[rows(cm.me)], 1 + turn, turn)
+        o_dgated[rows(cm.me), :] = jnp.dot(low, ow[cm.me], preferred_element_type=jnp.float32)
+
+    @cm.when(25)
+    def _():
+        c["e0"].wait_recv()
+        go("f0", relay.at[0], o_dgated.at[rows(L, 0)], 5, 1)
+        c["e1"].wait_recv()
+        go("f1", relay.at[1], o_dgated.at[rows(R, 1)], 6, 3)
+
+    @cm.when(901)
+    def _():
+        for name in (("d", 1), ("d", 3), "f0", "f1"):
+            c[name].wait_recv()
 
     w = act.shape[1]
     wa = 1792
@@ -466,7 +471,8 @@
     sm, sr = refs[29:31]
     ys, yr = refs[31:33]
     sems = refs[33:39]
-    ss, sr_sem = refs[39:]
+    ss, sr_sem = refs[39:41]
+    mine, theirs, hs, hr = refs[41:]
     H = toks.shape[0] // 2
     cm = Comm()
     greet_all(cm)
@@ -477,25 +483,36 @@
 
     head_sum(cm, dm, o_tok, yt, yf, ys, yr, finish_tokens, (0, 6.5, 17, 26), lambda: None)
 
-    wa = 512
+    wa = 768
+    heads = []
 
     def done_a():
         rows = G[cm.x, cm.z, cm.core, :, pl.ds(0, wa)]
-        o_in[0] = rows[:, :256]
-        o_in[1] = rows[:, 256:]
+        for k in range(3):
+            o_in[k] = rows[:, 256 * k : 256 * (k + 1)]
 
     def done_b():
-        rows = G[cm.x, cm.z, cm.core, :, pl.ds(wa, 512)]
-        o_in[2] = rows[:, :256]
-        o_out[...] = rows[:, 256:]
+        rows = G[cm.x, cm.z, cm.core, :, pl.ds(wa, 1024)]
+        for k in range(4):
+            mine[k] = rows[:, 256 * k : 256 * (k + 1)]
+        for n in (1, 2, 3):
+            heads.append(
+                cm.send(mine.at[ahead(cm.me, n)], theirs.at[n - 1], hs.at[n - 1], hr.at[n - 1], cm.at_y(n))
+            )
+
+    @cm.when(950)
+    def _():
+        for copy in heads:
+            copy.wait_recv()
+        o_out[...] = (mine[cm.me] + theirs[0]) + (theirs[1] + theirs[2])
 
     times = {
         "block": (0.1, 1, 2, 3),
-        "settle": (1.5, 2.5, 3.5, 4.5),
-        "A": (1.6, 2.6, 3.6, 6, 14),
-        "B": (4.6, 4.7, 4.8, 8.5, 16),
-        "A2": (14.1, 14.2, 14.3, 17.2, 20),
-        "B2": (16.1, 16.2, 16.3, 18.5, 21),
+        "settle": (2, 3, 4, 5),
+        "A": (2.1, 3.1, 4.1, 7.5, 19),
+        "B": (5.1, 5.2, 5.3, 12, 23),
+        "A2": (19.1, 19.2, 19.3, 21.5, 25.5),
+        "B2": (23.1, 23.2, 23.3, 25.7, 28),
     }
     products = [(normed, d_proj, 0), (d_low, [gated], 768)]
     grad_scatter(cm, products, G, RC, wa, bufs, sems, times, done_a, done_b)
@@ -549,23 +566,46 @@
 SCATTER_SEMS = [pltpu.SemaphoreType.DMA((n,)) for n in (4, 4, 12, 12, 12, 12)]
 
 
-def middle(dn, own_resid, gain, own_cot, normed, d_gate, d_up, act, cot, down):
+def front(gated, ow, tokens):
+    T, D = tokens.shape
+    f32, shape, dma = jnp.float32, jax.ShapeDtypeStruct, pltpu.SemaphoreType.DMA
+    outs = (
+        shape((T, D), f32),
+        shape((4, *ow.shape), jnp.bfloat16),
+        shape((T // 4, D), jnp.bfloat16),
+    )
+    scratch = [
+        pltpu.VMEM((4, *gated.shape), f32),
+        pltpu.VMEM((4, 4, 2, 4, 32, ow.shape[1]), f32),
+        dma((6,)),
+        dma((6,)),
+        dma((20,)),
+        dma((20,)),
+    ]
+    return call(front_kernel, "front", 3, (gated, ow, tokens), outs, scratch, 24)
+
+
+def middle(dn, own_resid, gain, own_cot, normed, d_gate, d_up, act, cot, down, ow):
     T, D = dn.shape
     H = T // 8
     f32, shape, dma = jnp.float32, jax.ShapeDtypeStruct, pltpu.SemaphoreType.DMA
     w = act.shape[1]
-    outs = (shape((T, D), f32), shape((T, D), jnp.bfloat16)) + (shape((32, w), f32),) * 3
+    outs = (shape((T // 4, D), f32), shape((T, 256), f32), shape((T, D), jnp.bfloat16)) + (shape((32, w), f32),) * 3
     scratch = [
         pltpu.VMEM((T, D), f32),
         pltpu.VMEM((T, D), f32),
+        pltpu.VMEM((3, 2 * H, 256), f32),
+        pltpu.VMEM((2, H, 256), f32),
         pltpu.VMEM((2, 2, H, D), f32),
         pltpu.VMEM((2, 2, 2, H, D), f32),
         *scatter_scratch(3 * w, 1792),
         dma((2, 12)),
         dma((2, 12)),
         *SCATTER_SEMS,
+        dma((7,)),
+        dma((7,)),
     ]
-    args = (dn, own_resid, gain, own_cot, normed, d_gate, d_up, act, cot, down)
+    args = (dn, own_resid, gain, own_cot, normed, d_gate, d_up, act, cot, down, ow)
     return call(middle_kernel, "middle", 5, args, outs, scratch, 56)
 
 
@@ -584,7 +624,7 @@
     scratch = [
         pltpu.VMEM((2, H, D), f32),
         pltpu.VMEM((2, 2, H, D), f32),
-        *scatter_scratch(1024, 512),
+        *scatter_scratch(1792, 768),
         pltpu.VMEM((3, 24, 128), f32),
         pltpu.VMEM((4, 4, 24, 128), f32),
         dma((12,)),
@@ -592,6 +632,10 @@
         *SCATTER_SEMS,
         dma((10,)),
         dma((10,)),
+        pltpu.VMEM((4, 32, 256), f32),
+        pltpu.VMEM((3, 32, 256), f32),
+        dma((3,)),
+        dma((3,)),
     ]
     args = (dm, toks, gain, d_res, normed, *d_proj, d_low, gated, small)
     return call(end_kernel, "end", 7, args, outs, scratch, 40)
@@ -678,7 +722,7 @@
     prev_two = extended[0:tok_rows]
     conv_out = kernel[0] * mixed + kernel[1] * near_own * prev_one + kernel[2] * far_own * prev_two
     gated = (chan_c * conv_out).astype(jnp.bfloat16)
-    (resid,) = ring([("add", right_product(gated, out_weight), own_rows(tokens))], 1)
+    resid, out_full, gated_rows = front(gated, out_weight, tokens)
     ffn_scale = rms_scale(resid)
     ffn_normed = (resid * ffn_scale * ffn_gain).astype(jnp.bfloat16)
     gate = jnp.dot(ffn_normed, gate_weight, preferred_element_type=jnp.float32)
@@ -690,7 +734,7 @@
     d_up = (d_act * gate * sigma).astype(jnp.bfloat16)
     d_normed_part = right_product(d_gate, gate_weight) + right_product(d_up, up_weight)
     grad_ffn_gain = jnp.sum(d_normed_part * resid * ffn_scale, axis=0)
-    d_resid, result, gate_share, up_share, down_share = middle(
+    d_resid, d_gated, result, gate_share, up_share, down_share = middle(
         d_normed_part,
         own_rows(resid),
         ffn_gain[None],
@@ -701,9 +745,8 @@
         act,
         cotangent,
         down_weight,
-    )
-    d_resid_low = d_resid.astype(jnp.bfloat16)
-    d_gated = jnp.dot(d_resid_low, out_weight, preferred_element_type=jnp.float32)
+        out_full,
+    )
     d_chan_c = d_gated * conv_out
     d_conv = d_gated * chan_c
     tail_rows = from_behind(d_conv[:2], "seq", -1)
@@ -740,11 +783,11 @@
         d_mix_part,
         own_rows(tokens),
         mix_gain[None],
-        own_rows(d_resid),
+        d_resid,
         mix_normed,
         d_projected,
-        d_resid_low,
-        gated,
+        d_resid.astype(jnp.bfloat16),
+        gated_rows,
         small,
     )
     (

time: 218 us -> 206 us (0.945)
  Pallas kernels: 173 us -> 159 us
  other arithmetic: 10.1 us -> 12.4 us
    pallas_call x1 -> x0, Pallas kernels: 42.5 us -> none  [ring(): pl.pallas_call(lambda *refs: ring_kernel(kinds, *refs), out_shape=tuple((...]
    pallas_call x2 -> x3, Pallas kernels: 126 us -> 155 us  [call(): pl.pallas_call(kernel, out_shape=outs, in_specs=[VMEM_SPEC] * len(args),...]
    dynamic_slice x4 -> x3, local copies, waits for them, and re-layouts: 5.51 us -> 3.3 us  [own_rows(): return lax.dynamic_slice_in_dim(x, own_at, own, 0)]
    dot_general x3 -> x2, matrix products: 4.98 us -> 4.46 us  [right_product(): lax.dot_general(left, right, (((1,), (1,)), ((), ())), preferred_element_...]
  transfers between devices with their start and end apart: 2 -> 2, of which waited for: 1 -> 1; matrix products, arithmetic and copies ran while one was open for 3% -> 4% of each run, Pallas kernels for 0% -> 0%
where the time goes in v5:
time: 206 us; the launch traced here: 205 us
  Pallas kernels  159 us (77%)
  matrix products  16.2 us (8%)
  local copies, waits for them, and re-layouts  12.9 us (6%)
  other arithmetic  12.4 us (6%)
  starting transfers between devices  2.56 us (1%)
    pallas_call x3, Pallas kernels, call(): pl.pallas_call(kernel, out_shape=outs, in_specs=[VMEM_SPEC] * len(args),...  155 us
    unnamed x64, local copies, waits for them, and re-layouts  9.27 us
    dot_general x1, matrix products, on_device(): d_act = jnp.dot(cotangent, down_weight, preferred_element_type=jnp.float32)  5.03 us
    dot_general x2, matrix products, right_product(): lax.dot_general(left, right, (((1,), (1,)), ((), ())), preferred_element_...  4.46 us
  transfers between devices with their start and end apart: 2, of which 1 were waited for; matrix products, arithmetic and copies ran while one was open for 4% of the time, Pallas kernels for 0%

profile of v5, /device:TPU:0, one launch (start us, length us, event | category | flops | bytes accessed | tf_op | source)
XLA Modules:
  0.0 205.0 jit_solution(462345793239005897)
XLA Ops:
  0.7 1.7 fusion
  2.3 1.5 fusion.2.refs_4_
  3.9 1.0 fusion.5
  5.0 1.1 copy-done.18
  6.9 1.3 collective-permute-start
  8.5 5.0 %fusion.28 = f32[512,1152]{1,0:T(8,128)} fusion(bf16[512,1024]{1,0:T(8,128)(2,1)} %refs_8_.1, bf16[1024,1152]{1,0:T(8,128)(2,1)} %refs_9_.1), kind=kOutput, calls=%fused_computation.64 | convolution fusion | flops 1207959552 | bytes 5767168 | tf_op jit(solution)/shard_map/dot_general | solution.py:732
  13.6 1.7 constant_dynamic-slice_fusion.1.refs_3_
  16.2 1.9 multiply_convert_fusion.7
  18.1 34.8 %front.1 = (f32[512,1024]{1,0:T(8,128)S(1)}, bf16[4,1024,256]{2,1,0:T(8,128)(2,1)S(1)}, bf16[128,1024]{1,0:T(8,128)(2,1)S(1)}) custom-call(bf16[512,256]{1,0:T(8,128)(2,1)S(1)} %get-tuple-element.66.gated, bf16[1024,256]{1,0:T(8,128)(2,1)S(1)} %copy-done.9, bf16[512,1024]{1,0:T(8,128)(2,1)S(1)} %copy-done.1), custom_call_target="tpu_custom_call" | custom-call | flops 1 | bytes 1 | tf_op jit(solution)/shard_map/front/pallas_call | solution.py:535
  54.5 1.1 copy-done.28
  55.6 1.5 fusion.29
  57.7 3.2 %multiply_convert_fusion = (bf16[512,1152]{1,0:T(8,128)(2,1)}, bf16[512,1152]{1,0:T(8,128)(2,1)S(1)}, bf16[512,1152]{1,0:T(8,128)(2,1)S(1)}) fusion(f32[512,1152]{1,0:T(8,128)S(1)} %fusion.29, f32[512,1152]{1,0:T(8,128)S(1)} %copy-done.31, bf16[512,1024]{1,0:T(8,128)(2,1)S(1)} %multiply_convert_fusion.3.refs_4_, bf16[1024,1152]{1,0:T(8,128)(2,1)S(1)} %copy-done), kind=kOutput, calls=%fused_computation.3 | convolution fusion | flops 1217396736 | bytes 11665408 | tf_op jit(solution)/shard_map/dot_general | solution.py:729
  60.9 1.6 fusion.30
  62.5 2.9 %multiply_reduce_fusion = (f32[1024]{0:T(1024)S(1)}, f32[512,1024]{1,0:T(8,128)}) fusion(f32[512,1024]{1,0:T(8,128)S(1)} %get-tuple-element.35, f32[512]{0:T(512)S(1)} %add_rsqrt_fusion, f32[512,1024]{1,0:T(8,128)S(1)} %fusion.30, bf16[512,1152]{1,0:T(8,128)(2,1)S(1)} %get-tuple-element.70.refs_6_, bf16[1024,1152]{1,0:T(8,128)(2,1)S(1)} %copy-done), kind=kOutput, calls=%fused_computation.12 | convolution fusion | flops 1210055680 | bytes 9836544 | tf_op jit(solution)/shard_map/dot_general | solution.py:676
  65.4 72.5 %middle.1 = (f32[128,1024]{1,0:T(8,128)}, f32[512,256]{1,0:T(8,128)}, bf16[512,1024]{1,0:T(8,128)(2,1)}, f32[32,1152]{1,0:T(8,128)}, f32[32,1152]{1,0:T(8,128)}, /*index=5*/f32[32,1152]{1,0:T(8,128)}) custom-call(f32[512,1024]{1,0:T(8,128)} %get-tuple-element.82.refs_0_, f32[128,1024]{1,0:T(8,128)} %constant_dynamic-slice_fusion.2.refs_1_, ...), custom_call_target="tpu_custom_call" | custom-call | flops 1 | bytes 1 | tf_op jit(solution)/shard_map/middle/pallas_call | solution.py:535
  137.9 2.2 %multiply_reduce_fusion.3 = (f32[256]{0:T(256)S(1)}, f32[256]{0:T(256)S(1)}, f32[256]{0:T(256)S(1)}, f32[512,256]{1,0:T(8,128)S(1)}, bf16[512,256]{1,0:T(8,128)(2,1)}) fusion(f32[512]{0:T(512)S(1)} %get-tuple-element.73, f32[512,256]{1,0:T(8,128)S(1)} %copy-done.20, f32[2,256]{1,0:T(2,128)S(1)} %collective-permute-done, f32[512]{0:T(512)S(1)} %get-tuple-element.85, ...), kind=kLoop, calls=%fused_computation.40 | loop fusion | flops 1703168 | bytes 2892800 | tf_op jit(solution)/shard_map/reduce_sum | solution.py:762
  140.9 1.3 collective-permute-start.1
  142.2 1.2 convert_element_type.55.refs_8_
  143.9 2.0 multiply_convert_fusion.6
  145.9 1.1 multiply_convert_fusion.4.refs_7_
  147.1 1.0 fusion.4
  148.6 48.0 %end.1 = (f32[512,1024]{1,0:T(8,128)S(1)}, f32[3,32,256]{2,1,0:T(8,128)S(1)}, f32[32,256]{1,0:T(8,128)S(1)}, f32[8,128]{1,0:T(8,128)S(1)}, f32[8,128]{1,0:T(8,128)S(1)}, /*index=5*/f32[3,256]{1,0:T(4,128)S(1)}) custom-call(f32[512,1024]{1,0:T(8,128)S(1)} %get-tuple-element.84.refs_0_, bf16[128,1024]{1,0:T(8,128)(2,1)S(1)} %copy-done.7, ...), custom_call_target="tpu_custom_call" | custom-call | flops 1 | bytes 1 | tf_op jit(solution)/shard_map/end/pallas_call | solution.py:535
  196.6 1.3 copy-done.5
  200.9 3.9 %place.1 = (bf16[512,1024]{1,0:T(8,128)(2,1)}, f32[512,1024]{1,0:T(8,128)}, f32[8,128]{1,0:T(8,128)}, f32[3,32,256]{2,1,0:T(8,128)}, f32[3,256]{1,0:T(4,128)}, /...) custom-call(bf16[512,1024]{1,0:T(8,128)(2,1)} %get-tuple-element.37.re, ...), custom_call_target="tpu_custom_call" | custom-call | tf_op jit(solution)/shard_map/place/pallas_call | solution.py:655
  (84 shorter events, 8.8 us)
Async XLA Ops:
  0.6 56.6 %copy-start = (bf16[1024,1152]{1,0:T(8,128)(2,1)S(1)}, bf16[1024,1152]{1,0:T(8,128)(2,1)}, u32[]{:S(2)}) copy-start(bf16[1024,1152]{1,0:T(8,128)(2,1)} %param.19) | copy-start | bytes 7077892
  0.7 3.2 %copy-start.29 = (bf16[1024,3,256]{2,0,1:T(8,128)(2,1)S(1)}, bf16[1024,3,256]{2,0,1:T(8,128)(2,1)}, u32[]{:S(2)}) copy-start(bf16[1024,3,256]{2,0,1:T(8,128)(2,1)} %param.14) | copy-start | bytes 4718596
  3.9 4.3 %copy-start.25 = (s32[16384]{0:T(1024)S(1)}, s32[16384]{0:T(1024)}, u32[]{:S(2)}) copy-start(s32[16384]{0:T(1024)} %param.12) | copy-start | bytes 196612
  3.9 4.6 %copy-start.27 = (bf16[3,256]{1,0:T(4,128)(2,1)S(1)}, bf16[3,256]{1,0:T(4,128)(2,1)}, u32[]{:S(2)}) copy-start(bf16[3,256]{1,0:T(4,128)(2,1)} %param.15) | copy-start | bytes 4612
  6.9 9.2 %collective-permute-start = (f32[2,256]{1,0:T(2,128)S(1)}, f32[2,256]{1,0:T(2,128)S(1)}, u32[]{:S(2)}, u32[]{:S(2)}) collective-permute-start(f32[2,256]{1,0:T(2,128)S(1)} %slice.85), channel_id=1, source_target_pairs={{0,4},{4,8},{8,12},{12,16},{16,20},{20,24},{24,28},{28,32},{32,36}... | collective-permute-start | bytes 6152 | tf_op jit(solution)/shard_map/ppermute | solution.py:668
  8.5 6.8 %copy-start.1 = (bf16[512,1024]{1,0:T(8,128)(2,1)S(1)}, bf16[512,1024]{1,0:T(8,128)(2,1)}, u32[]{:S(2)}) copy-start(bf16[512,1024]{1,0:T(8,128)(2,1)} %tokens.1) | copy-start | bytes 3145732
  13.6 4.6 %copy-start.9 = (bf16[1024,256]{1,0:T(8,128)(2,1)S(1)}, bf16[1024,256]{1,0:T(8,128)(2,1)}, u32[]{:S(2)}) copy-start(bf16[1024,256]{1,0:T(8,128)(2,1)} %ow.1) | copy-start | bytes 1572868
  18.1 35.9 %copy-start.26 = (f32[1024]{0:T(1024)S(1)}, f32[1024]{0:T(1024)}, u32[]{:S(2)}) copy-start(f32[1024]{0:T(1024)} %param.17) | copy-start | bytes 12292
  52.9 1.5 copy-start.6
  52.9 1.6 copy-start.10
  53.2 2.5 %copy-start.28 = (bf16[1024,1152]{1,0:T(8,128)(2,1)S(1)}, bf16[1024,1152]{1,0:T(8,128)(2,1)}, u32[]{:S(2)}) copy-start(bf16[1024,1152]{1,0:T(8,128)(2,1)} %param.18) | copy-start | bytes 7077892
  55.6 1.5 copy-start.22
  55.6 2.0 copy-start.31
  60.9 1.6 copy-start.24
  60.9 1.6 copy-start.21
  65.4 72.5 %copy-start.20 = (f32[512,256]{1,0:T(8,128)S(1)}, f32[512,256]{1,0:T(8,128)}, u32[]{:S(2)}) copy-start(f32[512,256]{1,0:T(8,128)} %copy-done.19) | copy-start | bytes 1572868
  140.9 3.0 %collective-permute-start.1 = (f32[2,256]{1,0:T(2,128)S(1)}, f32[2,256]{1,0:T(2,128)S(1)}, u32[]{:S(2)}, u32[]{:S(2)}) collective-permute-start(f32[2,256]{1,0:T(2,128)S(1)} %slice.89), channel_id=1, source_target_pairs={{4,0},{8,4},{12,8},{16,12},{20,16},{24,20},{28,24},{32,28},{36,32}... | collective-permute-start | bytes 6152 | tf_op jit(solution)/shard_map/ppermute | solution.py:668
  142.2 4.8 %copy-start.8 = (bf16[512,256]{1,0:T(8,128)(2,1)S(1)}, bf16[512,256]{1,0:T(8,128)(2,1)}, u32[]{:S(2)}) copy-start(bf16[512,256]{1,0:T(8,128)(2,1)} %get-tuple-element.71.refs_6_) | copy-start | bytes 786436
  142.2 4.8 %copy-start.30 = (bf16[1024,3,256]{2,0,1:T(8,128)(2,1)S(1)}, bf16[1024,3,256]{2,0,1:T(8,128)(2,1)}, u32[]{:S(2)}) copy-start(bf16[1024,3,256]{2,0,1:T(8,128)(2,1)} %param.14) | copy-start | bytes 4718596
  147.1 1.3 copy-start.4
  147.1 1.4 copy-start.7
  147.1 1.5 copy-start.11
  147.1 1.5 copy-start.14
  196.6 1.3 copy-start.5
  (10 other events, 8.0 us)

commit v6 on v5

--- a/solution.py
+++ b/solution.py
@@ -7,14 +7,14 @@
 
 EPS = 1e-05
 MESH = pl.DeviceIdType.MESH
-HEADS = 4
 
 
 def norm_back_rows(grad_normed, values, gain, extra):
     scale = lax.rsqrt(jnp.mean(values * values, axis=-1, keepdims=True) + EPS)
     weighted = grad_normed * gain
     inner = jnp.mean(weighted * values, axis=-1, keepdims=True)
-    return extra + (scale * weighted - values * (scale * scale * scale) * inner)
+    grad_values = extra + (scale * weighted - values * (scale * scale * scale) * inner)
+    return grad_values, jnp.sum(grad_normed * values * scale, axis=0, keepdims=True)
 
 
 class Comm:
@@ -281,7 +281,9 @@
     cm.greet([axis(n) for n in (1, 2, 3) for axis in (cm.at_x, cm.at_z, cm.at_y)] + [cm.twin()])
 
 
-def front_kernel(gated, ow, tokens, o_resid, o_full, o_own, GF, WF, ys, yr, ws, wr):
+def front_kernel(
+    gated, ow, tokens, cot, down, gain, o_normed, o_full, o_own, o_dact, o_resid, o_cot, o_tok, resid, GF, WF, ys, yr, ws, wr
+):
     cm = Comm()
     x, z, c, me = cm.x, cm.z, cm.core, cm.me
     R, L, O = ahead(me, 1), ahead(me, 3), ahead(me, 2)
@@ -313,9 +315,12 @@
     weight("ax3", WF.at[x, z, c, low], 4, cm.at_x(3))
     weight("bz1", WF.at[x, z, c, high], 5, cm.at_z(1))
     weight("bz3", WF.at[x, z, c, high], 6, cm.at_z(3))
-    o_resid[...] = tokens[...].astype(jnp.float32) + lax.dot_general(
+    resid[...] = tokens[...].astype(jnp.float32) + lax.dot_general(
         gated[...], ow[...], (((1,), (1,)), ((), ())), preferred_element_type=jnp.float32
     )
+    mine = pl.ds(pl.multiple_of(me * (T // 4), T // 4), T // 4)
+    o_cot[...] = cot[mine, :]
+    o_tok[...] = tokens[mine, :]
     xl, xr, zl, zr = ahead(x, 3), ahead(x, 1), ahead(z, 3), ahead(z, 1)
     h["ax1"].wait_recv()
     weight("ax1f", WF.at[xl, z, c, 0], 7, cm.at_x(1))
@@ -333,6 +338,7 @@
     h["bz3f"].wait_recv()
     weight("bx1", WF.at[x, :, c, high], 13, cm.at_x(1))
     weight("bx3", WF.at[x, :, c, high], 14, cm.at_x(3))
+    o_dact[...] = jnp.dot(cot[...], down[...], preferred_element_type=jnp.float32)
     h["r0"].wait_recv()
     gate("r0f", GF.at[L, first], 4, 1)
     h["l1"].wait_recv()
@@ -353,11 +359,10 @@
     h["twin"].wait_recv()
     for k in range(4):
         o_full[k] = WF[:, :, :, k].reshape(1024, 256).astype(jnp.bfloat16)
-    mine = pl.ds(pl.multiple_of(me * (T // 4), T // 4), T // 4)
 
     def add(k):
         low_gated = GF[k].astype(jnp.bfloat16)
-        o_resid[...] += lax.dot_general(
+        resid[...] += lax.dot_general(
             low_gated, o_full[k], (((1,), (1,)), ((), ())), preferred_element_type=jnp.float32
         )
 
@@ -368,21 +373,35 @@
     add(O)
     for k in range(4):
         o_own[:, 256 * k : 256 * (k + 1)] = GF[k, mine, :].astype(jnp.bfloat16)
+    o_resid[...] = resid[mine, :]
+
+    def body(i, carry):
+        rows = pl.ds(pl.multiple_of(i * 32, 32), 32)
+        values = resid[rows, :]
+        scale = lax.rsqrt(jnp.mean(values * values, axis=-1, keepdims=True) + EPS)
+        o_normed[rows, :] = (values * scale * gain[...]).astype(jnp.bfloat16)
+        return carry
+
+    lax.fori_loop(0, T // 32, body, 0)
     cm.run()
 
 
 def middle_kernel(*refs):
     (dn, own_resid, gain, own_cot, normed, d_gate, d_up, act, cot, down, ow) = refs[:11]
-    (o_dres, o_dgated, o_res, o_gate, o_up, o_down) = refs[11:17]
-    (rp, full, turned, relay, yt, yf, G, RC) = refs[17:25]
-    bufs, (ys, yr), sems, (xs, xr) = refs[25:33], refs[33:35], refs[35:41], refs[41:]
+    (o_dres, o_dlow, o_gain, o_dgated, o_res, o_gate, o_up, o_down) = refs[11:19]
+    (rp, full, turned, relay, yt, yf, G, RC) = refs[19:27]
+    bufs, (ys, yr), sems, (xs, xr) = refs[27:35], refs[35:37], refs[37:43], refs[43:]
     H = own_resid.shape[0] // 2
     cm = Comm()
     greet_all(cm)
 
     def finish_dres(half, total):
         mine = pl.ds(half * H, H)
-        return norm_back_rows(total, own_resid[mine, :], gain[...], own_cot[mine, :].astype(jnp.float32))
+        rows, gains = norm_back_rows(
+            total, own_resid[mine, :], gain[...], own_cot[mine, :].astype(jnp.float32)
+        )
+        o_gain[...] = gains if half == 0 else o_gain[...] + gains
+        return rows
 
     def finish_result(half, total):
         return total + own_resid[pl.ds(half * H, H), :]
@@ -414,6 +433,7 @@
     @cm.when(20.1)
     def _():
         low = o_dres[...].astype(jnp.bfloat16)
+        o_dlow[...] = low
         for turn in (2, 1, 3):
             turned[turn - 1] = jnp.dot(low, ow[ahead(cm.me, turn)], preferred_element_type=jnp.float32)
             if turn == 2:
@@ -479,7 +499,7 @@
 
     def finish_tokens(half, total):
         mine = pl.ds(half * H, H)
-        return norm_back_rows(total, toks[mine, :].astype(jnp.float32), gain[...], d_res[mine, :])
+        return norm_back_rows(total, toks[mine, :].astype(jnp.float32), gain[...], d_res[mine, :])[0]
 
     head_sum(cm, dm, o_tok, yt, yf, ys, yr, finish_tokens, (0, 6.5, 17, 26), lambda: None)
 
@@ -566,15 +586,20 @@
 SCATTER_SEMS = [pltpu.SemaphoreType.DMA((n,)) for n in (4, 4, 12, 12, 12, 12)]
 
 
-def front(gated, ow, tokens):
+def front(gated, ow, tokens, cot, down, gain):
     T, D = tokens.shape
-    f32, shape, dma = jnp.float32, jax.ShapeDtypeStruct, pltpu.SemaphoreType.DMA
+    f32, bf16, shape, dma = jnp.float32, jnp.bfloat16, jax.ShapeDtypeStruct, pltpu.SemaphoreType.DMA
     outs = (
-        shape((T, D), f32),
-        shape((4, *ow.shape), jnp.bfloat16),
-        shape((T // 4, D), jnp.bfloat16),
+        shape((T, D), bf16),
+        shape((4, *ow.shape), bf16),
+        shape((T // 4, D), bf16),
+        shape((T, down.shape[1]), f32),
+        shape((T // 4, D), f32),
+        shape((T // 4, D), bf16),
+        shape((T // 4, D), bf16),
     )
     scratch = [
+        pltpu.VMEM((T, D), f32),
         pltpu.VMEM((4, *gated.shape), f32),
         pltpu.VMEM((4, 4, 2, 4, 32, ow.shape[1]), f32),
         dma((6,)),
@@ -582,7 +607,7 @@
         dma((20,)),
         dma((20,)),
     ]
-    return call(front_kernel, "front", 3, (gated, ow, tokens), outs, scratch, 24)
+    return call(front_kernel, "front", 3, (gated, ow, tokens, cot, down, gain), outs, scratch, 24)
 
 
 def middle(dn, own_resid, gain, own_cot, normed, d_gate, d_up, act, cot, down, ow):
@@ -590,7 +615,13 @@
     H = T // 8
     f32, shape, dma = jnp.float32, jax.ShapeDtypeStruct, pltpu.SemaphoreType.DMA
     w = act.shape[1]
-    outs = (shape((T // 4, D), f32), shape((T, 256), f32), shape((T, D), jnp.bfloat16)) + (shape((32, w), f32),) * 3
+    outs = (
+        shape((T // 4, D), f32),
+        shape((T // 4, D), jnp.bfloat16),
+        shape((1, D), f32),
+        shape((T, 256), f32),
+        shape((T, D), jnp.bfloat16),
+    ) + (shape((32, w), f32),) * 3
     scratch = [
         pltpu.VMEM((T, D), f32),
         pltpu.VMEM((T, D), f32),
@@ -606,7 +637,7 @@
         dma((7,)),
     ]
     args = (dn, own_resid, gain, own_cot, normed, d_gate, d_up, act, cot, down, ow)
-    return call(middle_kernel, "middle", 5, args, outs, scratch, 56)
+    return call(middle_kernel, "middle", 5, args, outs, scratch, 42)
 
 
 def end(dm, toks, gain, d_res, normed, d_proj, d_low, gated, small):
@@ -638,7 +669,7 @@
         dma((3,)),
     ]
     args = (dm, toks, gain, d_res, normed, *d_proj, d_low, gated, small)
-    return call(end_kernel, "end", 7, args, outs, scratch, 40)
+    return call(end_kernel, "end", 7, args, outs, scratch, 24)
 
 
 def place(*arrays):
@@ -658,6 +689,7 @@
         in_specs=[VMEM_SPEC] * n,
         out_specs=(anywhere,) * n,
         scratch_shapes=[pltpu.SemaphoreType.DMA((n,))],
+        compiler_params=pltpu.CompilerParams(vmem_limit_bytes=2 << 20),
         name="place",
     )(*arrays)
 
@@ -692,12 +724,6 @@
     cotangent,
 ):
     tok_rows = tokens.shape[0]
-    own = tok_rows // HEADS
-    own_at = lax.axis_index("head") * own
-
-    def own_rows(x):
-        return lax.dynamic_slice_in_dim(x, own_at, own, 0)
-
     first_row = lax.axis_index("seq") * tok_rows
     padded_ids = jnp.concatenate(
         [jnp.full((2,), -1, jnp.int32), segment_ids, jnp.full((2,), -2, jnp.int32)]
@@ -722,23 +748,21 @@
     prev_two = extended[0:tok_rows]
     conv_out = kernel[0] * mixed + kernel[1] * near_own * prev_one + kernel[2] * far_own * prev_two
     gated = (chan_c * conv_out).astype(jnp.bfloat16)
-    resid, out_full, gated_rows = front(gated, out_weight, tokens)
-    ffn_scale = rms_scale(resid)
-    ffn_normed = (resid * ffn_scale * ffn_gain).astype(jnp.bfloat16)
+    ffn_normed, out_full, gated_rows, d_act, own_resid, own_cot, own_tok = front(
+        gated, out_weight, tokens, cotangent, down_weight, ffn_gain[None]
+    )
     gate = jnp.dot(ffn_normed, gate_weight, preferred_element_type=jnp.float32)
     upper = jnp.dot(ffn_normed, up_weight, preferred_element_type=jnp.float32)
     sigma = jax.nn.sigmoid(gate)
     act = (gate * sigma * upper).astype(jnp.bfloat16)
-    d_act = jnp.dot(cotangent, down_weight, preferred_element_type=jnp.float32)
     d_gate = (d_act * upper * sigma * (1.0 + gate * (1.0 - sigma))).astype(jnp.bfloat16)
     d_up = (d_act * gate * sigma).astype(jnp.bfloat16)
     d_normed_part = right_product(d_gate, gate_weight) + right_product(d_up, up_weight)
-    grad_ffn_gain = jnp.sum(d_normed_part * resid * ffn_scale, axis=0)
-    d_resid, d_gated, result, gate_share, up_share, down_share = middle(
+    d_resid, d_resid_low, grad_ffn_gain, d_gated, result, gate_share, up_share, down_share = middle(
         d_normed_part,
-        own_rows(resid),
+        own_resid,
         ffn_gain[None],
-        own_rows(cotangent),
+        own_cot,
         ffn_normed,
         d_gate,
         d_up,
@@ -781,12 +805,12 @@
     )
     grad_tokens, in_share, out_share, mix_total, ffn_total, conv_total = end(
         d_mix_part,
-        own_rows(tokens),
+        own_tok,
         mix_gain[None],
         d_resid,
         mix_normed,
         d_projected,
-        d_resid.astype(jnp.bfloat16),
+        d_resid_low,
         gated_rows,
         small,
     )

time: 206 us -> 191 us (0.927)
  matrix products: 16.2 us -> 8.93 us
  Pallas kernels: 159 us -> 155 us
    dot_general x1 -> x0, matrix products: 5.03 us -> none  [on_device(): d_act = jnp.dot(cotangent, down_weight, preferred_element_type=jnp.float32)]
    unnamed x64 -> x92, local copies, waits for them, and re-layouts: 9.27 us -> 5.23 us
    dynamic_slice x3 -> x0, local copies, waits for them, and re-layouts: 3.3 us -> none  [own_rows(): return lax.dynamic_slice_in_dim(x, own_at, own, 0)]
    pallas_call x3, Pallas kernels: 155 us -> 153 us  [call(): pl.pallas_call(kernel, out_shape=outs, in_specs=[VMEM_SPEC] * len(args),...]
  transfers between devices with their start and end apart: 2 -> 2, of which waited for: 1 -> 1; matrix products, arithmetic and copies ran while one was open for 4% -> 3% of each run, Pallas kernels for 0% -> 0%
where the time goes in v6:
time: 191 us; the launch traced here: 190 us
  Pallas kernels  155 us (81%)
  other arithmetic  11.2 us (6%)
  local copies, waits for them, and re-layouts  10.9 us (6%)
  matrix products  8.93 us (5%)
  starting transfers between devices  2.56 us (1%)
    pallas_call x3, Pallas kernels, call(): pl.pallas_call(kernel, out_shape=outs, in_specs=[VMEM_SPEC] * len(args),...  153 us
    unnamed x92, local copies, waits for them, and re-layouts  5.23 us
  transfers between devices with their start and end apart: 2, of which 1 were waited for; matrix products, arithmetic and copies ran while one was open for 3% of the time, Pallas kernels for 0%

profile of v6, /device:TPU:0, one launch (start us, length us, event | category | flops | bytes accessed | tf_op | source)
XLA Modules:
  0.0 190.3 jit_solution(14574355732286685686)
XLA Ops:
  0.7 1.7 fusion
  2.4 1.5 fusion.2.refs_4_
  3.9 1.0 fusion.5
  5.1 1.1 copy-done.28
  6.9 1.3 collective-permute-start
  9.2 0.8 concatenate.12
  11.6 1.9 multiply_convert_fusion.6
  13.5 1.7 copy-done.1
  15.2 36.2 %front.1 = (bf16[512,1024]{1,0:T(8,128)(2,1)S(1)}, bf16[4,1024,256]{2,1,0:T(8,128)(2,1)S(1)}, bf16[128,1024]{1,0:T(8,128)(2,1)S(1)}, f32[512,1152]{1,0:T(8,128)S...) custom-call(bf16[512,256]{1,0:T(8,128)(2,1)S(1)} %get-tuple-element.78.gated, ...), custom_call_target="tpu_custom_call" | custom-call | flops 1 | bytes 1 | tf_op jit(solution)/shard_map/front/pallas_call | solution.py:555
  51.4 1.5 fusion.28
  53.0 2.3 %multiply_convert_fusion = (bf16[512,1152]{1,0:T(8,128)(2,1)S(1)}, bf16[512,1152]{1,0:T(8,128)(2,1)S(1)}, bf16[512,1152]{1,0:T(8,128)(2,1)S(1)}) fusion(f32[512,1152]{1,0:T(8,128)S(1)} %fusion.28, f32[512,1152]{1,0:T(8,128)S(1)} %get-tuple-element.41, bf16[512,1024]{1,0:T(8,128)(2,1)S(1)} %get-tuple-element.42.refs_4_, bf16[1024,1152]{1,0:T(8,128)(2,1)S(1)} %copy-done), kind=kOutput, calls=%fused_computation.3 | convolution fusion | flops 1217396736 | bytes 11665408 | tf_op jit(solution)/shard_map/dot_general | solution.py:755
  55.3 1.5 fusion.29
  56.8 1.6 convolution_add_fusion.refs_0_
  58.4 68.4 %middle.1 = (f32[128,1024]{1,0:T(8,128)S(1)}, bf16[128,1024]{1,0:T(8,128)(2,1)S(1)}, f32[1,1024]{1,0:T(1,128)S(1)}, f32[512,256]{1,0:T(8,128)S(1)}, bf16[512,102...) custom-call(f32[512,1024]{1,0:T(8,128)S(1)} %convolution_add_fusion.refs_0_, ...), custom_call_target="tpu_custom_call" | custom-call | flops 1 | bytes 1 | tf_op jit(solution)/shard_map/middle/pallas_call | solution.py:555
  126.8 1.0 copy-done.7
  127.8 0.8 copy-done.11
  128.6 2.3 %multiply_reduce_fusion.1 = (f32[256]{0:T(256)S(1)}, f32[256]{0:T(256)S(1)}, f32[256]{0:T(256)S(1)}, f32[512,256]{1,0:T(8,128)S(1)}, bf16[512,256]{1,0:T(8,128)(2,1)}) fusion(f32[512]{0:T(512)S(1)} %get-tuple-element.85, f32[512,256]{1,0:T(8,128)S(1)} %copy-done.30, f32[2,256]{1,0:T(2,128)S(1)} %copy-done.40, f32[512]{0:T(512)S(1)} %get-tuple-element.95, ...), kind=kLoop, calls=%fused_computation.37 | loop fusion | flops 1703168 | bytes 2892800 | tf_op jit(solution)/shard_map/reduce_sum | solution.py:786
  131.5 1.3 collective-permute-start.1
  133.4 1.3 reshape.50
  134.9 1.9 %multiply_convert_fusion.5 = (bf16[512,256]{1,0:T(8,128)(2,1)S(1)}, f32[512,256]{1,0:T(8,128)S(1)}) fusion(f32[512,3,256]{2,0,1:T(8,128)} %copy-done.28, f32[2,256]{1,0:T(2,128)} %collective-permute-done.1, f32[512,256]{1,0:T(8,128)} %copy-done.31, f32[512]{0:T(512)} %get-tuple-element.96, f32[256]{0:T(256)} %bitcast.62, f32[512]{0:T(512)} %get-tuple-element.84, ...), kind=kLoop, calls=%fused_computation.41 | loop fusion | flops 1441792 | bytes 1844224 | tf_op jit(solution)/shard_map/convert_element_type | solution.py:790
  136.8 1.1 multiply_convert_fusion.3.refs_7_
  138.0 1.0 fusion.4
  139.6 48.6 %end.1 = (f32[512,1024]{1,0:T(8,128)S(1)}, f32[3,32,256]{2,1,0:T(8,128)S(1)}, f32[32,256]{1,0:T(8,128)S(1)}, f32[8,128]{1,0:T(8,128)S(1)}, f32[8,128]{1,0:T(8,128)S(1)}, /*index=5*/f32[3,256]{1,0:T(4,128)S(1)}) custom-call(f32[512,1024]{1,0:T(8,128)S(1)} %get-tuple-element.94.refs_0_, bf16[128,1024]{1,0:T(8,128)(2,1)S(1)} %copy-done.16, ...), custom_call_target="tpu_custom_call" | custom-call | flops 1 | bytes 1 | tf_op jit(solution)/shard_map/end/pallas_call | solution.py:555
  188.2 1.9 %place.1 = (bf16[512,1024]{1,0:T(8,128)(2,1)}, f32[512,1024]{1,0:T(8,128)}, f32[8,128]{1,0:T(8,128)}, f32[3,32,256]{2,1,0:T(8,128)}, f32[3,256]{1,0:T(4,128)}, /...) custom-call(bf16[512,1024]{1,0:T(8,128)(2,1)S(1)} %copy-done.8, ...), custom_call_target="tpu_custom_call" | custom-call | tf_op jit(solution)/shard_map/place/pallas_call | solution.py:686
  (104 shorter events, 5.4 us)
Async XLA Ops:
  0.6 52.3 %copy-start = (bf16[1024,1152]{1,0:T(8,128)(2,1)S(1)}, bf16[1024,1152]{1,0:T(8,128)(2,1)}, u32[]{:S(2)}) copy-start(bf16[1024,1152]{1,0:T(8,128)(2,1)} %param.19) | copy-start | bytes 7077892
  0.7 3.2 %copy-start.44 = (bf16[1024,3,256]{2,0,1:T(8,128)(2,1)S(1)}, bf16[1024,3,256]{2,0,1:T(8,128)(2,1)}, u32[]{:S(2)}) copy-start(bf16[1024,3,256]{2,0,1:T(8,128)(2,1)} %param.14) | copy-start | bytes 4718596
  3.9 5.3 %copy-start.32 = (s32[16384]{0:T(1024)S(1)}, s32[16384]{0:T(1024)}, u32[]{:S(2)}) copy-start(s32[16384]{0:T(1024)} %param.12) | copy-start | bytes 196612
  3.9 6.9 %copy-start.41 = (bf16[3,256]{1,0:T(4,128)(2,1)S(1)}, bf16[3,256]{1,0:T(4,128)(2,1)}, u32[]{:S(2)}) copy-start(bf16[3,256]{1,0:T(4,128)(2,1)} %param.15) | copy-start | bytes 4612
  5.0 8.5 %copy-start.2 = (bf16[512,1024]{1,0:T(8,128)(2,1)S(1)}, bf16[512,1024]{1,0:T(8,128)(2,1)}, u32[]{:S(2)}) copy-start(bf16[512,1024]{1,0:T(8,128)(2,1)} %tokens.1) | copy-start | bytes 3145732
  5.0 8.5 %copy-start.24 = (f32[1024]{0:T(1024)S(1)}, f32[1024]{0:T(1024)}, u32[]{:S(2)}) copy-start(f32[1024]{0:T(1024)} %param.17) | copy-start | bytes 12292
  6.9 4.6 %collective-permute-start = (f32[2,256]{1,0:T(2,128)}, f32[2,256]{1,0:T(2,128)S(1)}, u32[]{:S(2)}, u32[]{:S(2)}) collective-permute-start(f32[2,256]{1,0:T(2,128)} %slice.85), channel_id=1, source_target_pairs={{0,4},{4,8},{8,12},{12,16},{16,20},{20,24},{24,28},{28,32},{32,36}... | collective-permute-start | bytes 6152 | tf_op jit(solution)/shard_map/ppermute | solution.py:700
  10.0 3.5 %copy-start.5 = (bf16[512,1024]{1,0:T(8,128)(2,1)S(1)}, bf16[512,1024]{1,0:T(8,128)(2,1)}, u32[]{:S(2)}) copy-start(bf16[512,1024]{1,0:T(8,128)(2,1)} %refs_8_.1) | copy-start | bytes 3145732
  10.0 3.5 %copy-start.10 = (bf16[1024,256]{1,0:T(8,128)(2,1)S(1)}, bf16[1024,256]{1,0:T(8,128)(2,1)}, u32[]{:S(2)}) copy-start(bf16[1024,256]{1,0:T(8,128)(2,1)} %ow.1) | copy-start | bytes 1572868
  10.9 2.6 %copy-start.35 = (f32[1,256]{1,0:T(1,128)}, f32[1,256]{1,0:T(1,128)S(1)}, u32[]{:S(2)}) copy-start(f32[1,256]{1,0:T(1,128)S(1)} %get-tuple-element.91) | copy-start | bytes 3076
  10.9 2.6 %copy-start.36 = (f32[1,256]{1,0:T(1,128)}, f32[1,256]{1,0:T(1,128)S(1)}, u32[]{:S(2)}) copy-start(f32[1,256]{1,0:T(1,128)S(1)} %get-tuple-element.92) | copy-start | bytes 3076
  11.5 39.8 %copy-start.39 = (f32[2,256]{1,0:T(2,128)}, f32[2,256]{1,0:T(2,128)S(1)}, u32[]{:S(2)}) copy-start(f32[2,256]{1,0:T(2,128)S(1)} %collective-permute-done) | copy-start | bytes 6148
  15.2 36.2 %copy-start.43 = (bf16[1024,1152]{1,0:T(8,128)(2,1)S(1)}, bf16[1024,1152]{1,0:T(8,128)(2,1)}, u32[]{:S(2)}) copy-start(bf16[1024,1152]{1,0:T(8,128)(2,1)} %param.18) | copy-start | bytes 7077892
  58.4 70.2 %copy-start.30 = (f32[512,256]{1,0:T(8,128)S(1)}, f32[512,256]{1,0:T(8,128)}, u32[]{:S(2)}) copy-start(f32[512,256]{1,0:T(8,128)} %copy-done.29) | copy-start | bytes 1572868
  58.4 70.2 %copy-start.40 = (f32[2,256]{1,0:T(2,128)S(1)}, f32[2,256]{1,0:T(2,128)}, u32[]{:S(2)}) copy-start(f32[2,256]{1,0:T(2,128)} %copy-done.39) | copy-start | bytes 6148
  128.6 2.9 %copy-start.21 = (f32[32,1152]{1,0:T(8,128)}, f32[32,1152]{1,0:T(8,128)S(1)}, u32[]{:S(2)}) copy-start(f32[32,1152]{1,0:T(8,128)S(1)} %get-tuple-element.61.refs_9_) | copy-start | bytes 442372
  128.6 4.2 %copy-start.26 = (f32[1,1024]{1,0:T(1,128)}, f32[1,1024]{1,0:T(1,128)S(1)}, u32[]{:S(2)}) copy-start(f32[1,1024]{1,0:T(1,128)S(1)} %get-tuple-element.52) | copy-start | bytes 12292
  131.5 3.4 %collective-permute-start.1 = (f32[2,256]{1,0:T(2,128)}, f32[2,256]{1,0:T(2,128)}, u32[]{:S(2)}, u32[]{:S(2)}) collective-permute-start(f32[2,256]{1,0:T(2,128)} %slice.89), channel_id=1, source_target_pairs={{4,0},{8,4},{12,8},{16,12},{20,16},{24,20},{28,24},{32,28},{36,32}... | collective-permute-start | bytes 6152 | tf_op jit(solution)/shard_map/ppermute | solution.py:700
  134.7 3.2 %copy-start.9 = (bf16[512,256]{1,0:T(8,128)(2,1)S(1)}, bf16[512,256]{1,0:T(8,128)(2,1)}, u32[]{:S(2)}) copy-start(bf16[512,256]{1,0:T(8,128)(2,1)} %get-tuple-element.83.refs_6_) | copy-start | bytes 786436
  134.7 3.2 %copy-start.38 = (f32[512]{0:T(512)S(1)}, f32[512]{0:T(512)}, u32[]{:S(2)}) copy-start(f32[512]{0:T(512)} %copy-done.37) | copy-start | bytes 6148
  134.7 3.2 %copy-start.45 = (bf16[1024,3,256]{2,0,1:T(8,128)(2,1)S(1)}, bf16[1024,3,256]{2,0,1:T(8,128)(2,1)}, u32[]{:S(2)}) copy-start(bf16[1024,3,256]{2,0,1:T(8,128)(2,1)} %param.14) | copy-start | bytes 4718596
  139.6 48.6 %copy-start.8 = (bf16[512,1024]{1,0:T(8,128)(2,1)S(1)}, bf16[512,1024]{1,0:T(8,128)(2,1)}, u32[]{:S(2)}) copy-start(bf16[512,1024]{1,0:T(8,128)(2,1)} %copy-done.7) | copy-start | bytes 3145732
  139.6 48.6 %copy-start.20 = (f32[32,1152]{1,0:T(8,128)S(1)}, f32[32,1152]{1,0:T(8,128)}, u32[]{:S(2)}) copy-start(f32[32,1152]{1,0:T(8,128)} %copy-done.19) | copy-start | bytes 442372
  139.6 48.6 %copy-start.22 = (f32[32,1152]{1,0:T(8,128)S(1)}, f32[32,1152]{1,0:T(8,128)}, u32[]{:S(2)}) copy-start(f32[32,1152]{1,0:T(8,128)} %copy-done.21) | copy-start | bytes 442372
  (24 other events, 36.4 us)

commit v7 on v6

--- a/solution.py
+++ b/solution.py
@@ -38,6 +38,9 @@
 
     def twin(self, n=1):
         return {"seq": (self.x * 4 + self.z) * 2 + (1 - self.core), "head": self.me}
+
+    def along(self, n):
+        return {"seq": lax.rem((self.x * 4 + self.z) * 2 + self.core + n, 32), "head": self.me}
 
     def greet(self, devices):
         barrier = pltpu.get_barrier_semaphore()
@@ -277,8 +280,8 @@
         cm.when(times[2 + a])(end)
 
 
-def greet_all(cm):
-    cm.greet([axis(n) for n in (1, 2, 3) for axis in (cm.at_x, cm.at_z, cm.at_y)] + [cm.twin()])
+def greet_all(cm, more):
+    cm.greet([axis(n) for n in (1, 2, 3) for axis in (cm.at_x, cm.at_z, cm.at_y)] + [cm.twin()] + more)
 
 
 def front_kernel(
@@ -387,13 +390,15 @@
 
 
 def middle_kernel(*refs):
-    (dn, own_resid, gain, own_cot, normed, d_gate, d_up, act, cot, down, ow) = refs[:11]
-    (o_dres, o_dlow, o_gain, o_dgated, o_res, o_gate, o_up, o_down) = refs[11:19]
-    (rp, full, turned, relay, yt, yf, G, RC) = refs[19:27]
-    bufs, (ys, yr), sems, (xs, xr) = refs[27:35], refs[35:37], refs[37:43], refs[43:]
+    (dn, own_resid, gain, own_cot, normed, d_gate, d_up, act, down, ow) = refs[:10]
+    (proj, mixed, conv_out, marks, taps, in_w) = refs[10:16]
+    (o_dres, o_dlow, o_gain, o_res, o_gate, o_up, o_dproj, o_dm, o_taps) = refs[16:25]
+    (rp, full, turned, relay, dgated, DC, yt, yf, G, RC) = refs[25:35]
+    bufs, (ys, yr), sems, (xs, xr), (hs, hr) = refs[35:43], refs[43:45], refs[45:51], refs[51:53], refs[53:]
     H = own_resid.shape[0] // 2
+    T = 8 * H
     cm = Comm()
-    greet_all(cm)
+    greet_all(cm, [cm.along(1), cm.along(31)])
 
     def finish_dres(half, total):
         mine = pl.ds(half * H, H)
@@ -415,8 +420,8 @@
             act[...], down[...], (((1,), (1,)), ((), ())), preferred_element_type=jnp.float32
         )
 
-    head_sum(cm, dn, o_dres, yt.at[0], yf.at[0], ys.at[0], yr.at[0], finish_dres, (0, 7, 20, 0), lambda: None, False)
-    head_sum(cm, rp, full, yt.at[1], yf.at[1], ys.at[1], yr.at[1], finish_result, (7.05, 19, 33, 44), rounded)
+    head_sum(cm, dn, o_dres, yt.at[0], yf.at[0], ys.at[0], yr.at[0], finish_dres, (0, 7, 18, 0), lambda: None, False)
+    head_sum(cm, rp, full, yt.at[1], yf.at[1], ys.at[1], yr.at[1], finish_result, (7.05, 25, 44, 56), rounded)
 
     C = 2 * H
     R, L = ahead(cm.me, 1), ahead(cm.me, 3)
@@ -430,7 +435,7 @@
     def go(name, src, dst, i, n):
         c[name] = cm.send(src, dst, xs.at[i], xr.at[i], cm.at_y(n))
 
-    @cm.when(20.1)
+    @cm.when(18.1)
     def _():
         low = o_dres[...].astype(jnp.bfloat16)
         o_dlow[...] = low
@@ -440,81 +445,130 @@
                 go("e0", turned.at[1, pl.ds(0, H)], relay.at[0], 0, 1)
                 go("e1", turned.at[1, pl.ds(H, H)], relay.at[1], 1, 3)
             else:
-                go(("d", turn), turned.at[turn - 1], o_dgated.at[rows(cm.me)], 1 + turn, turn)
-        o_dgated[rows(cm.me), :] = jnp.dot(low, ow[cm.me], preferred_element_type=jnp.float32)
-
-    @cm.when(25)
+                go(("d", turn), turned.at[turn - 1], dgated.at[rows(cm.me)], 1 + turn, turn)
+        dgated[rows(cm.me), :] = jnp.dot(low, ow[cm.me], preferred_element_type=jnp.float32)
+
+    @cm.when(32)
     def _():
         c["e0"].wait_recv()
-        go("f0", relay.at[0], o_dgated.at[rows(L, 0)], 5, 1)
+        go("f0", relay.at[0], dgated.at[rows(L, 0)], 5, 1)
         c["e1"].wait_recv()
-        go("f1", relay.at[1], o_dgated.at[rows(R, 1)], 6, 3)
-
-    @cm.when(901)
+        go("f1", relay.at[1], dgated.at[rows(R, 1)], 6, 3)
+
+    N = 64
+
+    @cm.when(38)
     def _():
         for name in (("d", 1), ("d", 3), "f0", "f1"):
             c[name].wait_recv()
+        for i in range(T // N):
+            at = pl.ds(i * N, N)
+            dg = dgated[at, :]
+            o_dproj[1, at, :] = (dg * conv_out[at, :]).astype(jnp.bfloat16)
+            DC[at, :] = dg * proj[1, at, :]
+        c["halo"] = cm.send(DC.at[pl.ds(0, 8)], DC.at[pl.ds(T, 8)], hs.at[0], hr.at[0], cm.along(31))
+
+    @cm.when(41)
+    def _():
+        c["halo"].wait_recv()
+        w0, w1, w2 = taps[0:1, :], taps[1:2, :], taps[2:3, :]
+        sums = [jnp.zeros((1, 256), jnp.float32)] * 3
+        for i in range(T // N):
+            at = pl.ds(i * N, N)
+            near, far = marks[at, 0:1], marks[at, 1:2]
+            near_next, far_next = marks[at, 2:3], marks[at, 3:4]
+            dc = DC[at, :]
+            d_mixed = w0 * dc + w1 * near_next * DC[pl.ds(i * N + 1, N), :] + w2 * far_next * DC[pl.ds(i * N + 2, N), :]
+            o_dproj[0, at, :] = (d_mixed * proj[2, at, :]).astype(jnp.bfloat16)
+            o_dproj[2, at, :] = (d_mixed * proj[0, at, :]).astype(jnp.bfloat16)
+            terms = (
+                dc * mixed[pl.ds(i * N + 8, N), :],
+                dc * near * mixed[pl.ds(i * N + 7, N), :],
+                dc * far * mixed[pl.ds(i * N + 6, N), :],
+            )
+            sums = [s + jnp.sum(t, axis=0, keepdims=True) for s, t in zip(sums, terms)]
+        for k in range(3):
+            o_taps[k : k + 1, :] = sums[k]
+
+    @cm.when(45)
+    def _():
+        right = jnp.concatenate([in_w[0], in_w[1], in_w[2]], axis=1)
+        for i in range(4):
+            at = pl.ds(i * C, C)
+            left = jnp.concatenate([o_dproj[0, at, :], o_dproj[1, at, :], o_dproj[2, at, :]], axis=1)
+            o_dm[at, :] = lax.dot_general(
+                left, right, (((1,), (1,)), ((), ())), preferred_element_type=jnp.float32
+            )
 
     w = act.shape[1]
-    wa = 1792
+
+    def done_a():
+        o_gate[...] = G[cm.x, cm.z, cm.core, :, pl.ds(0, w)]
+
+    def done_b():
+        o_up[...] = G[cm.x, cm.z, cm.core, :, pl.ds(w, w)]
+
+    times = {
+        "block": (4, 5.2, 7.2, 8.4),
+        "settle": (6.8, 8, 9.5, 11),
+        "A": (6.9, 8.1, 9.6, 15, 32),
+        "B": (11.1, 11.2, 11.3, 20, 36),
+        "A2": (32.1, 32.2, 32.3, 36.1, 41.1),
+        "B2": (36.2, 36.3, 36.4, 41.2, 46),
+    }
+    products = [(normed, [d_gate], 0), (normed, [d_up], w)]
+    grad_scatter(cm, products, G, RC, w, bufs, sems, times, done_a, done_b)
+    cm.run()
+
+
+def end_kernel(*refs):
+    (dm, toks, gain, d_res, normed, d_proj, d_low, gated, act, cot, ffn_gains, taps) = refs[:12]
+    (o_tok, o_in, o_out, o_down, o_mix, o_ffn, o_conv) = refs[12:19]
+    (yt, yf, G, RC) = refs[19:23]
+    bufs = refs[23:31]
+    small, sm, sr = refs[31:34]
+    ys, yr = refs[34:36]
+    sems = refs[36:42]
+    ss, sr_sem = refs[42:44]
+    mine, theirs, hs, hr = refs[44:]
+    H = toks.shape[0] // 2
+    cm = Comm()
+    greet_all(cm, [])
+
+    def finish_tokens(half, total):
+        at = pl.ds(half * H, H)
+        rows, gains = norm_back_rows(total, toks[at, :].astype(jnp.float32), gain[...], d_res[at, :])
+        for k in range(8):
+            part = gains[:, 128 * k : 128 * (k + 1)]
+            small[k : k + 1, :] = part if half == 0 else small[k : k + 1, :] + part
+        return rows
+
+    @cm.when(0.05)
+    def _():
+        small[16:24, :] = jnp.zeros((8, 128), jnp.float32)
+        for k in range(8):
+            small[8 + k : 9 + k, :] = ffn_gains[:, 128 * k : 128 * (k + 1)]
+        for k in range(3):
+            for h in range(2):
+                small[16 + 2 * k + h : 17 + 2 * k + h, :] = taps[k : k + 1, 128 * h : 128 * (h + 1)]
+
+    head_sum(cm, dm, o_tok, yt, yf, ys, yr, finish_tokens, (0, 7, 19, 26), lambda: None)
+
+    w = act.shape[1]
+    wa = w + 256
+    heads = []
 
     def done_a():
         rows = G[cm.x, cm.z, cm.core, :, pl.ds(0, wa)]
-        o_gate[...] = rows[:, :w]
-        o_up[:, pl.ds(0, wa - w)] = rows[:, w:]
+        o_down[...] = rows[:, :w]
+        o_in[0] = rows[:, w:]
 
     def done_b():
-        rows = G[cm.x, cm.z, cm.core, :, pl.ds(wa, 3 * w - wa)]
-        o_up[:, pl.ds(wa - w, 2 * w - wa)] = rows[:, : 2 * w - wa]
-        o_down[...] = rows[:, 2 * w - wa :]
-
-    times = {
-        "block": (4, 5.5, 7.5, 9),
-        "settle": (7.1, 8.5, 10, 12),
-        "A": (7.2, 8.6, 10.1, 18.5, 42),
-        "B": (12.1, 12.2, 12.3, 24, 45),
-        "A2": (42.1, 42.2, 42.3, 46, 52),
-        "B2": (45.1, 45.2, 45.3, 49, 55),
-    }
-    products = [(normed, [d_gate], 0), (normed, [d_up], w), (cot, [act], 2 * w)]
-    grad_scatter(cm, products, G, RC, wa, bufs, sems, times, done_a, done_b)
-    cm.run()
-
-
-def end_kernel(*refs):
-    (dm, toks, gain, d_res, normed) = refs[:5]
-    d_proj = refs[5:8]
-    (d_low, gated, small) = refs[8:11]
-    (o_tok, o_in, o_out, o_mix, o_ffn, o_conv) = refs[11:17]
-    (yt, yf, G, RC) = refs[17:21]
-    bufs = refs[21:29]
-    sm, sr = refs[29:31]
-    ys, yr = refs[31:33]
-    sems = refs[33:39]
-    ss, sr_sem = refs[39:41]
-    mine, theirs, hs, hr = refs[41:]
-    H = toks.shape[0] // 2
-    cm = Comm()
-    greet_all(cm)
-
-    def finish_tokens(half, total):
-        mine = pl.ds(half * H, H)
-        return norm_back_rows(total, toks[mine, :].astype(jnp.float32), gain[...], d_res[mine, :])[0]
-
-    head_sum(cm, dm, o_tok, yt, yf, ys, yr, finish_tokens, (0, 6.5, 17, 26), lambda: None)
-
-    wa = 768
-    heads = []
-
-    def done_a():
-        rows = G[cm.x, cm.z, cm.core, :, pl.ds(0, wa)]
-        for k in range(3):
-            o_in[k] = rows[:, 256 * k : 256 * (k + 1)]
-
-    def done_b():
-        rows = G[cm.x, cm.z, cm.core, :, pl.ds(wa, 1024)]
+        rows = G[cm.x, cm.z, cm.core, :, pl.ds(wa, 1536)]
+        o_in[1] = rows[:, :256]
+        o_in[2] = rows[:, 256:512]
         for k in range(4):
-            mine[k] = rows[:, 256 * k : 256 * (k + 1)]
+            mine[k] = rows[:, 512 + 256 * k : 768 + 256 * k]
         for n in (1, 2, 3):
             heads.append(
                 cm.send(mine.at[ahead(cm.me, n)], theirs.at[n - 1], hs.at[n - 1], hr.at[n - 1], cm.at_y(n))
@@ -527,14 +581,14 @@
         o_out[...] = (mine[cm.me] + theirs[0]) + (theirs[1] + theirs[2])
 
     times = {
-        "block": (0.1, 1, 2, 3),
-        "settle": (2, 3, 4, 5),
-        "A": (2.1, 3.1, 4.1, 7.5, 19),
-        "B": (5.1, 5.2, 5.3, 12, 23),
-        "A2": (19.1, 19.2, 19.3, 21.5, 25.5),
-        "B2": (23.1, 23.2, 23.3, 25.7, 28),
+        "block": (0.1, 1.5, 3, 4.5),
+        "settle": (2.9, 4.4, 5.9, 7.1),
+        "A": (3, 4.5, 6, 13.5, 32),
+        "B": (7.2, 7.3, 7.4, 17.5, 36.5),
+        "A2": (32.1, 32.2, 32.3, 36, 39.5),
+        "B2": (36.6, 36.7, 36.8, 40.5, 44),
     }
-    products = [(normed, d_proj, 0), (d_low, [gated], 768)]
+    products = [(cot, [act], 0), (normed, [d_proj.at[k] for k in range(3)], w), (d_low, [gated], w + 768)]
     grad_scatter(cm, products, G, RC, wa, bufs, sems, times, done_a, done_b)
 
     def small_done(gains, rest):
@@ -544,7 +598,7 @@
             for h in range(2):
                 o_conv[k : k + 1, pl.ds(128 * h, 128)] = rest[2 * k + h : 2 * k + h + 1]
 
-    small_sums(cm, small, sm, sr, ss, sr_sem, (0.05, 5, 9, 15, 22), small_done)
+    small_sums(cm, small, sm, sr, ss, sr_sem, (19.1, 23, 27, 33, 38), small_done)
     cm.run()
 
 
@@ -610,44 +664,55 @@
     return call(front_kernel, "front", 3, (gated, ow, tokens, cot, down, gain), outs, scratch, 24)
 
 
-def middle(dn, own_resid, gain, own_cot, normed, d_gate, d_up, act, cot, down, ow):
+def middle(*args):
+    dn, act, proj = args[0], args[7], args[10]
     T, D = dn.shape
     H = T // 8
-    f32, shape, dma = jnp.float32, jax.ShapeDtypeStruct, pltpu.SemaphoreType.DMA
+    f32, bf16, shape, dma = jnp.float32, jnp.bfloat16, jax.ShapeDtypeStruct, pltpu.SemaphoreType.DMA
     w = act.shape[1]
     outs = (
         shape((T // 4, D), f32),
-        shape((T // 4, D), jnp.bfloat16),
+        shape((T // 4, D), bf16),
         shape((1, D), f32),
-        shape((T, 256), f32),
-        shape((T, D), jnp.bfloat16),
-    ) + (shape((32, w), f32),) * 3
+        shape((T, D), bf16),
+        shape((32, w), f32),
+        shape((32, w), f32),
+        shape(proj.shape, bf16),
+        shape((T, D), f32),
+        shape((3, 256), f32),
+    )
     scratch = [
         pltpu.VMEM((T, D), f32),
         pltpu.VMEM((T, D), f32),
         pltpu.VMEM((3, 2 * H, 256), f32),
         pltpu.VMEM((2, H, 256), f32),
+        pltpu.VMEM((T, 256), f32),
+        pltpu.VMEM((T + 8, 256), f32),
         pltpu.VMEM((2, 2, H, D), f32),
         pltpu.VMEM((2, 2, 2, H, D), f32),
-        *scatter_scratch(3 * w, 1792),
+        *scatter_scratch(2 * w, w),
         dma((2, 12)),
         dma((2, 12)),
         *SCATTER_SEMS,
         dma((7,)),
         dma((7,)),
+        dma((1,)),
+        dma((1,)),
     ]
-    args = (dn, own_resid, gain, own_cot, normed, d_gate, d_up, act, cot, down, ow)
-    return call(middle_kernel, "middle", 5, args, outs, scratch, 42)
-
-
-def end(dm, toks, gain, d_res, normed, d_proj, d_low, gated, small):
+    return call(middle_kernel, "middle", 5, args, outs, scratch, 38)
+
+
+def end(*args):
+    dm, act = args[0], args[8]
     T, D = dm.shape
     H = T // 8
     f32, shape, dma = jnp.float32, jax.ShapeDtypeStruct, pltpu.SemaphoreType.DMA
+    w = act.shape[1]
     outs = (
         shape((T, D), f32),
         shape((3, 32, 256), f32),
         shape((32, 256), f32),
+        shape((32, w), f32),
         shape((8, 128), f32),
         shape((8, 128), f32),
         shape((3, 256), f32),
@@ -655,7 +720,8 @@
     scratch = [
         pltpu.VMEM((2, H, D), f32),
         pltpu.VMEM((2, 2, H, D), f32),
-        *scatter_scratch(1792, 768),
+        *scatter_scratch(w + 1792, w + 256),
+        pltpu.VMEM((24, 128), f32),
         pltpu.VMEM((3, 24, 128), f32),
         pltpu.VMEM((4, 4, 24, 128), f32),
         dma((12,)),
@@ -668,8 +734,7 @@
         dma((3,)),
         dma((3,)),
     ]
-    args = (dm, toks, gain, d_res, normed, *d_proj, d_low, gated, small)
-    return call(end_kernel, "end", 7, args, outs, scratch, 24)
+    return call(end_kernel, "end", 7, args, outs, scratch, 36)
 
 
 def place(*arrays):
@@ -758,7 +823,10 @@
     d_gate = (d_act * upper * sigma * (1.0 + gate * (1.0 - sigma))).astype(jnp.bfloat16)
     d_up = (d_act * gate * sigma).astype(jnp.bfloat16)
     d_normed_part = right_product(d_gate, gate_weight) + right_product(d_up, up_weight)
-    d_resid, d_resid_low, grad_ffn_gain, d_gated, result, gate_share, up_share, down_share = middle(
+    marks = jnp.stack(
+        [near_own[:, 0], far_own[:, 0], near_ext[1 : tok_rows + 1], far_ext[2 : tok_rows + 2]], axis=1
+    )
+    d_resid, d_resid_low, grad_ffn_gain, result, gate_share, up_share, d_projected, d_mix_part, grad_conv = middle(
         d_normed_part,
         own_resid,
         ffn_gain[None],
@@ -767,43 +835,16 @@
         d_gate,
         d_up,
         act,
-        cotangent,
         down_weight,
         out_full,
-    )
-    d_chan_c = d_gated * conv_out
-    d_conv = d_gated * chan_c
-    tail_rows = from_behind(d_conv[:2], "seq", -1)
-    later = jnp.concatenate([d_conv, tail_rows])
-    next_one = later[1 : tok_rows + 1]
-    next_two = later[2 : tok_rows + 2]
-    near_next = near_ext[1 : tok_rows + 1, None]
-    far_next = far_ext[2 : tok_rows + 2, None]
-    d_mixed = kernel[0] * d_conv + kernel[1] * near_next * next_one + kernel[2] * far_next * next_two
-    grad_conv = jnp.stack(
-        [
-            jnp.sum(d_conv * mixed, axis=0),
-            jnp.sum(d_conv * near_own * prev_one, axis=0),
-            jnp.sum(d_conv * far_own * prev_two, axis=0),
-        ]
-    )
-    d_projected = [p.astype(jnp.bfloat16) for p in (d_mixed * chan_x, d_chan_c, d_mixed * chan_b)]
-    d_mix_part = jnp.einsum(
-        "tkc,dkc->td",
-        jnp.stack(d_projected, axis=1),
-        in_weight,
-        preferred_element_type=jnp.float32,
-    )
-    grad_mix_gain = jnp.sum(d_mix_part * inputs * mix_scale, axis=0)
-    small = jnp.concatenate(
-        [
-            grad_mix_gain.reshape(8, 128),
-            grad_ffn_gain.reshape(8, 128),
-            grad_conv.reshape(6, 128),
-            jnp.zeros((2, 128), jnp.float32),
-        ]
-    )
-    grad_tokens, in_share, out_share, mix_total, ffn_total, conv_total = end(
+        projected.transpose(1, 0, 2),
+        jnp.concatenate([jnp.zeros((6, mixed.shape[1]), jnp.float32), extended]),
+        conv_out,
+        marks,
+        kernel,
+        in_weight.transpose(1, 0, 2),
+    )
+    grad_tokens, in_share, out_share, down_share, mix_total, ffn_total, conv_total = end(
         d_mix_part,
         own_tok,
         mix_gain[None],
@@ -812,7 +853,10 @@
         d_projected,
         d_resid_low,
         gated_rows,
-        small,
+        act,
+        cotangent,
+        grad_ffn_gain,
+        grad_conv,
     )
     (
         result,

time: 191 us -> 196 us (1.026)
  Pallas kernels: 155 us -> 172 us
  local copies, waits for them, and re-layouts: 10.9 us -> 5.81 us
  other arithmetic: 11.2 us -> 6.25 us
    pallas_call x3, Pallas kernels: 153 us -> 170 us  [call(): pl.pallas_call(kernel, out_shape=outs, in_specs=[VMEM_SPEC] * len(args),...]
    unnamed x92 -> x38, local copies, waits for them, and re-layouts: 5.23 us -> 1.83 us
    convert_element_type x2 -> x1, other arithmetic: 3 us -> 0.01 us  [on_device(): kernel = conv_weight.astype(jnp.float32)]
    reduce_sum x1 -> x0, other arithmetic: 2.25 us -> none  [on_device(): jnp.sum(d_conv * near_own * prev_one, axis=0)]
  transfers between devices with their start and end apart: 2 -> 1, of which waited for: 1 -> 0; matrix products, arithmetic and copies ran while one was open for 3% -> 2% of each run, Pallas kernels for 0% -> 0%
where the time goes in v7:
time: 196 us; the launch traced here: 195 us
  Pallas kernels  172 us (88%)
  matrix products  9.19 us (5%)
  other arithmetic  6.25 us (3%)
  local copies, waits for them, and re-layouts  5.81 us (3%)
    pallas_call x3, Pallas kernels, call(): pl.pallas_call(kernel, out_shape=outs, in_specs=[VMEM_SPEC] * len(args),...  170 us
    dot_general x2, matrix products, right_product(): lax.dot_general(left, right, (((1,), (1,)), ((), ())), preferred_element_...  4.42 us
  transfers between devices with their start and end apart: 1, of which 0 were waited for; matrix products, arithmetic and copies ran while one was open for 2% of the time, Pallas kernels for 0%

profile of v7, /device:TPU:0, one launch (start us, length us, event | category | flops | bytes accessed | tf_op | source)
XLA Modules:
  0.0 195.4 jit_solution(168368487634901679)
XLA Ops:
  0.7 1.7 fusion
  2.3 1.5 fusion.2.refs_4_
  3.9 1.0 fusion.3
  5.0 0.6 slice_bitcast_fusion.1
  5.6 1.4 collective-permute-start
  7.1 0.8 fusion.29
  7.9 0.6 fusion.17
  8.5 0.5 broadcast.23
  9.0 0.5 broadcast.24
  9.5 0.8 concatenate.10
  10.3 0.1 dynamic_slice.3
  10.4 0.1 fusion.12
  10.5 0.9 copy.25.refs_13_
  11.4 1.9 fusion.11
  13.4 1.7 copy-done.3
  15.1 36.3 %front.1 = (bf16[512,1024]{1,0:T(8,128)(2,1)S(1)}, bf16[4,1024,256]{2,1,0:T(8,128)(2,1)S(1)}, bf16[128,1024]{1,0:T(8,128)(2,1)S(1)}, f32[512,1152]{1,0:T(8,128)S...) custom-call(bf16[512,256]{1,0:T(8,128)(2,1)S(1)} %get-tuple-element.76.gated, ...), custom_call_target="tpu_custom_call" | custom-call | flops 1 | bytes 1 | tf_op jit(solution)/shard_map/front/pallas_call | solution.py:609
  51.4 1.5 fusion.18
  53.0 2.3 %multiply_convert_fusion = (bf16[512,1152]{1,0:T(8,128)(2,1)S(1)}, bf16[512,1152]{1,0:T(8,128)(2,1)S(1)}, bf16[512,1152]{1,0:T(8,128)(2,1)S(1)}) fusion(f32[512,1152]{1,0:T(8,128)S(1)} %fusion.18, f32[512,1152]{1,0:T(8,128)S(1)} %get-tuple-element.43, bf16[512,1024]{1,0:T(8,128)(2,1)S(1)} %get-tuple-element.44.refs_4_, bf16[1024,1152]{1,0:T(8,128)(2,1)S(1)} %copy-done), kind=kOutput, calls=%fused_computation.2 | convolution fusion | flops 1217396736 | bytes 11665408 | tf_op jit(solution)/shard_map/dot_general | solution.py:820
  55.2 1.5 fusion.19
  56.8 2.9 %convolution_add_fusion.refs_0_ = f32[512,1024]{1,0:T(8,128)} fusion(f32[512,1024]{1,0:T(8,128)S(1)} %fusion.19, bf16[512,1152]{1,0:T(8,128)(2,1)S(1)} %get-tuple-element.80.refs_6_, bf16[1024,1152]{1,0:T(8,128)(2,1)S(1)} %copy-done), kind=kOutput, calls=%fused_computation.9 | convolution fusion | flops 1208483840 | bytes 7733248 | tf_op jit(solution)/shard_map/dot_general | solution.py:773
  59.7 0.1 pad_maximum_fusion.refs_11_
  59.9 71.4 %middle.1 = (f32[128,1024]{1,0:T(8,128)S(1)}, bf16[128,1024]{1,0:T(8,128)(2,1)S(1)}, f32[1,1024]{1,0:T(1,128)S(1)}, bf16[512,1024]{1,0:T(8,128)(2,1)S(1)}, f32[3...) custom-call(f32[512,1024]{1,0:T(8,128)} %convolution_add_fusion.refs, ...), custom_call_target="tpu_custom_call" | custom-call | flops 1 | bytes 1 | tf_op jit(solution)/shard_map/middle/pallas_call | solution.py:609
  131.3 61.9 %end.1 = (f32[512,1024]{1,0:T(8,128)S(1)}, f32[3,32,256]{2,1,0:T(8,128)S(1)}, f32[32,256]{1,0:T(8,128)S(1)}, f32[32,1152]{1,0:T(8,128)S(1)}, f32[8,128]{1,0:T(8,...) custom-call(f32[512,1024]{1,0:T(8,128)S(1)} %get-tuple-element.49.refs_0_, ...), custom_call_target="tpu_custom_call" | custom-call | flops 1 | bytes 1 | tf_op jit(solution)/shard_map/end/pallas_call | solution.py:609
  193.2 1.9 place.1
  (45 shorter events, 0.4 us)
Async XLA Ops:
  0.6 52.3 %copy-start = (bf16[1024,1152]{1,0:T(8,128)(2,1)S(1)}, bf16[1024,1152]{1,0:T(8,128)(2,1)}, u32[]{:S(2)}) copy-start(bf16[1024,1152]{1,0:T(8,128)(2,1)} %param.19) | copy-start | bytes 7077892
  0.7 3.2 %copy-start.9 = (bf16[1024,3,256]{2,0,1:T(8,128)(2,1)S(1)}, bf16[1024,3,256]{2,0,1:T(8,128)(2,1)}, u32[]{:S(2)}) copy-start(bf16[1024,3,256]{2,0,1:T(8,128)(2,1)} %param.14) | copy-start | bytes 4718596
  3.9 1.0 copy-start.5
  4.9 2.1 %copy-start.1 = (f32[512,3,256]{2,0,1:T(8,128)}, f32[512,3,256]{2,0,1:T(8,128)S(1)}, u32[]{:S(2)}) copy-start(f32[512,3,256]{2,0,1:T(8,128)S(1)} %fusion.3) | copy-start | bytes 4718596
  4.9 3.0 %copy-start.17 = (bf16[3,256]{1,0:T(4,128)(2,1)S(1)}, bf16[3,256]{1,0:T(4,128)(2,1)}, u32[]{:S(2)}) copy-start(bf16[3,256]{1,0:T(4,128)(2,1)} %param.15) | copy-start | bytes 4612
  4.9 4.6 %copy-start.16 = (s32[16384]{0:T(1024)S(1)}, s32[16384]{0:T(1024)}, u32[]{:S(2)}) copy-start(s32[16384]{0:T(1024)} %param.12) | copy-start | bytes 196612
  5.0 8.3 %copy-start.4 = (bf16[512,1024]{1,0:T(8,128)(2,1)S(1)}, bf16[512,1024]{1,0:T(8,128)(2,1)}, u32[]{:S(2)}) copy-start(bf16[512,1024]{1,0:T(8,128)(2,1)} %tokens.1) | copy-start | bytes 3145732
  5.0 8.3 %copy-start.14 = (f32[1024]{0:T(1024)S(1)}, f32[1024]{0:T(1024)}, u32[]{:S(2)}) copy-start(f32[1024]{0:T(1024)} %param.17) | copy-start | bytes 12292
  5.6 5.8 %collective-permute-start = (f32[2,256]{1,0:T(2,128)}, f32[2,256]{1,0:T(2,128)S(1)}, u32[]{:S(2)}, u32[]{:S(2)}) collective-permute-start(f32[2,256]{1,0:T(2,128)} %slice_bitcast_fusion.1), channel_id=1, source_target_pairs={{0,4},{4,8},{8,12},{12,16},{16,20},{20,24},{24,28},{28,32},{32,36}... | collective-permute-start | bytes 6152 | tf_op jit(solution)/shard_map/ppermute | solution.py:765
  11.4 1.9 copy-start.7
  11.4 2.0 %copy-start.12 = (bf16[1024,256]{1,0:T(8,128)(2,1)S(1)}, bf16[1024,256]{1,0:T(8,128)(2,1)}, u32[]{:S(2)}) copy-start(bf16[1024,256]{1,0:T(8,128)(2,1)} %ow.1) | copy-start | bytes 1572868
  13.4 1.7 copy-start.3
  15.1 36.3 %copy-start.18 = (bf16[1024,1152]{1,0:T(8,128)(2,1)S(1)}, bf16[1024,1152]{1,0:T(8,128)(2,1)}, u32[]{:S(2)}) copy-start(bf16[1024,1152]{1,0:T(8,128)(2,1)} %param.18) | copy-start | bytes 7077892
  51.4 1.6 copy-start.8
  56.8 2.9 %copy-start.15 = (f32[512,256]{1,0:T(8,128)S(1)}, f32[512,256]{1,0:T(8,128)}, u32[]{:S(2)}) copy-start(f32[512,256]{1,0:T(8,128)} %fusion.29) | copy-start | bytes 1572868
  56.8 3.1 %copy-start.2 = (f32[512,3,256]{2,0,1:T(8,128)S(1)}, f32[512,3,256]{2,0,1:T(8,128)}, u32[]{:S(2)}) copy-start(f32[512,3,256]{2,0,1:T(8,128)} %copy-done.1) | copy-start | bytes 4718596
  56.8 3.1 %copy-start.10 = (bf16[1024,3,256]{2,0,1:T(8,128)(2,1)S(1)}, bf16[1024,3,256]{2,0,1:T(8,128)(2,1)}, u32[]{:S(2)}) copy-start(bf16[1024,3,256]{2,0,1:T(8,128)(2,1)} %param.14) | copy-start | bytes 4718596
  56.8 3.0 %copy-start.11 = (f32[512,4]{1,0:T(8,128)S(1)}, f32[512,4]{1,0:T(8,128)}, u32[]{:S(2)}) copy-start(f32[512,4]{1,0:T(8,128)} %copy.25.refs_13_) | copy-start | bytes 24580
  59.9 71.4 %copy-start.6 = (bf16[512,1024]{1,0:T(8,128)(2,1)S(1)}, bf16[512,1024]{1,0:T(8,128)(2,1)}, u32[]{:S(2)}) copy-start(bf16[512,1024]{1,0:T(8,128)(2,1)} %copy-done.5) | copy-start | bytes 3145732
  59.9 71.4 %copy-start.13 = (f32[1024]{0:T(1024)S(1)}, f32[1024]{0:T(1024)}, u32[]{:S(2)}) copy-start(f32[1024]{0:T(1024)} %param.13) | copy-start | bytes 12292

commit v8 on v7

--- a/solution.py
+++ b/solution.py
@@ -389,12 +389,15 @@
     cm.run()
 
 
+EARLY = 256
+
+
 def middle_kernel(*refs):
     (dn, own_resid, gain, own_cot, normed, d_gate, d_up, act, down, ow) = refs[:10]
-    (proj, mixed, conv_out, marks, taps, in_w) = refs[10:16]
-    (o_dres, o_dlow, o_gain, o_res, o_gate, o_up, o_dproj, o_dm, o_taps) = refs[16:25]
-    (rp, full, turned, relay, dgated, DC, yt, yf, G, RC) = refs[25:35]
-    bufs, (ys, yr), sems, (xs, xr), (hs, hr) = refs[35:43], refs[43:45], refs[45:51], refs[51:53], refs[53:]
+    (proj, mixed, conv_out, marks, taps, in_w, toks, cot) = refs[10:18]
+    (o_dres, o_dlow, o_gain, o_res, o_gate, o_up, o_down, o_dproj, o_dm, o_taps, o_mix) = refs[18:29]
+    (rp, full, turned, relay, dgated, DC, yt, yf, G, RC) = refs[29:39]
+    bufs, (ys, yr), sems, (xs, xr), (hs, hr) = refs[39:47], refs[47:49], refs[49:55], refs[55:57], refs[57:]
     H = own_resid.shape[0] // 2
     T = 8 * H
     cm = Comm()
@@ -500,13 +503,26 @@
                 left, right, (((1,), (1,)), ((), ())), preferred_element_type=jnp.float32
             )
 
+        def body(i, total):
+            at = pl.ds(pl.multiple_of(i * 32, 32), 32)
+            values = toks[at, :].astype(jnp.float32)
+            scale = lax.rsqrt(jnp.mean(values * values, axis=-1, keepdims=True) + EPS)
+            return total + jnp.sum(o_dm[at, :] * values * scale, axis=0, keepdims=True)
+
+        o_mix[...] = lax.fori_loop(0, T // 32, body, jnp.zeros(o_mix.shape, jnp.float32))
+
     w = act.shape[1]
+    e = EARLY // 2
 
     def done_a():
-        o_gate[...] = G[cm.x, cm.z, cm.core, :, pl.ds(0, w)]
+        rows = G[cm.x, cm.z, cm.core, :, pl.ds(0, w + e)]
+        o_gate[...] = rows[:, :w]
+        o_down[:, pl.ds(0, e)] = rows[:, w:]
 
     def done_b():
-        o_up[...] = G[cm.x, cm.z, cm.core, :, pl.ds(w, w)]
+        rows = G[cm.x, cm.z, cm.core, :, pl.ds(w + e, w + e)]
+        o_down[:, pl.ds(e, e)] = rows[:, :e]
+        o_up[...] = rows[:, e:]
 
     times = {
         "block": (4, 5.2, 7.2, 8.4),
@@ -516,59 +532,56 @@
         "A2": (32.1, 32.2, 32.3, 36.1, 41.1),
         "B2": (36.2, 36.3, 36.4, 41.2, 46),
     }
-    products = [(normed, [d_gate], 0), (normed, [d_up], w)]
-    grad_scatter(cm, products, G, RC, w, bufs, sems, times, done_a, done_b)
+    products = [(normed, [d_gate], 0), (cot, [act.at[:, pl.ds(0, EARLY)]], w), (normed, [d_up], w + EARLY)]
+    grad_scatter(cm, products, G, RC, w + e, bufs, sems, times, done_a, done_b)
     cm.run()
 
 
 def end_kernel(*refs):
-    (dm, toks, gain, d_res, normed, d_proj, d_low, gated, act, cot, ffn_gains, taps) = refs[:12]
-    (o_tok, o_in, o_out, o_down, o_mix, o_ffn, o_conv) = refs[12:19]
-    (yt, yf, G, RC) = refs[19:23]
-    bufs = refs[23:31]
-    small, sm, sr = refs[31:34]
-    ys, yr = refs[34:36]
-    sems = refs[36:42]
-    ss, sr_sem = refs[42:44]
-    mine, theirs, hs, hr = refs[44:]
+    (dm, toks, gain, d_res, normed, d_proj, d_low, gated, act, cot, mix_gains, ffn_gains, taps) = refs[:13]
+    (o_tok, o_in, o_out, o_down, o_mix, o_ffn, o_conv) = refs[13:20]
+    (yt, yf, G, RC) = refs[20:24]
+    bufs = refs[24:32]
+    small, sm, sr = refs[32:35]
+    ys, yr = refs[35:37]
+    sems = refs[37:43]
+    ss, sr_sem = refs[43:45]
+    mine, theirs, hs, hr = refs[45:]
     H = toks.shape[0] // 2
     cm = Comm()
     greet_all(cm, [])
 
     def finish_tokens(half, total):
         at = pl.ds(half * H, H)
-        rows, gains = norm_back_rows(total, toks[at, :].astype(jnp.float32), gain[...], d_res[at, :])
-        for k in range(8):
-            part = gains[:, 128 * k : 128 * (k + 1)]
-            small[k : k + 1, :] = part if half == 0 else small[k : k + 1, :] + part
-        return rows
-
-    @cm.when(0.05)
+        return norm_back_rows(total, toks[at, :].astype(jnp.float32), gain[...], d_res[at, :])[0]
+
+    @cm.when(-1)
     def _():
         small[16:24, :] = jnp.zeros((8, 128), jnp.float32)
         for k in range(8):
+            small[k : k + 1, :] = mix_gains[:, 128 * k : 128 * (k + 1)]
             small[8 + k : 9 + k, :] = ffn_gains[:, 128 * k : 128 * (k + 1)]
         for k in range(3):
             for h in range(2):
                 small[16 + 2 * k + h : 17 + 2 * k + h, :] = taps[k : k + 1, 128 * h : 128 * (h + 1)]
 
-    head_sum(cm, dm, o_tok, yt, yf, ys, yr, finish_tokens, (0, 7, 19, 26), lambda: None)
-
-    w = act.shape[1]
-    wa = w + 256
+    head_sum(cm, dm, o_tok, yt, yf, ys, yr, finish_tokens, (0, 7, 19.5, 27), lambda: None)
+
+    w = act.shape[1] - EARLY
+    wa = w + 512
     heads = []
 
     def done_a():
         rows = G[cm.x, cm.z, cm.core, :, pl.ds(0, wa)]
         o_down[...] = rows[:, :w]
-        o_in[0] = rows[:, w:]
+        o_in[0] = rows[:, w : w + 256]
+        o_in[1] = rows[:, w + 256 :]
 
     def done_b():
-        rows = G[cm.x, cm.z, cm.core, :, pl.ds(wa, 1536)]
-        o_in[1] = rows[:, :256]
-        o_in[2] = rows[:, 256:512]
+        rows = G[cm.x, cm.z, cm.core, :, pl.ds(wa, 1280)]
+        o_in[2] = rows[:, :256]
         for k in range(4):
-            mine[k] = rows[:, 512 + 256 * k : 768 + 256 * k]
+            mine[k] = rows[:, 256 + 256 * k : 512 + 256 * k]
         for n in (1, 2, 3):
             heads.append(
                 cm.send(mine.at[ahead(cm.me, n)], theirs.at[n - 1], hs.at[n - 1], hr.at[n - 1], cm.at_y(n))
@@ -582,13 +595,13 @@
 
     times = {
         "block": (0.1, 1.5, 3, 4.5),
-        "settle": (2.9, 4.4, 5.9, 7.1),
-        "A": (3, 4.5, 6, 13.5, 32),
-        "B": (7.2, 7.3, 7.4, 17.5, 36.5),
-        "A2": (32.1, 32.2, 32.3, 36, 39.5),
-        "B2": (36.6, 36.7, 36.8, 40.5, 44),
+        "settle": (2.9, 4.4, 5.9, 6.9),
+        "A": (3.02, 4.45, 5.95, 11, 25.5),
+        "B": (6.95, 6.96, 6.97, 15.5, 31.5),
+        "A2": (25.6, 25.7, 25.8, 28, 31),
+        "B2": (31.6, 31.7, 31.8, 34, 37),
     }
-    products = [(cot, [act], 0), (normed, [d_proj.at[k] for k in range(3)], w), (d_low, [gated], w + 768)]
+    products = [(cot, [act.at[:, pl.ds(EARLY, w)]], 0), (normed, [d_proj.at[k] for k in range(3)], w), (d_low, [gated], w + 768)]
     grad_scatter(cm, products, G, RC, wa, bufs, sems, times, done_a, done_b)
 
     def small_done(gains, rest):
@@ -598,7 +611,7 @@
             for h in range(2):
                 o_conv[k : k + 1, pl.ds(128 * h, 128)] = rest[2 * k + h : 2 * k + h + 1]
 
-    small_sums(cm, small, sm, sr, ss, sr_sem, (19.1, 23, 27, 33, 38), small_done)
+    small_sums(cm, small, sm, sr, ss, sr_sem, (-0.9, 0.05, 1.6, 3.05, 19), small_done)
     cm.run()
 
 
@@ -677,9 +690,11 @@
         shape((T, D), bf16),
         shape((32, w), f32),
         shape((32, w), f32),
+        shape((32, EARLY), f32),
         shape(proj.shape, bf16),
         shape((T, D), f32),
         shape((3, 256), f32),
+        shape((1, D), f32),
     )
     scratch = [
         pltpu.VMEM((T, D), f32),
@@ -690,7 +705,7 @@
         pltpu.VMEM((T + 8, 256), f32),
         pltpu.VMEM((2, 2, H, D), f32),
         pltpu.VMEM((2, 2, 2, H, D), f32),
-        *scatter_scratch(2 * w, w),
+        *scatter_scratch(2 * w + EARLY, w + EARLY // 2),
         dma((2, 12)),
         dma((2, 12)),
         *SCATTER_SEMS,
@@ -699,7 +714,7 @@
         dma((1,)),
         dma((1,)),
     ]
-    return call(middle_kernel, "middle", 5, args, outs, scratch, 38)
+    return call(middle_kernel, "middle", 5, args, outs, scratch, 36)
 
 
 def end(*args):
@@ -707,7 +722,7 @@
     T, D = dm.shape
     H = T // 8
     f32, shape, dma = jnp.float32, jax.ShapeDtypeStruct, pltpu.SemaphoreType.DMA
-    w = act.shape[1]
+    w = act.shape[1] - EARLY
     outs = (
         shape((T, D), f32),
         shape((3, 32, 256), f32),
@@ -720,7 +735,7 @@
     scratch = [
         pltpu.VMEM((2, H, D), f32),
         pltpu.VMEM((2, 2, H, D), f32),
-        *scatter_scratch(w + 1792, w + 256),
+        *scatter_scratch(w + 1792, w + 512),
         pltpu.VMEM((24, 128), f32),
         pltpu.VMEM((3, 24, 128), f32),
         pltpu.VMEM((4, 4, 24, 128), f32),
@@ -737,26 +752,36 @@
     return call(end_kernel, "end", 7, args, outs, scratch, 36)
 
 
-def place(*arrays):
+def place(down_early, down_late, *arrays):
     n = len(arrays)
+    early, late = down_early.shape[1], down_late.shape[1]
 
     def kernel(*refs):
-        copies = [pltpu.make_async_copy(refs[i], refs[n + i], refs[2 * n].at[i]) for i in range(n)]
+        first, second, ins = refs[0], refs[1], refs[2 : n + 2]
+        whole, outs, sems = refs[n + 2], refs[n + 3 : 2 * n + 3], refs[2 * n + 3]
+        pairs = [
+            (first, whole.at[:, pl.ds(0, early)]),
+            (second, whole.at[:, pl.ds(early, late)]),
+            *zip(ins, outs),
+        ]
+        copies = [pltpu.make_async_copy(a, b, sems.at[i]) for i, (a, b) in enumerate(pairs)]
         for copy in copies:
             copy.start()
         for copy in copies:
             copy.wait()
 
     anywhere = pl.BlockSpec(memory_space=pl.ANY)
+    shapes = [jax.ShapeDtypeStruct((down_early.shape[0], early + late), jnp.float32)]
+    shapes += [jax.ShapeDtypeStruct(a.shape, a.dtype) for a in arrays]
     return pl.pallas_call(
         kernel,
-        out_shape=tuple(jax.ShapeDtypeStruct(a.shape, a.dtype) for a in arrays),
-        in_specs=[VMEM_SPEC] * n,
-        out_specs=(anywhere,) * n,
-        scratch_shapes=[pltpu.SemaphoreType.DMA((n,))],
+        out_shape=tuple(shapes),
+        in_specs=[VMEM_SPEC] * (n + 2),
+        out_specs=(anywhere,) * (n + 1),
+        scratch_shapes=[pltpu.SemaphoreType.DMA((n + 2,))],
         compiler_params=pltpu.CompilerParams(vmem_limit_bytes=2 << 20),
         name="place",
-    )(*arrays)
+    )(down_early, down_late, *arrays)
 
 
 def from_behind(block, axis, distance):
@@ -826,7 +851,7 @@
     marks = jnp.stack(
         [near_own[:, 0], far_own[:, 0], near_ext[1 : tok_rows + 1], far_ext[2 : tok_rows + 2]], axis=1
     )
-    d_resid, d_resid_low, grad_ffn_gain, result, gate_share, up_share, d_projected, d_mix_part, grad_conv = middle(
+    d_resid, d_resid_low, grad_ffn_gain, result, gate_share, up_share, down_early, d_projected, d_mix_part, grad_conv, grad_mix_gain = middle(
         d_normed_part,
         own_resid,
         ffn_gain[None],
@@ -843,6 +868,8 @@
         marks,
         kernel,
         in_weight.transpose(1, 0, 2),
+        tokens,
+        cotangent,
     )
     grad_tokens, in_share, out_share, down_share, mix_total, ffn_total, conv_total = end(
         d_mix_part,
@@ -855,10 +882,12 @@
         gated_rows,
         act,
         cotangent,
+        grad_mix_gain,
         grad_ffn_gain,
         grad_conv,
     )
     (
+        down_share,
         result,
         grad_tokens,
         mix_total,
@@ -868,8 +897,9 @@
         ffn_total,
         gate_share,
         up_share,
+    ) = place(
+        down_early,
         down_share,
-    ) = place(
         result,
         grad_tokens,
         mix_total,
@@ -879,7 +909,6 @@
         ffn_total,
         gate_share,
         up_share,
-        down_share,
     )
     return (
         result,

time: 196 us -> 193 us (0.985)
  Pallas kernels: 172 us -> 169 us
    pallas_call x3, Pallas kernels: 170 us -> 167 us  [call(): pl.pallas_call(kernel, out_shape=outs, in_specs=[VMEM_SPEC] * len(args),...]
where the time goes in v8:
time: 193 us
  Pallas kernels  169 us (88%)
  matrix products  9.2 us (5%)
  other arithmetic  6.25 us (3%)
  local copies, waits for them, and re-layouts  5.81 us (3%)
    pallas_call x3, Pallas kernels, call(): pl.pallas_call(kernel, out_shape=outs, in_specs=[VMEM_SPEC] * len(args),...  167 us
    dot_general x2, matrix products, right_product(): lax.dot_general(left, right, (((1,), (1,)), ((), ())), preferred_element_...  4.43 us
  transfers between devices with their start and end apart: 1, of which 0 were waited for; matrix products, arithmetic and copies ran while one was open for 2% of the time, Pallas kernels for 0%

profile of v8, /device:TPU:0, one launch (start us, length us, event | category | flops | bytes accessed | tf_op | source)
XLA Modules:
  0.0 192.6 jit_solution(13984106750970340911)
XLA Ops:
  0.7 1.7 fusion
  2.3 1.5 fusion.2.refs_4_
  3.9 1.0 fusion.3
  5.0 0.6 slice_bitcast_fusion.1
  5.6 1.4 collective-permute-start
  7.1 0.8 fusion.29
  7.9 0.6 fusion.17
  8.5 0.5 broadcast.23
  9.0 0.5 broadcast.24
  9.5 0.8 concatenate.10
  10.3 0.1 dynamic_slice.3
  10.4 0.1 fusion.12
  10.5 0.9 copy.25.refs_13_
  11.4 1.9 fusion.11
  13.4 1.7 copy-done.4
  15.1 36.3 %front.1 = (bf16[512,1024]{1,0:T(8,128)(2,1)S(1)}, bf16[4,1024,256]{2,1,0:T(8,128)(2,1)S(1)}, bf16[128,1024]{1,0:T(8,128)(2,1)S(1)}, f32[512,1152]{1,0:T(8,128)S...) custom-call(bf16[512,256]{1,0:T(8,128)(2,1)S(1)} %get-tuple-element.80.gated, ...), custom_call_target="tpu_custom_call" | custom-call | flops 1 | bytes 1 | tf_op jit(solution)/shard_map/front/pallas_call | solution.py:622
  51.4 1.5 fusion.18
  53.0 2.3 %multiply_convert_fusion = (bf16[512,1152]{1,0:T(8,128)(2,1)S(1)}, bf16[512,1152]{1,0:T(8,128)(2,1)S(1)}, bf16[512,1152]{1,0:T(8,128)(2,1)S(1)}) fusion(f32[512,1152]{1,0:T(8,128)S(1)} %fusion.18, f32[512,1152]{1,0:T(8,128)S(1)} %get-tuple-element.45, bf16[512,1024]{1,0:T(8,128)(2,1)S(1)} %get-tuple-element.46.refs_4_, bf16[1024,1152]{1,0:T(8,128)(2,1)S(1)} %copy-done), kind=kOutput, calls=%fused_computation.2 | convolution fusion | flops 1217396736 | bytes 11665408 | tf_op jit(solution)/shard_map/dot_general | solution.py:845
  55.2 1.5 fusion.19
  56.8 2.9 %convolution_add_fusion.refs_0_ = f32[512,1024]{1,0:T(8,128)} fusion(f32[512,1024]{1,0:T(8,128)S(1)} %fusion.19, bf16[512,1152]{1,0:T(8,128)(2,1)S(1)} %get-tuple-element.84.refs_6_, bf16[1024,1152]{1,0:T(8,128)(2,1)S(1)} %copy-done), kind=kOutput, calls=%fused_computation.9 | convolution fusion | flops 1208483840 | bytes 7733248 | tf_op jit(solution)/shard_map/dot_general | solution.py:798
  59.7 0.1 pad_maximum_fusion.refs_11_
  59.9 73.0 %middle.1 = (f32[128,1024]{1,0:T(8,128)S(1)}, bf16[128,1024]{1,0:T(8,128)(2,1)S(1)}, f32[1,1024]{1,0:T(1,128)S(1)}, bf16[512,1024]{1,0:T(8,128)(2,1)S(1)}, f32[3...) custom-call(f32[512,1024]{1,0:T(8,128)} %convolution_add_fusion.refs, ...), custom_call_target="tpu_custom_call" | custom-call | flops 1 | bytes 1 | tf_op jit(solution)/shard_map/middle/pallas_call | solution.py:622
  132.9 57.6 %end.1 = (f32[512,1024]{1,0:T(8,128)S(1)}, f32[3,32,256]{2,1,0:T(8,128)S(1)}, f32[32,256]{1,0:T(8,128)S(1)}, f32[32,896]{1,0:T(8,128)S(1)}, f32[8,128]{1,0:T(8,1...) custom-call(f32[512,1024]{1,0:T(8,128)S(1)} %get-tuple-element.51.refs_0_, ...), custom_call_target="tpu_custom_call" | custom-call | flops 1 | bytes 1 | tf_op jit(solution)/shard_map/end/pallas_call | solution.py:622
  190.5 2.0 %place.1 = (f32[32,1152]{1,0:T(8,128)}, bf16[512,1024]{1,0:T(8,128)(2,1)}, f32[512,1024]{1,0:T(8,128)}, f32[8,128]{1,0:T(8,128)}, f32[3,32,256]{2,1,0:T(8,128)},...) custom-call(f32[32,256]{1,0:T(8,128)S(1)} %get-tuple-element.50.refs_0, ...), custom_call_target="tpu_custom_call" | custom-call | tf_op jit(solution)/shard_map/place/pallas_call | solution.py:776
  (45 shorter events, 0.4 us)
Async XLA Ops:
  0.6 52.3 %copy-start = (bf16[1024,1152]{1,0:T(8,128)(2,1)S(1)}, bf16[1024,1152]{1,0:T(8,128)(2,1)}, u32[]{:S(2)}) copy-start(bf16[1024,1152]{1,0:T(8,128)(2,1)} %param.19) | copy-start | bytes 7077892
  0.7 3.2 %copy-start.9 = (bf16[1024,3,256]{2,0,1:T(8,128)(2,1)S(1)}, bf16[1024,3,256]{2,0,1:T(8,128)(2,1)}, u32[]{:S(2)}) copy-start(bf16[1024,3,256]{2,0,1:T(8,128)(2,1)} %param.14) | copy-start | bytes 4718596
  3.9 1.0 copy-start.6
  4.9 2.1 %copy-start.2 = (f32[512,3,256]{2,0,1:T(8,128)}, f32[512,3,256]{2,0,1:T(8,128)S(1)}, u32[]{:S(2)}) copy-start(f32[512,3,256]{2,0,1:T(8,128)S(1)} %fusion.3) | copy-start | bytes 4718596
  4.9 3.0 %copy-start.17 = (bf16[3,256]{1,0:T(4,128)(2,1)S(1)}, bf16[3,256]{1,0:T(4,128)(2,1)}, u32[]{:S(2)}) copy-start(bf16[3,256]{1,0:T(4,128)(2,1)} %param.15) | copy-start | bytes 4612
  4.9 4.6 %copy-start.16 = (s32[16384]{0:T(1024)S(1)}, s32[16384]{0:T(1024)}, u32[]{:S(2)}) copy-start(s32[16384]{0:T(1024)} %param.12) | copy-start | bytes 196612
  5.0 8.3 %copy-start.1 = (bf16[512,1024]{1,0:T(8,128)(2,1)S(1)}, bf16[512,1024]{1,0:T(8,128)(2,1)}, u32[]{:S(2)}) copy-start(bf16[512,1024]{1,0:T(8,128)(2,1)} %refs_16_.1) | copy-start | bytes 3145732
  5.0 8.3 %copy-start.14 = (f32[1024]{0:T(1024)S(1)}, f32[1024]{0:T(1024)}, u32[]{:S(2)}) copy-start(f32[1024]{0:T(1024)} %param.17) | copy-start | bytes 12292
  5.6 5.8 %collective-permute-start = (f32[2,256]{1,0:T(2,128)}, f32[2,256]{1,0:T(2,128)S(1)}, u32[]{:S(2)}, u32[]{:S(2)}) collective-permute-start(f32[2,256]{1,0:T(2,128)} %slice_bitcast_fusion.1), channel_id=1, source_target_pairs={{0,4},{4,8},{8,12},{12,16},{16,20},{20,24},{24,28},{28,32},{32,36}... | collective-permute-start | bytes 6152 | tf_op jit(solution)/shard_map/ppermute | solution.py:790
  11.4 1.9 %copy-start.5 = (bf16[512,1024]{1,0:T(8,128)(2,1)S(1)}, bf16[512,1024]{1,0:T(8,128)(2,1)}, u32[]{:S(2)}) copy-start(bf16[512,1024]{1,0:T(8,128)(2,1)} %refs_9_.1) | copy-start | bytes 3145732
  11.4 2.0 %copy-start.12 = (bf16[1024,256]{1,0:T(8,128)(2,1)S(1)}, bf16[1024,256]{1,0:T(8,128)(2,1)}, u32[]{:S(2)}) copy-start(bf16[1024,256]{1,0:T(8,128)(2,1)} %ow.1) | copy-start | bytes 1572868
  13.4 1.7 copy-start.4
  15.1 36.3 %copy-start.18 = (bf16[1024,1152]{1,0:T(8,128)(2,1)S(1)}, bf16[1024,1152]{1,0:T(8,128)(2,1)}, u32[]{:S(2)}) copy-start(bf16[1024,1152]{1,0:T(8,128)(2,1)} %param.18) | copy-start | bytes 7077892
  51.4 1.6 copy-start.8
  56.8 2.9 %copy-start.15 = (f32[512,256]{1,0:T(8,128)S(1)}, f32[512,256]{1,0:T(8,128)}, u32[]{:S(2)}) copy-start(f32[512,256]{1,0:T(8,128)} %fusion.29) | copy-start | bytes 1572868
  56.8 3.1 %copy-start.3 = (f32[512,3,256]{2,0,1:T(8,128)S(1)}, f32[512,3,256]{2,0,1:T(8,128)}, u32[]{:S(2)}) copy-start(f32[512,3,256]{2,0,1:T(8,128)} %copy-done.2) | copy-start | bytes 4718596
  56.8 3.1 %copy-start.10 = (bf16[1024,3,256]{2,0,1:T(8,128)(2,1)S(1)}, bf16[1024,3,256]{2,0,1:T(8,128)(2,1)}, u32[]{:S(2)}) copy-start(bf16[1024,3,256]{2,0,1:T(8,128)(2,1)} %param.14) | copy-start | bytes 4718596
  56.8 3.1 %copy-start.11 = (f32[512,4]{1,0:T(8,128)S(1)}, f32[512,4]{1,0:T(8,128)}, u32[]{:S(2)}) copy-start(f32[512,4]{1,0:T(8,128)} %copy.25.refs_13_) | copy-start | bytes 24580
  59.9 73.0 %copy-start.7 = (bf16[512,1024]{1,0:T(8,128)(2,1)S(1)}, bf16[512,1024]{1,0:T(8,128)(2,1)}, u32[]{:S(2)}) copy-start(bf16[512,1024]{1,0:T(8,128)(2,1)} %copy-done.6) | copy-start | bytes 3145732
  59.9 73.0 %copy-start.13 = (f32[1024]{0:T(1024)S(1)}, f32[1024]{0:T(1024)}, u32[]{:S(2)}) copy-start(f32[1024]{0:T(1024)} %param.13) | copy-start | bytes 12292

commit v9 on v8

--- a/solution.py
+++ b/solution.py
@@ -132,12 +132,12 @@
             return
         o[rows(me, 0), :] = first
         go("b0", o.at[rows(me, 0)], o.at[rows(me, 0)], 6, 1)
-        go("c0", o.at[rows(me, 0)], o.at[rows(me, 0)], 8, 3)
         c["a2"].wait_recv()
         c["a5"].wait_recv()
         o[rows(me, 1), :] = finish(1, p[rows(me, 1), :] + f[0, 1] + f[1, 1])
         go("c1", o.at[rows(me, 1)], o.at[rows(me, 1)], 9, 3)
         go("b1", o.at[rows(me, 1)], o.at[rows(me, 1)], 7, 1)
+        go("c0", o.at[rows(me, 0)], o.at[rows(me, 0)], 8, 3)
 
     if not share:
         return
@@ -195,15 +195,18 @@
         done()
 
 
-def grad_scatter(cm, products, G, RC, wa, bufs, sems, times, done_a, done_b):
+def grad_scatter(cm, products_a, products_b, G, RC, wa, bufs, sems, times, done_a, done_b):
     tA, tB, fA, fB, t2A, t2B, f2A, f2B = bufs
     cs, cr, as_, ar, bs, br = sems
     W = G.shape[-1]
-    quarter = products[0][0].shape[1] // 4
+    quarter = products_a[0][0].shape[1] // 4
     got = {}
 
-    def block(turn):
+    cols_a, cols_b = pl.ds(0, wa), pl.ds(wa, W - wa)
+
+    def block(part, turn):
         k = ahead(cm.x, turn)
+        products, cols, i = (products_a, cols_a, turn) if part == "a" else (products_b, cols_b, 4 + turn)
         for left, rights, at in products:
             right = jnp.concatenate([r[...] for r in rights], axis=1)
             w = right.shape[1]
@@ -212,18 +215,21 @@
                 lhs, right, (((0,), (0,)), ((), ())), preferred_element_type=jnp.float32
             )
             G[k, :, :, :, pl.ds(at, w)] = value.reshape(4, 2, 32, w)
-        got[turn] = cm.send(G.at[k, :, 1 - cm.core], RC.at[k], cs.at[turn], cr.at[turn], cm.twin())
-
-    def settle(turn):
+        got[part, turn] = cm.send(
+            G.at[k, :, 1 - cm.core, :, cols], RC.at[k, :, :, cols], cs.at[i], cr.at[i], cm.twin()
+        )
+
+    def settle(part, turn):
         k = ahead(cm.x, turn)
-        got[turn].wait_recv()
-        add_up(G.at[k, :, cm.core], RC.at[k])
-
-    for i, turn in enumerate((2, 1, 3, 0)):
-        cm.when(times["block"][i])(lambda turn=turn: block(turn))
-        cm.when(times["settle"][i])(lambda turn=turn: settle(turn))
-
-    cols_a, cols_b = pl.ds(0, wa), pl.ds(wa, W - wa)
+        cols = cols_a if part == "a" else cols_b
+        got[part, turn].wait_recv()
+        add_up(G.at[k, :, cm.core, :, cols], RC.at[k, :, :, cols])
+
+    for part in "ba":
+        for i, turn in enumerate((2, 1, 3, 0)):
+            cm.when(times["block_" + part][i])(lambda part=part, turn=turn: block(part, turn))
+            cm.when(times["settle_" + part][i])(lambda part=part, turn=turn: settle(part, turn))
+
     core = cm.core
 
     def a1(turn, half):
@@ -417,14 +423,14 @@
     def rounded():
         o_res[...] = full[...].astype(jnp.bfloat16)
 
-    @cm.when(0.02)
+    @cm.when(6.1)
     def _():
         rp[...] = lax.dot_general(
             act[...], down[...], (((1,), (1,)), ((), ())), preferred_element_type=jnp.float32
         )
 
-    head_sum(cm, dn, o_dres, yt.at[0], yf.at[0], ys.at[0], yr.at[0], finish_dres, (0, 7, 18, 0), lambda: None, False)
-    head_sum(cm, rp, full, yt.at[1], yf.at[1], ys.at[1], yr.at[1], finish_result, (7.05, 25, 44, 56), rounded)
+    head_sum(cm, dn, o_dres, yt.at[0], yf.at[0], ys.at[0], yr.at[0], finish_dres, (0, 6, 18, 0), lambda: None, False)
+    head_sum(cm, rp, full, yt.at[1], yf.at[1], ys.at[1], yr.at[1], finish_result, (6.2, 25, 44, 56), rounded)
 
     C = 2 * H
     R, L = ahead(cm.me, 1), ahead(cm.me, 3)
@@ -525,15 +531,18 @@
         o_up[...] = rows[:, e:]
 
     times = {
-        "block": (4, 5.2, 7.2, 8.4),
-        "settle": (6.8, 8, 9.5, 11),
-        "A": (6.9, 8.1, 9.6, 15, 32),
-        "B": (11.1, 11.2, 11.3, 20, 36),
-        "A2": (32.1, 32.2, 32.3, 36.1, 41.1),
-        "B2": (36.2, 36.3, 36.4, 41.2, 46),
+        "block_b": (0.1, 0.2, 0.3, 0.4),
+        "block_a": (0.5, 1.3, 2.1, 2.9),
+        "settle_b": (1.21, 1.22, 1.23, 1.24),
+        "settle_a": (2, 2.8, 3.6, 4.4),
+        "B": (1.25, 1.26, 1.27, 11.5, 27),
+        "A": (2.01, 2.81, 3.61, 12.5, 28.5),
+        "B2": (27.1, 27.2, 27.3, 32.1, 35),
+        "A2": (28.6, 28.7, 28.8, 31, 34.5),
     }
-    products = [(normed, [d_gate], 0), (cot, [act.at[:, pl.ds(0, EARLY)]], w), (normed, [d_up], w + EARLY)]
-    grad_scatter(cm, products, G, RC, w + e, bufs, sems, times, done_a, done_b)
+    products_a = [(normed, [d_gate], 0), (cot, [act.at[:, pl.ds(0, e)]], w)]
+    products_b = [(cot, [act.at[:, pl.ds(e, e)]], w + e), (normed, [d_up], w + EARLY)]
+    grad_scatter(cm, products_a, products_b, G, RC, w + e, bufs, sems, times, done_a, done_b)
     cm.run()
 
 
@@ -565,7 +574,7 @@
             for h in range(2):
                 small[16 + 2 * k + h : 17 + 2 * k + h, :] = taps[k : k + 1, 128 * h : 128 * (h + 1)]
 
-    head_sum(cm, dm, o_tok, yt, yf, ys, yr, finish_tokens, (0, 7, 19.5, 27), lambda: None)
+    head_sum(cm, dm, o_tok, yt, yf, ys, yr, finish_tokens, (0, 8, 19.5, 27), lambda: None)
 
     w = act.shape[1] - EARLY
     wa = w + 512
@@ -594,15 +603,21 @@
         o_out[...] = (mine[cm.me] + theirs[0]) + (theirs[1] + theirs[2])
 
     times = {
-        "block": (0.1, 1.5, 3, 4.5),
-        "settle": (2.9, 4.4, 5.9, 6.9),
-        "A": (3.02, 4.45, 5.95, 11, 25.5),
-        "B": (6.95, 6.96, 6.97, 15.5, 31.5),
-        "A2": (25.6, 25.7, 25.8, 28, 31),
-        "B2": (31.6, 31.7, 31.8, 34, 37),
+        "block_b": (0.1, 0.2, 0.3, 0.4),
+        "block_a": (0.5, 1.5, 2.6, 3.6),
+        "settle_b": (1.41, 1.42, 1.43, 1.44),
+        "settle_a": (2.5, 3.5, 4.5, 5.5),
+        "B": (1.45, 1.46, 1.47, 13, 29),
+        "A": (2.51, 3.51, 4.51, 15, 33),
+        "B2": (29.1, 29.2, 29.3, 34.5, 40),
+        "A2": (33.1, 33.2, 33.3, 36.5, 40.5),
     }
-    products = [(cot, [act.at[:, pl.ds(EARLY, w)]], 0), (normed, [d_proj.at[k] for k in range(3)], w), (d_low, [gated], w + 768)]
-    grad_scatter(cm, products, G, RC, wa, bufs, sems, times, done_a, done_b)
+    products_a = [
+        (cot, [act.at[:, pl.ds(EARLY, w)]], 0),
+        (normed, [d_proj.at[0], d_proj.at[1]], w),
+    ]
+    products_b = [(normed, [d_proj.at[2]], wa), (d_low, [gated], wa + 256)]
+    grad_scatter(cm, products_a, products_b, G, RC, wa, bufs, sems, times, done_a, done_b)
 
     def small_done(gains, rest):
         o_mix[...] = gains[0:8]
@@ -611,7 +626,7 @@
             for h in range(2):
                 o_conv[k : k + 1, pl.ds(128 * h, 128)] = rest[2 * k + h : 2 * k + h + 1]
 
-    small_sums(cm, small, sm, sr, ss, sr_sem, (-0.9, 0.05, 1.6, 3.05, 19), small_done)
+    small_sums(cm, small, sm, sr, ss, sr_sem, (-0.9, 1.443, 8.1, 19.6, 38), small_done)
     cm.run()
 
 
@@ -650,7 +665,7 @@
     ]
 
 
-SCATTER_SEMS = [pltpu.SemaphoreType.DMA((n,)) for n in (4, 4, 12, 12, 12, 12)]
+SCATTER_SEMS = [pltpu.SemaphoreType.DMA((n,)) for n in (8, 8, 12, 12, 12, 12)]
 
 
 def front(gated, ow, tokens, cot, down, gain):

time: 193 us -> 179 us (0.927)
  Pallas kernels: 169 us -> 155 us
    pallas_call x3, Pallas kernels: 167 us -> 153 us  [call(): pl.pallas_call(kernel, out_shape=outs, in_specs=[VMEM_SPEC] * len(args),...]
where the time goes in v9:
time: 179 us
  Pallas kernels  155 us (87%)
  matrix products  9.2 us (5%)
  other arithmetic  6.25 us (3%)
  local copies, waits for them, and re-layouts  5.81 us (3%)
    pallas_call x3, Pallas kernels, call(): pl.pallas_call(kernel, out_shape=outs, in_specs=[VMEM_SPEC] * len(args),...  153 us
    dot_general x2, matrix products, right_product(): lax.dot_general(left, right, (((1,), (1,)), ((), ())), preferred_element_...  4.43 us
  transfers between devices with their start and end apart: 1, of which 0 were waited for; matrix products, arithmetic and copies ran while one was open for 2% of the time, Pallas kernels for 0%

profile of v9, /device:TPU:0, one launch (start us, length us, event | category | flops | bytes accessed | tf_op | source)
XLA Modules:
  0.0 179.0 jit_solution(2113324726813337512)
XLA Ops:
  0.7 1.7 fusion
  2.3 1.5 fusion.2.refs_4_
  3.9 1.0 fusion.3
  5.0 0.6 slice_bitcast_fusion.1
  5.6 1.4 collective-permute-start
  7.1 0.8 fusion.29
  7.9 0.6 fusion.17
  8.5 0.5 broadcast.23
  9.0 0.5 broadcast.24
  9.5 0.8 concatenate.10
  10.3 0.1 dynamic_slice.3
  10.4 0.1 fusion.12
  10.5 0.9 copy.25.refs_13_
  11.4 1.9 %fusion.11 = (bf16[512,256]{1,0:T(8,128)(2,1)S(1)}, f32[512,256]{1,0:T(8,128)S(1)}) fusion(f32[512,3,256]{2,0,1:T(8,128)} %copy-done.2, f32[512,256]{1,0:T(8,128)} %fusion.29, f32[2,256]{1,0:T(2,128)S(1)} %collective-permute-done, f32[512]{0:T(512)S(1)} %get-tuple-element.94, f32[256]{0:T(256)} %bitcast.47, f32[512]{0:T(512)S(1)} %get-tuple-element.86, ...), kind=kLoop, calls=%fused_computation.24 | loop fusion | flops 1441792 | bytes 1844224 | tf_op jit(solution)/shard_map/convert_element_type | solution.py:855
  13.4 1.7 copy-done.4
  15.1 36.3 %front.1 = (bf16[512,1024]{1,0:T(8,128)(2,1)S(1)}, bf16[4,1024,256]{2,1,0:T(8,128)(2,1)S(1)}, bf16[128,1024]{1,0:T(8,128)(2,1)S(1)}, f32[512,1152]{1,0:T(8,128)S...) custom-call(bf16[512,256]{1,0:T(8,128)(2,1)S(1)} %get-tuple-element.80.gated, ...), custom_call_target="tpu_custom_call" | custom-call | flops 1 | bytes 1 | tf_op jit(solution)/shard_map/front/pallas_call | solution.py:637
  51.4 1.5 fusion.18
  53.0 2.3 %multiply_convert_fusion = (bf16[512,1152]{1,0:T(8,128)(2,1)S(1)}, bf16[512,1152]{1,0:T(8,128)(2,1)S(1)}, bf16[512,1152]{1,0:T(8,128)(2,1)S(1)}) fusion(f32[512,1152]{1,0:T(8,128)S(1)} %fusion.18, f32[512,1152]{1,0:T(8,128)S(1)} %get-tuple-element.45, bf16[512,1024]{1,0:T(8,128)(2,1)S(1)} %get-tuple-element.46.refs_4_, bf16[1024,1152]{1,0:T(8,128)(2,1)S(1)} %copy-done), kind=kOutput, calls=%fused_computation.2 | convolution fusion | flops 1217396736 | bytes 11665408 | tf_op jit(solution)/shard_map/dot_general | solution.py:860
  55.2 1.5 fusion.19
  56.8 2.9 %convolution_add_fusion.refs_0_ = f32[512,1024]{1,0:T(8,128)} fusion(f32[512,1024]{1,0:T(8,128)S(1)} %fusion.19, bf16[512,1152]{1,0:T(8,128)(2,1)S(1)} %get-tuple-element.84.refs_6_, bf16[1024,1152]{1,0:T(8,128)(2,1)S(1)} %copy-done), kind=kOutput, calls=%fused_computation.9 | convolution fusion | flops 1208483840 | bytes 7733248 | tf_op jit(solution)/shard_map/dot_general | solution.py:813
  59.7 0.1 pad_maximum_fusion.refs_11_
  59.9 71.9 %middle.1 = (f32[128,1024]{1,0:T(8,128)S(1)}, bf16[128,1024]{1,0:T(8,128)(2,1)S(1)}, f32[1,1024]{1,0:T(1,128)S(1)}, bf16[512,1024]{1,0:T(8,128)(2,1)S(1)}, f32[3...) custom-call(f32[512,1024]{1,0:T(8,128)} %convolution_add_fusion.refs, ...), custom_call_target="tpu_custom_call" | custom-call | flops 1 | bytes 1 | tf_op jit(solution)/shard_map/middle/pallas_call | solution.py:637
  131.8 45.0 %end.1 = (f32[512,1024]{1,0:T(8,128)S(1)}, f32[3,32,256]{2,1,0:T(8,128)S(1)}, f32[32,256]{1,0:T(8,128)S(1)}, f32[32,896]{1,0:T(8,128)S(1)}, f32[8,128]{1,0:T(8,1...) custom-call(f32[512,1024]{1,0:T(8,128)S(1)} %get-tuple-element.51.refs_0_, ...), custom_call_target="tpu_custom_call" | custom-call | flops 1 | bytes 1 | tf_op jit(solution)/shard_map/end/pallas_call | solution.py:637
  176.9 2.0 %place.1 = (f32[32,1152]{1,0:T(8,128)}, bf16[512,1024]{1,0:T(8,128)(2,1)}, f32[512,1024]{1,0:T(8,128)}, f32[8,128]{1,0:T(8,128)}, f32[3,32,256]{2,1,0:T(8,128)},...) custom-call(f32[32,256]{1,0:T(8,128)S(1)} %get-tuple-element.50.refs_0, ...), custom_call_target="tpu_custom_call" | custom-call | tf_op jit(solution)/shard_map/place/pallas_call | solution.py:791
  (45 shorter events, 0.3 us)
Async XLA Ops:
  0.6 52.3 %copy-start = (bf16[1024,1152]{1,0:T(8,128)(2,1)S(1)}, bf16[1024,1152]{1,0:T(8,128)(2,1)}, u32[]{:S(2)}) copy-start(bf16[1024,1152]{1,0:T(8,128)(2,1)} %param.19) | copy-start | bytes 7077892
  0.7 3.2 %copy-start.9 = (bf16[1024,3,256]{2,0,1:T(8,128)(2,1)S(1)}, bf16[1024,3,256]{2,0,1:T(8,128)(2,1)}, u32[]{:S(2)}) copy-start(bf16[1024,3,256]{2,0,1:T(8,128)(2,1)} %param.14) | copy-start | bytes 4718596
  3.9 1.0 copy-start.6
  4.9 2.1 %copy-start.2 = (f32[512,3,256]{2,0,1:T(8,128)}, f32[512,3,256]{2,0,1:T(8,128)S(1)}, u32[]{:S(2)}) copy-start(f32[512,3,256]{2,0,1:T(8,128)S(1)} %fusion.3) | copy-start | bytes 4718596
  4.9 3.0 %copy-start.17 = (bf16[3,256]{1,0:T(4,128)(2,1)S(1)}, bf16[3,256]{1,0:T(4,128)(2,1)}, u32[]{:S(2)}) copy-start(bf16[3,256]{1,0:T(4,128)(2,1)} %param.15) | copy-start | bytes 4612
  4.9 4.6 %copy-start.16 = (s32[16384]{0:T(1024)S(1)}, s32[16384]{0:T(1024)}, u32[]{:S(2)}) copy-start(s32[16384]{0:T(1024)} %param.12) | copy-start | bytes 196612
  5.0 8.3 %copy-start.1 = (bf16[512,1024]{1,0:T(8,128)(2,1)S(1)}, bf16[512,1024]{1,0:T(8,128)(2,1)}, u32[]{:S(2)}) copy-start(bf16[512,1024]{1,0:T(8,128)(2,1)} %refs_16_.1) | copy-start | bytes 3145732
  5.0 8.3 %copy-start.14 = (f32[1024]{0:T(1024)S(1)}, f32[1024]{0:T(1024)}, u32[]{:S(2)}) copy-start(f32[1024]{0:T(1024)} %param.17) | copy-start | bytes 12292
  5.6 5.8 %collective-permute-start = (f32[2,256]{1,0:T(2,128)}, f32[2,256]{1,0:T(2,128)S(1)}, u32[]{:S(2)}, u32[]{:S(2)}) collective-permute-start(f32[2,256]{1,0:T(2,128)} %slice_bitcast_fusion.1), channel_id=1, source_target_pairs={{0,4},{4,8},{8,12},{12,16},{16,20},{20,24},{24,28},{28,32},{32,36}... | collective-permute-start | bytes 6152 | tf_op jit(solution)/shard_map/ppermute | solution.py:805
  11.4 1.9 %copy-start.5 = (bf16[512,1024]{1,0:T(8,128)(2,1)S(1)}, bf16[512,1024]{1,0:T(8,128)(2,1)}, u32[]{:S(2)}) copy-start(bf16[512,1024]{1,0:T(8,128)(2,1)} %refs_9_.1) | copy-start | bytes 3145732
  11.4 2.0 %copy-start.12 = (bf16[1024,256]{1,0:T(8,128)(2,1)S(1)}, bf16[1024,256]{1,0:T(8,128)(2,1)}, u32[]{:S(2)}) copy-start(bf16[1024,256]{1,0:T(8,128)(2,1)} %ow.1) | copy-start | bytes 1572868
  13.4 1.7 copy-start.4
  15.1 36.3 %copy-start.18 = (bf16[1024,1152]{1,0:T(8,128)(2,1)S(1)}, bf16[1024,1152]{1,0:T(8,128)(2,1)}, u32[]{:S(2)}) copy-start(bf16[1024,1152]{1,0:T(8,128)(2,1)} %param.18) | copy-start | bytes 7077892
  51.4 1.6 copy-start.8
  56.8 2.9 %copy-start.15 = (f32[512,256]{1,0:T(8,128)S(1)}, f32[512,256]{1,0:T(8,128)}, u32[]{:S(2)}) copy-start(f32[512,256]{1,0:T(8,128)} %fusion.29) | copy-start | bytes 1572868
  56.8 3.1 %copy-start.3 = (f32[512,3,256]{2,0,1:T(8,128)S(1)}, f32[512,3,256]{2,0,1:T(8,128)}, u32[]{:S(2)}) copy-start(f32[512,3,256]{2,0,1:T(8,128)} %copy-done.2) | copy-start | bytes 4718596
  56.8 3.1 %copy-start.10 = (bf16[1024,3,256]{2,0,1:T(8,128)(2,1)S(1)}, bf16[1024,3,256]{2,0,1:T(8,128)(2,1)}, u32[]{:S(2)}) copy-start(bf16[1024,3,256]{2,0,1:T(8,128)(2,1)} %param.14) | copy-start | bytes 4718596
  56.8 3.1 %copy-start.11 = (f32[512,4]{1,0:T(8,128)S(1)}, f32[512,4]{1,0:T(8,128)}, u32[]{:S(2)}) copy-start(f32[512,4]{1,0:T(8,128)} %copy.25.refs_13_) | copy-start | bytes 24580
  59.9 72.0 %copy-start.7 = (bf16[512,1024]{1,0:T(8,128)(2,1)S(1)}, bf16[512,1024]{1,0:T(8,128)(2,1)}, u32[]{:S(2)}) copy-start(bf16[512,1024]{1,0:T(8,128)(2,1)} %copy-done.6) | copy-start | bytes 3145732
  59.9 72.0 %copy-start.13 = (f32[1024]{0:T(1024)S(1)}, f32[1024]{0:T(1024)}, u32[]{:S(2)}) copy-start(f32[1024]{0:T(1024)} %param.13) | copy-start | bytes 12292

commit v10 on v9

--- a/solution.py
+++ b/solution.py
@@ -347,6 +347,9 @@
     h["bz3f"].wait_recv()
     weight("bx1", WF.at[x, :, c, high], 13, cm.at_x(1))
     weight("bx3", WF.at[x, :, c, high], 14, cm.at_x(3))
+    zo, xo = ahead(z, 2), ahead(x, 2)
+    weight("t0", WF.at[:, z, c, low], 19, cm.twin())
+    weight("t1", WF.at[x, :, c, high], 20, cm.twin())
     o_dact[...] = jnp.dot(cot[...], down[...], preferred_element_type=jnp.float32)
     h["r0"].wait_recv()
     gate("r0f", GF.at[L, first], 4, 1)
@@ -354,29 +357,38 @@
     gate("l1f", GF.at[R, second], 5, 3)
     h["az1"].wait_recv()
     weight("az1f", WF.at[:, zl, c, 0], 15, cm.at_z(1))
+    weight("t2", WF.at[:, zl, c, low], 21, cm.twin())
     h["az3"].wait_recv()
     weight("az3f", WF.at[:, zr, c, 1], 16, cm.at_z(3))
+    weight("t3", WF.at[:, zr, c, low], 22, cm.twin())
     h["bx1"].wait_recv()
     weight("bx1f", WF.at[xl, :, c, 2], 17, cm.at_x(1))
+    weight("t4", WF.at[xl, :, c, high], 23, cm.twin())
     h["bx3"].wait_recv()
     weight("bx3f", WF.at[xr, :, c, 3], 18, cm.at_x(3))
-    for name in ("az1f", "az3f", "bx1f", "bx3f"):
-        h[name].wait_recv()
-    weight("twin", WF.at[:, :, c], 19, cm.twin())
+    weight("t5", WF.at[xr, :, c, high], 24, cm.twin())
+    h["az1f"].wait_recv()
+    h["az3f"].wait_recv()
+    weight("t6", WF.at[:, zo, c, low], 25, cm.twin())
+    h["bx1f"].wait_recv()
+    h["bx3f"].wait_recv()
+    weight("t7", WF.at[xo, :, c, high], 26, cm.twin())
     h["r1"].wait_recv()
     h["l0"].wait_recv()
-    h["twin"].wait_recv()
+    for k in range(8):
+        h[f"t{k}"].wait_recv()
     for k in range(4):
         o_full[k] = WF[:, :, :, k].reshape(1024, 256).astype(jnp.bfloat16)
 
-    def add(k):
-        low_gated = GF[k].astype(jnp.bfloat16)
+    def add(*heads):
         resid[...] += lax.dot_general(
-            low_gated, o_full[k], (((1,), (1,)), ((), ())), preferred_element_type=jnp.float32
+            jnp.concatenate([GF[k].astype(jnp.bfloat16) for k in heads], axis=1),
+            jnp.concatenate([o_full[k] for k in heads], axis=1),
+            (((1,), (1,)), ((), ())),
+            preferred_element_type=jnp.float32,
         )
 
-    add(L)
-    add(R)
+    add(L, R)
     h["r0f"].wait_recv()
     h["l1f"].wait_recv()
     add(O)
@@ -686,8 +698,8 @@
         pltpu.VMEM((4, 4, 2, 4, 32, ow.shape[1]), f32),
         dma((6,)),
         dma((6,)),
-        dma((20,)),
-        dma((20,)),
+        dma((27,)),
+        dma((27,)),
     ]
     return call(front_kernel, "front", 3, (gated, ow, tokens, cot, down, gain), outs, scratch, 24)
 

time: 179 us -> 177 us (0.989)
  Pallas kernels: 155 us -> 152 us
    pallas_call x3, Pallas kernels: 153 us -> 150 us  [call(): pl.pallas_call(kernel, out_shape=outs, in_specs=[VMEM_SPEC] * len(args),...]
where the time goes in v10:
time: 177 us; the launch traced here: 176 us
  Pallas kernels  152 us (86%)
  matrix products  9.2 us (5%)
  other arithmetic  6.25 us (4%)
  local copies, waits for them, and re-layouts  5.81 us (3%)
    pallas_call x3, Pallas kernels, call(): pl.pallas_call(kernel, out_shape=outs, in_specs=[VMEM_SPEC] * len(args),...  150 us
    dot_general x2, matrix products, right_product(): lax.dot_general(left, right, (((1,), (1,)), ((), ())), preferred_element_...  4.43 us
  transfers between devices with their start and end apart: 1, of which 0 were waited for; matrix products, arithmetic and copies ran while one was open for 2% of the time, Pallas kernels for 0%

profile of v10, /device:TPU:0, one launch (start us, length us, event | category | flops | bytes accessed | tf_op | source)
XLA Modules:
  0.0 176.2 jit_solution(8758679313527428144)
XLA Ops:
  0.7 1.7 fusion
  2.3 1.5 fusion.2.refs_4_
  3.9 1.0 fusion.3
  5.0 0.6 slice_bitcast_fusion.1
  5.6 1.4 collective-permute-start
  7.1 0.8 fusion.29
  7.9 0.6 fusion.17
  8.5 0.5 broadcast.23
  9.0 0.5 broadcast.24
  9.5 0.8 concatenate.10
  10.3 0.1 dynamic_slice.3
  10.4 0.1 fusion.12
  10.5 0.9 copy.25.refs_13_
  11.4 1.9 %fusion.11 = (bf16[512,256]{1,0:T(8,128)(2,1)S(1)}, f32[512,256]{1,0:T(8,128)S(1)}) fusion(f32[512,3,256]{2,0,1:T(8,128)} %copy-done.2, f32[512,256]{1,0:T(8,128)} %fusion.29, f32[2,256]{1,0:T(2,128)S(1)} %collective-permute-done, f32[512]{0:T(512)S(1)} %get-tuple-element.94, f32[256]{0:T(256)} %bitcast.47, f32[512]{0:T(512)S(1)} %get-tuple-element.86, ...), kind=kLoop, calls=%fused_computation.24 | loop fusion | flops 1441792 | bytes 1844224 | tf_op jit(solution)/shard_map/convert_element_type | solution.py:867
  13.4 1.7 copy-done.4
  15.1 34.3 %front.1 = (bf16[512,1024]{1,0:T(8,128)(2,1)S(1)}, bf16[4,1024,256]{2,1,0:T(8,128)(2,1)S(1)}, bf16[128,1024]{1,0:T(8,128)(2,1)S(1)}, f32[512,1152]{1,0:T(8,128)S...) custom-call(bf16[512,256]{1,0:T(8,128)(2,1)S(1)} %get-tuple-element.80.gated, ...), custom_call_target="tpu_custom_call" | custom-call | flops 1 | bytes 1 | tf_op jit(solution)/shard_map/front/pallas_call | solution.py:649
  49.5 1.5 fusion.18
  51.0 2.3 %multiply_convert_fusion = (bf16[512,1152]{1,0:T(8,128)(2,1)S(1)}, bf16[512,1152]{1,0:T(8,128)(2,1)S(1)}, bf16[512,1152]{1,0:T(8,128)(2,1)S(1)}) fusion(f32[512,1152]{1,0:T(8,128)S(1)} %fusion.18, f32[512,1152]{1,0:T(8,128)S(1)} %get-tuple-element.45, bf16[512,1024]{1,0:T(8,128)(2,1)S(1)} %get-tuple-element.46.refs_4_, bf16[1024,1152]{1,0:T(8,128)(2,1)S(1)} %copy-done), kind=kOutput, calls=%fused_computation.2 | convolution fusion | flops 1217396736 | bytes 11665408 | tf_op jit(solution)/shard_map/dot_general | solution.py:872
  53.3 1.5 fusion.19
  54.9 2.9 %convolution_add_fusion.refs_0_ = f32[512,1024]{1,0:T(8,128)} fusion(f32[512,1024]{1,0:T(8,128)S(1)} %fusion.19, bf16[512,1152]{1,0:T(8,128)(2,1)S(1)} %get-tuple-element.84.refs_6_, bf16[1024,1152]{1,0:T(8,128)(2,1)S(1)} %copy-done), kind=kOutput, calls=%fused_computation.9 | convolution fusion | flops 1208483840 | bytes 7733248 | tf_op jit(solution)/shard_map/dot_general | solution.py:825
  57.8 0.1 pad_maximum_fusion.refs_11_
  57.9 71.0 %middle.1 = (f32[128,1024]{1,0:T(8,128)S(1)}, bf16[128,1024]{1,0:T(8,128)(2,1)S(1)}, f32[1,1024]{1,0:T(1,128)S(1)}, bf16[512,1024]{1,0:T(8,128)(2,1)S(1)}, f32[3...) custom-call(f32[512,1024]{1,0:T(8,128)} %convolution_add_fusion.refs, ...), custom_call_target="tpu_custom_call" | custom-call | flops 1 | bytes 1 | tf_op jit(solution)/shard_map/middle/pallas_call | solution.py:649
  129.0 45.1 %end.1 = (f32[512,1024]{1,0:T(8,128)S(1)}, f32[3,32,256]{2,1,0:T(8,128)S(1)}, f32[32,256]{1,0:T(8,128)S(1)}, f32[32,896]{1,0:T(8,128)S(1)}, f32[8,128]{1,0:T(8,1...) custom-call(f32[512,1024]{1,0:T(8,128)S(1)} %get-tuple-element.51.refs_0_, ...), custom_call_target="tpu_custom_call" | custom-call | flops 1 | bytes 1 | tf_op jit(solution)/shard_map/end/pallas_call | solution.py:649
  174.1 2.0 %place.1 = (f32[32,1152]{1,0:T(8,128)}, bf16[512,1024]{1,0:T(8,128)(2,1)}, f32[512,1024]{1,0:T(8,128)}, f32[8,128]{1,0:T(8,128)}, f32[3,32,256]{2,1,0:T(8,128)},...) custom-call(f32[32,256]{1,0:T(8,128)S(1)} %get-tuple-element.50.refs_0, ...), custom_call_target="tpu_custom_call" | custom-call | tf_op jit(solution)/shard_map/place/pallas_call | solution.py:803
  (45 shorter events, 0.4 us)
Async XLA Ops:
  0.6 50.4 %copy-start = (bf16[1024,1152]{1,0:T(8,128)(2,1)S(1)}, bf16[1024,1152]{1,0:T(8,128)(2,1)}, u32[]{:S(2)}) copy-start(bf16[1024,1152]{1,0:T(8,128)(2,1)} %param.19) | copy-start | bytes 7077892
  0.7 3.2 %copy-start.9 = (bf16[1024,3,256]{2,0,1:T(8,128)(2,1)S(1)}, bf16[1024,3,256]{2,0,1:T(8,128)(2,1)}, u32[]{:S(2)}) copy-start(bf16[1024,3,256]{2,0,1:T(8,128)(2,1)} %param.14) | copy-start | bytes 4718596
  3.9 1.0 copy-start.6
  4.9 2.1 %copy-start.2 = (f32[512,3,256]{2,0,1:T(8,128)}, f32[512,3,256]{2,0,1:T(8,128)S(1)}, u32[]{:S(2)}) copy-start(f32[512,3,256]{2,0,1:T(8,128)S(1)} %fusion.3) | copy-start | bytes 4718596
  4.9 3.0 %copy-start.17 = (bf16[3,256]{1,0:T(4,128)(2,1)S(1)}, bf16[3,256]{1,0:T(4,128)(2,1)}, u32[]{:S(2)}) copy-start(bf16[3,256]{1,0:T(4,128)(2,1)} %param.15) | copy-start | bytes 4612
  4.9 4.6 %copy-start.16 = (s32[16384]{0:T(1024)S(1)}, s32[16384]{0:T(1024)}, u32[]{:S(2)}) copy-start(s32[16384]{0:T(1024)} %param.12) | copy-start | bytes 196612
  5.0 8.3 %copy-start.1 = (bf16[512,1024]{1,0:T(8,128)(2,1)S(1)}, bf16[512,1024]{1,0:T(8,128)(2,1)}, u32[]{:S(2)}) copy-start(bf16[512,1024]{1,0:T(8,128)(2,1)} %refs_16_.1) | copy-start | bytes 3145732
  5.0 8.3 %copy-start.14 = (f32[1024]{0:T(1024)S(1)}, f32[1024]{0:T(1024)}, u32[]{:S(2)}) copy-start(f32[1024]{0:T(1024)} %param.17) | copy-start | bytes 12292
  5.6 5.8 %collective-permute-start = (f32[2,256]{1,0:T(2,128)}, f32[2,256]{1,0:T(2,128)S(1)}, u32[]{:S(2)}, u32[]{:S(2)}) collective-permute-start(f32[2,256]{1,0:T(2,128)} %slice_bitcast_fusion.1), channel_id=1, source_target_pairs={{0,4},{4,8},{8,12},{12,16},{16,20},{20,24},{24,28},{28,32},{32,36}... | collective-permute-start | bytes 6152 | tf_op jit(solution)/shard_map/ppermute | solution.py:817
  11.4 1.9 %copy-start.5 = (bf16[512,1024]{1,0:T(8,128)(2,1)S(1)}, bf16[512,1024]{1,0:T(8,128)(2,1)}, u32[]{:S(2)}) copy-start(bf16[512,1024]{1,0:T(8,128)(2,1)} %refs_9_.1) | copy-start | bytes 3145732
  11.4 2.0 %copy-start.12 = (bf16[1024,256]{1,0:T(8,128)(2,1)S(1)}, bf16[1024,256]{1,0:T(8,128)(2,1)}, u32[]{:S(2)}) copy-start(bf16[1024,256]{1,0:T(8,128)(2,1)} %ow.1) | copy-start | bytes 1572868
  13.4 1.7 copy-start.4
  15.1 34.3 %copy-start.18 = (bf16[1024,1152]{1,0:T(8,128)(2,1)S(1)}, bf16[1024,1152]{1,0:T(8,128)(2,1)}, u32[]{:S(2)}) copy-start(bf16[1024,1152]{1,0:T(8,128)(2,1)} %param.18) | copy-start | bytes 7077892
  49.4 1.6 copy-start.8
  54.8 2.9 %copy-start.15 = (f32[512,256]{1,0:T(8,128)S(1)}, f32[512,256]{1,0:T(8,128)}, u32[]{:S(2)}) copy-start(f32[512,256]{1,0:T(8,128)} %fusion.29) | copy-start | bytes 1572868
  54.8 3.1 %copy-start.3 = (f32[512,3,256]{2,0,1:T(8,128)S(1)}, f32[512,3,256]{2,0,1:T(8,128)}, u32[]{:S(2)}) copy-start(f32[512,3,256]{2,0,1:T(8,128)} %copy-done.2) | copy-start | bytes 4718596
  54.8 3.1 %copy-start.10 = (bf16[1024,3,256]{2,0,1:T(8,128)(2,1)S(1)}, bf16[1024,3,256]{2,0,1:T(8,128)(2,1)}, u32[]{:S(2)}) copy-start(bf16[1024,3,256]{2,0,1:T(8,128)(2,1)} %param.14) | copy-start | bytes 4718596
  54.9 3.1 %copy-start.11 = (f32[512,4]{1,0:T(8,128)S(1)}, f32[512,4]{1,0:T(8,128)}, u32[]{:S(2)}) copy-start(f32[512,4]{1,0:T(8,128)} %copy.25.refs_13_) | copy-start | bytes 24580
  57.9 71.0 %copy-start.7 = (bf16[512,1024]{1,0:T(8,128)(2,1)S(1)}, bf16[512,1024]{1,0:T(8,128)(2,1)}, u32[]{:S(2)}) copy-start(bf16[512,1024]{1,0:T(8,128)(2,1)} %copy-done.6) | copy-start | bytes 3145732
  57.9 71.0 %copy-start.13 = (f32[1024]{0:T(1024)S(1)}, f32[1024]{0:T(1024)}, u32[]{:S(2)}) copy-start(f32[1024]{0:T(1024)} %param.13) | copy-start | bytes 12292

commit v11 on v10

--- a/solution.py
+++ b/solution.py
@@ -741,7 +741,7 @@
         dma((1,)),
         dma((1,)),
     ]
-    return call(middle_kernel, "middle", 5, args, outs, scratch, 36)
+    return call(middle_kernel, "middle", 5, args, outs, scratch, 30)
 
 
 def end(*args):

time: 177 us -> 174 us (0.983)
  Pallas kernels: 152 us -> 149 us
    pallas_call x3, Pallas kernels: 150 us -> 147 us  [call(): pl.pallas_call(kernel, out_shape=outs, in_specs=[VMEM_SPEC] * len(args),...]
  transfers between devices with their start and end apart: 1 -> 1, of which waited for: 0 -> 0; matrix products, arithmetic and copies ran while one was open for 2% -> 3% of each run, Pallas kernels for 0% -> 0%
where the time goes in v11:
time: 174 us; the launch traced here: 173 us
  Pallas kernels  149 us (86%)
  matrix products  7.86 us (5%)
  local copies, waits for them, and re-layouts  6.78 us (4%)
  other arithmetic  6.27 us (4%)
    pallas_call x3, Pallas kernels, call(): pl.pallas_call(kernel, out_shape=outs, in_specs=[VMEM_SPEC] * len(args),...  147 us
  transfers between devices with their start and end apart: 1, of which 0 were waited for; matrix products, arithmetic and copies ran while one was open for 3% of the time, Pallas kernels for 0%

profile of v11, /device:TPU:0, one launch (start us, length us, event | category | flops | bytes accessed | tf_op | source)
XLA Modules:
  0.0 172.9 jit_solution(17350625777210965012)
XLA Ops:
  0.7 1.7 fusion
  2.3 1.5 fusion.2.refs_4_
  3.9 1.0 fusion.3
  5.0 0.6 slice_bitcast_fusion.1
  5.6 1.4 collective-permute-start
  7.1 0.9 fusion.29
  7.9 0.6 fusion.17
  8.5 0.5 broadcast.23
  9.0 0.5 broadcast.24
  9.5 0.8 concatenate.10
  10.6 0.9 copy.25.refs_13_
  11.4 1.9 %fusion.11 = (bf16[512,256]{1,0:T(8,128)(2,1)S(1)}, f32[512,256]{1,0:T(8,128)S(1)}) fusion(f32[512,3,256]{2,0,1:T(8,128)} %copy-done.2, f32[512,256]{1,0:T(8,128)} %fusion.29, f32[2,256]{1,0:T(2,128)S(1)} %collective-permute-done, f32[512]{0:T(512)S(1)} %get-tuple-element.94, f32[256]{0:T(256)} %bitcast.47, f32[512]{0:T(512)S(1)} %get-tuple-element.86, ...), kind=kLoop, calls=%fused_computation.24 | loop fusion | flops 1441792 | bytes 1844224 | tf_op jit(solution)/shard_map/convert_element_type | solution.py:867
  13.4 1.7 copy-done.4
  15.1 34.3 %front.1 = (bf16[512,1024]{1,0:T(8,128)(2,1)S(1)}, bf16[4,1024,256]{2,1,0:T(8,128)(2,1)S(1)}, bf16[128,1024]{1,0:T(8,128)(2,1)S(1)}, f32[512,1152]{1,0:T(8,128)S...) custom-call(bf16[512,256]{1,0:T(8,128)(2,1)S(1)} %get-tuple-element.80.gated, ...), custom_call_target="tpu_custom_call" | custom-call | flops 1 | bytes 1 | tf_op jit(solution)/shard_map/front/pallas_call | solution.py:649
  49.4 1.5 fusion.18
  51.0 2.3 %multiply_convert_fusion = (bf16[512,1152]{1,0:T(8,128)(2,1)S(1)}, bf16[512,1152]{1,0:T(8,128)(2,1)S(1)}, bf16[512,1152]{1,0:T(8,128)(2,1)S(1)}) fusion(f32[512,1152]{1,0:T(8,128)S(1)} %fusion.18, f32[512,1152]{1,0:T(8,128)S(1)} %get-tuple-element.45, bf16[512,1024]{1,0:T(8,128)(2,1)S(1)} %get-tuple-element.46.refs_4_, bf16[1024,1152]{1,0:T(8,128)(2,1)S(1)} %copy-done), kind=kOutput, calls=%fused_computation.2 | convolution fusion | flops 1217396736 | bytes 11665408 | tf_op jit(solution)/shard_map/dot_general | solution.py:872
  53.2 1.5 fusion.19
  54.9 1.6 convolution_add_fusion.refs_0_
  56.4 0.1 pad_maximum_fusion.refs_11_
  56.6 0.5 copy-done.5
  57.1 0.5 copy-done.10
  57.6 67.9 %middle.1 = (f32[128,1024]{1,0:T(8,128)S(1)}, bf16[128,1024]{1,0:T(8,128)(2,1)S(1)}, f32[1,1024]{1,0:T(1,128)S(1)}, bf16[512,1024]{1,0:T(8,128)(2,1)S(1)}, f32[3...) custom-call(f32[512,1024]{1,0:T(8,128)S(1)} %convolution_add_fusion., ...), custom_call_target="tpu_custom_call" | custom-call | flops 1 | bytes 1 | tf_op jit(solution)/shard_map/middle/pallas_call | solution.py:649
  125.5 45.2 %end.1 = (f32[512,1024]{1,0:T(8,128)S(1)}, f32[3,32,256]{2,1,0:T(8,128)S(1)}, f32[32,256]{1,0:T(8,128)S(1)}, f32[32,896]{1,0:T(8,128)S(1)}, f32[8,128]{1,0:T(8,1...) custom-call(f32[512,1024]{1,0:T(8,128)S(1)} %get-tuple-element.51.refs_0_, ...), custom_call_target="tpu_custom_call" | custom-call | flops 1 | bytes 1 | tf_op jit(solution)/shard_map/end/pallas_call | solution.py:649
  170.7 2.0 %place.1 = (f32[32,1152]{1,0:T(8,128)}, bf16[512,1024]{1,0:T(8,128)(2,1)}, f32[512,1024]{1,0:T(8,128)}, f32[8,128]{1,0:T(8,128)}, f32[3,32,256]{2,1,0:T(8,128)},...) custom-call(f32[32,256]{1,0:T(8,128)S(1)} %get-tuple-element.50.refs_0, ...), custom_call_target="tpu_custom_call" | custom-call | tf_op jit(solution)/shard_map/place/pallas_call | solution.py:803
  (45 shorter events, 0.5 us)
Async XLA Ops:
  0.6 50.3 %copy-start = (bf16[1024,1152]{1,0:T(8,128)(2,1)S(1)}, bf16[1024,1152]{1,0:T(8,128)(2,1)}, u32[]{:S(2)}) copy-start(bf16[1024,1152]{1,0:T(8,128)(2,1)} %param.19) | copy-start | bytes 7077892
  0.7 3.2 %copy-start.9 = (bf16[1024,3,256]{2,0,1:T(8,128)(2,1)S(1)}, bf16[1024,3,256]{2,0,1:T(8,128)(2,1)}, u32[]{:S(2)}) copy-start(bf16[1024,3,256]{2,0,1:T(8,128)(2,1)} %param.14) | copy-start | bytes 4718596
  3.9 1.0 copy-start.7
  4.9 2.1 %copy-start.2 = (f32[512,3,256]{2,0,1:T(8,128)}, f32[512,3,256]{2,0,1:T(8,128)S(1)}, u32[]{:S(2)}) copy-start(f32[512,3,256]{2,0,1:T(8,128)S(1)} %fusion.3) | copy-start | bytes 4718596
  4.9 3.0 %copy-start.17 = (bf16[3,256]{1,0:T(4,128)(2,1)S(1)}, bf16[3,256]{1,0:T(4,128)(2,1)}, u32[]{:S(2)}) copy-start(bf16[3,256]{1,0:T(4,128)(2,1)} %param.15) | copy-start | bytes 4612
  4.9 4.6 %copy-start.16 = (s32[16384]{0:T(1024)S(1)}, s32[16384]{0:T(1024)}, u32[]{:S(2)}) copy-start(s32[16384]{0:T(1024)} %param.12) | copy-start | bytes 196612
  5.0 8.3 %copy-start.1 = (bf16[512,1024]{1,0:T(8,128)(2,1)S(1)}, bf16[512,1024]{1,0:T(8,128)(2,1)}, u32[]{:S(2)}) copy-start(bf16[512,1024]{1,0:T(8,128)(2,1)} %refs_16_.1) | copy-start | bytes 3145732
  5.0 8.3 %copy-start.14 = (f32[1024]{0:T(1024)S(1)}, f32[1024]{0:T(1024)}, u32[]{:S(2)}) copy-start(f32[1024]{0:T(1024)} %param.17) | copy-start | bytes 12292
  5.6 5.8 %collective-permute-start = (f32[2,256]{1,0:T(2,128)}, f32[2,256]{1,0:T(2,128)S(1)}, u32[]{:S(2)}, u32[]{:S(2)}) collective-permute-start(f32[2,256]{1,0:T(2,128)} %slice_bitcast_fusion.1), channel_id=1, source_target_pairs={{0,4},{4,8},{8,12},{12,16},{16,20},{20,24},{24,28},{28,32},{32,36}... | collective-permute-start | bytes 6152 | tf_op jit(solution)/shard_map/ppermute | solution.py:817
  11.4 1.9 %copy-start.6 = (bf16[512,1024]{1,0:T(8,128)(2,1)S(1)}, bf16[512,1024]{1,0:T(8,128)(2,1)}, u32[]{:S(2)}) copy-start(bf16[512,1024]{1,0:T(8,128)(2,1)} %refs_9_.1) | copy-start | bytes 3145732
  11.4 2.0 %copy-start.12 = (bf16[1024,256]{1,0:T(8,128)(2,1)S(1)}, bf16[1024,256]{1,0:T(8,128)(2,1)}, u32[]{:S(2)}) copy-start(bf16[1024,256]{1,0:T(8,128)(2,1)} %ow.1) | copy-start | bytes 1572868
  13.4 1.7 copy-start.4
  15.1 34.3 %copy-start.18 = (bf16[1024,1152]{1,0:T(8,128)(2,1)S(1)}, bf16[1024,1152]{1,0:T(8,128)(2,1)}, u32[]{:S(2)}) copy-start(bf16[1024,1152]{1,0:T(8,128)(2,1)} %param.18) | copy-start | bytes 7077892
  54.8 1.6 copy-start.15
  54.8 1.8 %copy-start.3 = (f32[512,3,256]{2,0,1:T(8,128)S(1)}, f32[512,3,256]{2,0,1:T(8,128)}, u32[]{:S(2)}) copy-start(f32[512,3,256]{2,0,1:T(8,128)} %copy-done.2) | copy-start | bytes 4718596
  54.8 2.3 %copy-start.5 = (bf16[1024,1152]{1,0:T(8,128)(2,1)S(1)}, bf16[1024,1152]{1,0:T(8,128)(2,1)}, u32[]{:S(2)}) copy-start(bf16[1024,1152]{1,0:T(8,128)(2,1)} %refs_8_.1) | copy-start | bytes 7077892
  54.8 2.7 %copy-start.10 = (bf16[1024,3,256]{2,0,1:T(8,128)(2,1)S(1)}, bf16[1024,3,256]{2,0,1:T(8,128)(2,1)}, u32[]{:S(2)}) copy-start(bf16[1024,3,256]{2,0,1:T(8,128)(2,1)} %param.14) | copy-start | bytes 4718596
  54.8 2.7 %copy-start.11 = (f32[512,4]{1,0:T(8,128)S(1)}, f32[512,4]{1,0:T(8,128)}, u32[]{:S(2)}) copy-start(f32[512,4]{1,0:T(8,128)} %copy.25.refs_13_) | copy-start | bytes 24580
  57.6 67.9 %copy-start.8 = (bf16[512,1024]{1,0:T(8,128)(2,1)S(1)}, bf16[512,1024]{1,0:T(8,128)(2,1)}, u32[]{:S(2)}) copy-start(bf16[512,1024]{1,0:T(8,128)(2,1)} %copy-done.7) | copy-start | bytes 3145732
  57.6 67.9 %copy-start.13 = (f32[1024]{0:T(1024)S(1)}, f32[1024]{0:T(1024)}, u32[]{:S(2)}) copy-start(f32[1024]{0:T(1024)} %param.13) | copy-start | bytes 12292
